TPU v7x, 32 devices: a whole 2x2x4 slice. The times are simulated.
32 devices in a mesh: src: 4 (over y, core), rcv: 8 (over z, x).
Axes of the slice: x: 2, y: 2, z: 4, core: 2. Of those that a mesh axis runs over, the one named last changes fastest.
Arguments:
- data: bfloat16 [2, 4096, 4096], P(None, ('src', 'rcv')), may hold values from -0.8984375 to 0.8984375
- fill_mask: int32 [4096, 4096], P(('src', 'rcv')), may hold values 0 or 1
- obliquity: float32 [4096], replicated, may hold values from 0.25 to 4
- aperture: int32 [8, 8, 8], P('src'), may hold values from 0 to 7, as said below
- lengths: int32 [8, 8], P('src', 'rcv'), may hold values from 1 to 8, as said below
Outputs:
- predicted: float32 [2, 4096, 4096], P(None, 'src', 'rcv')
Inputs may be any that keep to these rules, and one draw needn't show every extreme that they name: `aperture`: every entry is a tile index; the 8 entries of one output tile are distinct; only the first lengths entries of a list are used. `lengths`: some output tile uses all 8 entries of its list.
All inputs are finite; a program needn't handle non-finite values. No bound on the sum of `fill_mask` on one device may be relied on, other than what follows from the above.
Results may differ from a plain program's by a relative error of at most 0.0028.
Values may be sent and summed in bfloat16 or wider, within the bound.
No kernel may reach another device: no remote copies, remote signals or barrier semaphores. Data moves between devices by JAX's collectives and lax.ppermute only.
A program may use at most 128 MiB of HBM per device.

v0:
```python
import functools

import jax
import jax.numpy as jnp
from jax import lax
from jax.experimental import pallas as pl
from jax.experimental.pallas import tpu as pltpu
from jax.sharding import PartitionSpec as P

TILE_SIZE = 512


def ring_order(count):
    return list(range(0, count, 2)) + list(range(1, count, 2))[::-1]


def split_kernel(data_ref, *out_refs):
    rows = data_ref.shape[1]
    for part, out_ref in enumerate(out_refs):
        for block in range(out_ref.shape[0]):
            out_ref[block] = data_ref[part, :, block * rows : (block + 1) * rows].T


def transposed_blocks(data, devices):
    _, rows, total = data.shape
    if rows % 128:
        return tuple(jnp.transpose(p.reshape(rows, devices, rows), (1, 0, 2)) for p in data)
    group = 8
    return pl.pallas_call(
        split_kernel,
        out_shape=(jax.ShapeDtypeStruct((devices, rows, rows), data.dtype),) * 2,
        grid=(devices // group,),
        in_specs=[pl.BlockSpec((2, rows, group * rows), lambda i: (0, 0, i))],
        out_specs=(pl.BlockSpec((group, rows, rows), lambda i: (i, 0, 0)),) * 2,
    )(data)


def fill_kernel(data_ref, mask_ref, arrived_ref, out_ref):
    rows = data_ref.shape[0]
    for block in range(arrived_ref.shape[0]):
        span = slice(block * rows, (block + 1) * rows)
        out_ref[:, span] = jnp.where(
            mask_ref[:, span] == 1, data_ref[:, span], arrived_ref[block]
        )


def fill(data, mask, arrived, part):
    _, rows, total = data.shape
    devices = arrived.shape[0]
    if rows % 128:
        transposed = jnp.transpose(arrived, (2, 0, 1)).reshape(rows, total)
        return jnp.where(mask == 1, data[part], transposed)
    group = 8
    return pl.pallas_call(
        fill_kernel,
        out_shape=jax.ShapeDtypeStruct((rows, total), data.dtype),
        grid=(devices // group,),
        in_specs=[
            pl.BlockSpec((None, rows, group * rows), lambda i: (part, 0, i)),
            pl.BlockSpec((rows, group * rows), lambda i: (0, i)),
            pl.BlockSpec((group, rows, rows), lambda i: (i, 0, 0)),
        ],
        out_specs=pl.BlockSpec((rows, group * rows), lambda i: (0, i)),
    )(data, mask, arrived)


def product_kernel(rows, src_count, plan_ref, used_ref, *refs):
    (row_refs, piece_refs), out_ref, scratch = refs[0], refs[1], refs[2:]
    left, right, row_sem, piece_sem = scratch
    inner_tiles = right.shape[0]
    out_tiles = out_ref.shape[1] // TILE_SIZE

    def piece_copies():
        copies = []
        at = len(row_refs)
        for ref in piece_refs:
            for index in range(ref.shape[0]):
                first = plan_ref[at]
                tile, offset = first // TILE_SIZE, first % TILE_SIZE
                for part in range(2):
                    row = pl.multiple_of(offset + (1 - part) * TILE_SIZE, rows)
                    copies.append(
                        pltpu.make_async_copy(
                            ref.at[index, part],
                            right.at[tile, pl.ds(row, rows), :],
                            piece_sem,
                        )
                    )
                at += 1
        return copies

    def start_rows(tile):
        for index, (ref, part) in enumerate(row_refs):
            row = pl.multiple_of(plan_ref[index], rows)
            column = pl.multiple_of(tile * 2 * TILE_SIZE + part * TILE_SIZE, TILE_SIZE)
            pltpu.make_async_copy(
                ref.at[:, pl.ds(pl.multiple_of(tile * TILE_SIZE, TILE_SIZE), TILE_SIZE)],
                left.at[pl.ds(row, rows), pl.ds(column, TILE_SIZE)],
                row_sem.at[tile],
            ).start()

    for copy in piece_copies():
        copy.start()

    @pl.loop(0, inner_tiles)
    def _(tile):
        start_rows(tile)

    out_ref[...] = jnp.zeros_like(out_ref)
    pltpu.make_async_copy(
        right.at[:, pl.ds(0, 2 * TILE_SIZE), :], right.at[:, pl.ds(0, 2 * TILE_SIZE), :], piece_sem
    ).wait()

    @pl.loop(0, inner_tiles)
    def _(tile):
        columns = pl.ds(pl.multiple_of(tile * 2 * TILE_SIZE, 2 * TILE_SIZE), 2 * TILE_SIZE)
        pltpu.make_async_copy(left.at[:, columns], left.at[:, columns], row_sem.at[tile]).wait()
        right[tile, 2 * TILE_SIZE :, :] = -right[tile, :TILE_SIZE, :]

        @pl.loop(0, out_tiles)
        def _(out_tile):
            @pl.when(used_ref[out_tile, tile] == 1)
            def _():
                span = pl.ds(pl.multiple_of(out_tile * TILE_SIZE, TILE_SIZE), TILE_SIZE)
                lhs = left[span, columns]
                for part in range(2):
                    rhs = right[tile, pl.ds((1 - part) * TILE_SIZE, 2 * TILE_SIZE), :]
                    out_ref[part, span, :] += jnp.dot(lhs, rhs, preferred_element_type=jnp.float32)


def product(row_buffers, row_starts, pieces, piece_starts, used, span, total):
    rows = row_buffers[0][0].shape[0]
    parts = [part for _, part in row_buffers]
    arrays = [array for array, _ in row_buffers] + list(pieces)
    plan = jnp.stack(row_starts + piece_starts).astype(jnp.int32)

    def kernel(plan_ref, used_ref, *refs):
        ins = refs[: len(arrays)]
        row_refs = list(zip(ins[: len(parts)], parts))
        product_kernel(
            rows, None, plan_ref, used_ref, (row_refs, ins[len(parts) :]), *refs[len(arrays) :]
        )

    inner_tiles = total // TILE_SIZE
    return pl.pallas_call(
        kernel,
        out_shape=jax.ShapeDtypeStruct((2, span, TILE_SIZE), jnp.float32),
        grid_spec=pltpu.PrefetchScalarGridSpec(
            num_scalar_prefetch=2,
            grid=(1,),
            in_specs=[pl.BlockSpec(memory_space=pl.ANY)] * len(arrays),
            out_specs=pl.BlockSpec((2, span, TILE_SIZE), lambda i, *_: (0, 0, 0), pipeline_mode=pl.Buffered(1)),
            scratch_shapes=[
                pltpu.VMEM((span, 2 * total), jnp.bfloat16),
                pltpu.VMEM((inner_tiles, 3 * TILE_SIZE, TILE_SIZE), jnp.bfloat16),
                pltpu.SemaphoreType.DMA((inner_tiles,)),
                pltpu.SemaphoreType.DMA,
            ],
        ),
        compiler_params=pltpu.CompilerParams(vmem_limit_bytes=67_000_000),
    )(plan, used, *arrays)


def cut_kernel(place_ref, *refs):
    planes, out_ref = refs[:-1], refs[-1]
    for block in range(out_ref.shape[0]):
        first, second, gain = planes[3 * block : 3 * block + 3]
        for part, ref in enumerate((first, second)):
            out_ref[block, part] = (ref[...].astype(jnp.float32) * gain[...]).astype(jnp.bfloat16)


def cut(blocks, column, gains):
    rows = blocks[0][0][0].shape[0]
    place = jnp.stack([column] + [first for _, first in blocks]).astype(jnp.int32)
    specs, operands = [], []
    for index, (planes, _) in enumerate(blocks):
        specs += [pl.BlockSpec((rows, TILE_SIZE), lambda i, place: (0, place[0]))] * 2
        specs.append(pl.BlockSpec((None, rows, 1), lambda i, place, at=index + 1: (place[at], 0, 0)))
        operands += [planes[0], planes[1], gains]
    shape = (len(blocks), 2, rows, TILE_SIZE)
    return pl.pallas_call(
        cut_kernel,
        out_shape=jax.ShapeDtypeStruct(shape, jnp.bfloat16),
        grid_spec=pltpu.PrefetchScalarGridSpec(
            num_scalar_prefetch=1,
            grid=(1,),
            in_specs=specs,
            out_specs=pl.BlockSpec(shape, lambda i, place: (0, 0, 0, 0)),
        ),
    )(place, *operands)


def job(base, row_blocks, columns, absent, used, span, total, full, accumulate, choice=()):
    rows = row_blocks[0][0][0].shape[0]
    count, height = len(row_blocks), len(row_blocks) * rows
    chunks = 1 + max(column[3] for column in columns)
    depth = total if full else len(columns) * rows
    span_depth = depth // chunks
    plan = jnp.stack(
        [first for _, first in row_blocks]
        + [column[2] for column in columns]
        + list(absent)
        + list(choice)
    ).astype(jnp.int32)
    planes = [plane for block, _ in row_blocks for plane in block]
    sources, source_at = [], []
    for pieces, *_ in columns:
        if not any(pieces is source for source in sources):
            sources.append(pieces)
        source_at.append([source is pieces for source in sources].index(True))
    given = [] if base is None else [base]

    def kernel(plan_ref, used_ref, *refs):
        plane_refs = refs[: len(planes)]
        source_refs = refs[len(planes) : len(planes) + len(sources)]
        out_ref, left, right, held, left_sem, right_sem, held_sem = refs[-7:]

        def first_of(at):
            return pl.multiple_of(plan_ref[at], rows)

        def held_copy(block, part, out):
            here = held.at[part, pl.ds(block * rows, rows), :]
            there = out_ref.at[part, pl.ds(first_of(block), rows), :]
            pair = (here, there) if out else (there, here)
            return pltpu.make_async_copy(*pair, held_sem)

        if accumulate:
            for block in range(count):
                for part in range(2):
                    held_copy(block, part, False).start()
        else:
            held[...] = jnp.zeros_like(held)
        for at in range(len(absent)):
            row = first_of(count + len(columns) + at)
            right[:, pl.ds(row, rows), :] = jnp.zeros((3, rows, TILE_SIZE), jnp.bfloat16)
        for at, (_, index, _, chunk) in enumerate(columns):
            row = first_of(count + at) if full else at * rows
            for part in range(2):
                pltpu.make_async_copy(
                    source_refs[source_at[at]].at[index, part],
                    right.at[part, pl.ds(row, rows), :],
                    right_sem.at[chunk],
                ).start()
        for block in range(count):
            for part in range(2):
                ref, here = plane_refs[2 * block + part], pl.ds(block * rows, rows)
                if full and choice:
                    for at in range(len(planes) // 2):

                        @pl.when(plan_ref[plan.shape[0] - 1] == at)
                        def _():
                            pltpu.make_async_copy(
                                plane_refs[2 * at + part], left.at[part, here, :], left_sem
                            ).start()

                    continue
                if full:
                    pltpu.make_async_copy(ref, left.at[part, here, :], left_sem).start()
                    continue
                for at in range(len(columns)):
                    pltpu.make_async_copy(
                        ref.at[:, pl.ds(first_of(count + at), rows)],
                        left.at[part, here, pl.ds(at * rows, rows)],
                        left_sem,
                    ).start()
        pltpu.make_async_copy(left, left, left_sem).wait()
        if accumulate:
            pltpu.make_async_copy(held, held, held_sem).wait()

        for chunk in range(chunks):
            members = [at for at, column in enumerate(columns) if column[3] == chunk]
            bytes_view = right.at[pl.ds(0, 2), pl.ds(0, len(members) * rows), :]
            pltpu.make_async_copy(bytes_view, bytes_view, right_sem.at[chunk]).wait()
            if full:
                base_row = plan_ref[count + members[0]] // span_depth * span_depth
                inner = pl.ds(pl.multiple_of(base_row, span_depth), span_depth)
                pieces = [(base_row + t * TILE_SIZE, TILE_SIZE) for t in range(span_depth // TILE_SIZE)]
                spots = [pl.ds(pl.multiple_of(p, TILE_SIZE), n) for p, n in pieces]
            else:
                inner = slice(None)
                pieces = [(plan_ref[count + at], rows) for at in members]
                spots = [pl.ds(at * rows, rows) for at in members]
            for block in range(count):
                own_tile = plan_ref[block] // TILE_SIZE
                for (first, size), spot in zip(pieces, spots):

                    @pl.when(used_ref[own_tile, first // TILE_SIZE] == 0)
                    def _():
                        left[:, block * rows : (block + 1) * rows, spot] = jnp.zeros(
                            (2, rows, size), jnp.bfloat16
                        )

            right[2, inner, :] = -right[1, inner, :]
            lead, trail = left[0, :, inner], left[1, :, inner]
            for part, (upper, lower) in enumerate(((0, 2), (1, 0))):
                held[part] += jnp.dot(
                    lead, right[upper, inner, :], preferred_element_type=jnp.float32
                ) + jnp.dot(trail, right[lower, inner, :], preferred_element_type=jnp.float32)

        for block in range(count):
            for part in range(2):
                held_copy(block, part, True).start()
        pltpu.make_async_copy(held, held, held_sem).wait()

    operands = planes + sources + given
    moved = 4 * height * depth + 4 * depth * TILE_SIZE + 8 * height * TILE_SIZE
    return pl.pallas_call(
        kernel,
        out_shape=jax.ShapeDtypeStruct((2, span, TILE_SIZE), jnp.float32),
        grid_spec=pltpu.PrefetchScalarGridSpec(
            num_scalar_prefetch=2,
            grid=(1,),
            in_specs=[pl.BlockSpec(memory_space=pl.ANY)] * len(operands),
            out_specs=pl.BlockSpec(memory_space=pl.ANY),
            scratch_shapes=[
                pltpu.VMEM((2, height, depth), jnp.bfloat16),
                pltpu.VMEM((3, depth, TILE_SIZE), jnp.bfloat16),
                pltpu.VMEM((2, height, TILE_SIZE), jnp.float32),
                pltpu.SemaphoreType.DMA,
                pltpu.SemaphoreType.DMA((chunks,)),
                pltpu.SemaphoreType.DMA,
            ],
        ),
        input_output_aliases={} if base is None else {2 + len(operands) - 1: 0},
        cost_estimate=pl.CostEstimate(
            flops=8 * height * depth * TILE_SIZE, bytes_accessed=moved, transcendentals=0
        ),
        compiler_params=pltpu.CompilerParams(vmem_limit_bytes=60 * 1024 * 1024),
    )(plan, used, *operands)


def used_tiles(aperture, lengths, rcv_index, total):
    lists = lax.dynamic_index_in_dim(aperture, rcv_index, 1, keepdims=False)
    slot = jnp.arange(lists.shape[1], dtype=jnp.int32)
    wanted = (slot[None, :] < lengths)[:, :, None]
    tiles = jnp.arange(total // TILE_SIZE, dtype=jnp.int32)
    return jnp.any(wanted & (lists[:, :, None] == tiles), axis=1).astype(jnp.int32)


def local(data, fill_mask, obliquity, aperture, lengths):
    _, rows, total = data.shape
    src_count = lax.axis_size("src")
    rcv_count = lax.axis_size("rcv")
    src_index = lax.axis_index("src")
    rcv_index = lax.axis_index("rcv")
    devices = src_count * rcv_count
    span = rows * rcv_count
    phased = rows % 128 == 0 and rcv_count % 4 == 0 and rcv_count > 4

    blocks = transposed_blocks(data, devices)
    arrived = [
        lax.all_to_all(b, ("src", "rcv"), split_axis=0, concat_axis=0, tiled=True) for b in blocks
    ]
    own = tuple(fill(data, fill_mask, a, part) for part, a in enumerate(arrived))
    used = used_tiles(aperture, lengths, rcv_index, total)

    order = ring_order(rcv_count)
    forward = [(order[i], order[(i + 1) % rcv_count]) for i in range(rcv_count)]
    backward = [(b, a) for a, b in forward]
    place = jnp.asarray([order.index(i) for i in range(rcv_count)], jnp.int32)[rcv_index]
    table = jnp.asarray(order + order, jnp.int32)
    half = rcv_count // 2

    def origin(offset):
        return lax.dynamic_index_in_dim(table, place + offset % rcv_count, keepdims=False)

    my_gains = -lax.dynamic_slice_in_dim(obliquity, src_index * span, span)
    gains = my_gains.reshape(rcv_count, rows, 1)

    def tiles_of(blocks, column):
        if rows % 128 == 0:
            return cut(blocks, column, gains)
        out = []
        for planes, first in blocks:
            cuts = [lax.dynamic_slice_in_dim(p, column * TILE_SIZE, TILE_SIZE, 1) for p in planes]
            gain = lax.dynamic_index_in_dim(gains, first, 0, keepdims=True)
            out.append((jnp.stack(cuts).astype(jnp.float32) * gain).astype(jnp.bfloat16))
        return jnp.stack(out)

    columns = []

    def spread(held, origins):
        held_by = [(held, 0)]
        bit = src_count // 2
        while bit:
            swap = [(i, i ^ bit) for i in range(src_count)]
            held_by += [(lax.ppermute(x, "src", swap), mask ^ bit) for x, mask in held_by]
            bit //= 2
        for pieces, mask in held_by:
            for index, first in enumerate(origins):
                columns.append((pieces, index, (src_index ^ mask) * span + first * rows, mask))

    def collect(blocks):
        spread(tiles_of(blocks, rcv_index), [first for _, first in blocks])

    steps = (rcv_count - 1) // 2
    rows_of = {0: (own, origin(0))}
    far = origin(half)
    if phased:
        across = [(order[i], order[(i + half) % rcv_count]) for i in range(rcv_count)]
        spread(lax.ppermute(tiles_of([(own, origin(0))], far), "rcv", across), [far])
    collect([rows_of[0]])
    ahead, behind = own, own
    trail = {}
    for step in range(1, steps + 1):
        ahead = tuple(lax.ppermute(p, "rcv", forward) for p in ahead)
        behind = tuple(lax.ppermute(p, "rcv", backward) for p in behind)
        rows_of[-step], rows_of[step] = (ahead, origin(-step)), (behind, origin(step))
        trail[step] = len(columns)
        collect([rows_of[-step], rows_of[step]])
    if not phased:
        if rcv_count % 2 == 0:
            last = (lax.ppermute(ahead[0], "rcv", forward), lax.ppermute(behind[1], "rcv", backward))
            rows_of[half] = (last, far)
            collect([rows_of[half]])
        row_buffers, row_starts, pieces, starts = [], [], [], []
        for planes, first in rows_of.values():
            row_buffers += [(planes[0], 0), (planes[1], 1)]
            row_starts += [first * rows] * 2
        for array, index, first, _ in columns:
            if index == 0:
                pieces.append(array)
            starts.append(first)
        return product(row_buffers, row_starts, pieces, starts, used, span, total)

    quarter = rcv_count // 4
    near = [quarter - 1, quarter, rcv_count - 1 - quarter, rcv_count - quarter]
    last = [
        lax.ppermute(p, "rcv", [(order[(i + d) % rcv_count], order[i]) for i in range(rcv_count) if i not in near])
        for p, d in ((ahead[0], -1), (behind[1], 1))
    ]
    taken = []
    for offset in (-1, 1):
        pairs = []
        for i in near:
            mate = rcv_count - 1 - i
            if (mate + offset) % rcv_count == (i + half) % rcv_count:
                pairs.append((order[mate], order[i]))
        taken.append([lax.ppermute(p, "rcv", pairs) for p in rows_of[offset][0]])
    is_near = jnp.any(place == jnp.asarray(near, jnp.int32))
    side = jnp.any(jnp.asarray([(rcv_count - 2 - i - i - half) % rcv_count == 0 for i in range(rcv_count)])[None, place])
    chosen = jnp.where(is_near, jnp.where(side, 1, 2), 0)

    def as_rows(offsets):
        return [(rows_of[o][0], rows_of[o][1] * rows) for o in offsets]

    inside = [0] + [o for step in range(1, steps) for o in (-step, step)]
    outside = [-steps, steps]
    early, late = columns[: trail[steps]], columns[trail[steps] :]
    out = job(
        None, as_rows(inside), early, [c[2] for c in late], used, span, total, True, False
    )
    packed = [(array, index, first, 0) for array, index, first, _ in late]
    out = job(out, as_rows(inside), packed, [], used, span, total, False, True)
    out = job(out, as_rows(outside), columns, [], used, span, total, True, False)
    candidates = (*last, *taken[0], *taken[1])
    return job(
        out, [(candidates, far * rows)], columns, [], used, span, total, True, False, [chosen]
    )


def solution(mesh):
    placed = (
        P(None, ("src", "rcv"), None),
        P(("src", "rcv"), None),
        P(),
        P("src", None, None),
        P("src", "rcv"),
    )
    return jax.shard_map(
        local, mesh=mesh, in_specs=placed, out_specs=P(None, "src", "rcv"), check_vma=False
    )
```

profile of v0, /device:TPU:18, one launch (start us, length us, event | category | flops | bytes accessed | tf_op | source)
XLA Modules:
  0.0 319.2 jit_solution(15878007691894006284)
XLA Ops:
  0.0 4.0 %shard_map.94 = (bf16[32,128,128]{2,1,0:T(8,128)(2,1)}, bf16[32,128,128]{2,1,0:T(8,128)(2,1)}) custom-call(bf16[2,128,4096]{2,1,0:T(8,128)(2,1)} %data_ref.5), custom_call_target="tpu_custom_call" | custom-call | tf_op jit(solution)/shard_map/pallas_call | solution.py:29
  4.0 29.9 %all_to_all.10.arrived_ref = bf16[32,128,128]{2,1,0:T(8,128)(2,1)} all-to-all(bf16[32,128,128]{2,1,0:T(8,128)(2,1)} %get-tuple-element.7), channel_id=1, replica_groups=mesh['src'=4,'rcv'=8] {'src','rcv'}, dimensions={0} | all-to-all | bytes 2097152 | tf_op jit(solution)/shard_map/all_to_all | solution.py:352
  33.9 6.2 %all-to-all-start.1 = ((bf16[32,128,128]{2,1,0:T(8,128)(2,1)}), bf16[32,128,128]{2,1,0:T(8,128)(2,1)S(1)}, u32[]{:S(2)}, u32[]{:S(2)}) async-start(bf16[32,128,128]{2,1,0:T(8,128)(2,1)} %get-tuple-element.8), calls=%async_computation.1 | async-start | bytes 2097152 | tf_op jit(solution)/shard_map/all_to_all | solution.py:352
  40.1 4.1 %shard_map.95.refs_0_ = bf16[128,4096]{1,0:T(8,128)(2,1)} custom-call(bf16[2,128,4096]{2,1,0:T(8,128)(2,1)} %data_ref.5, s32[128,4096]{1,0:T(8,128)} %mask_ref.3, bf16[32,128,128]{2,1,0:T(8,128)(2,1)} %all_to_all.10.arrived_ref), custom_call_target="tpu_custom_call" | custom-call | tf_op jit(solution)/shard_map/pallas_call | solution.py:54
  44.8 19.4 %all-to-all-done.1.arrived_ref = bf16[32,128,128]{2,1,0:T(8,128)(2,1)S(1)} async-done(((bf16[32,128,128]{2,1,0:T(8,128)(2,1)}), bf16[32,128,128]{2,1,0:T(8,128)(2,1)S(1)}, u32[]{:S(2)}, u32[]{:S(2)}) %all-to-all-start.1) | async-done | bytes 1048608 | tf_op jit(solution)/shard_map/all_to_all | solution.py:352
  65.1 4.1 %shard_map.96.refs_1_ = bf16[128,4096]{1,0:T(8,128)(2,1)} custom-call(bf16[2,128,4096]{2,1,0:T(8,128)(2,1)} %data_ref.5, s32[128,4096]{1,0:T(8,128)} %mask_ref.3, bf16[32,128,128]{2,1,0:T(8,128)(2,1)} %copy-done.11), custom_call_target="tpu_custom_call" | custom-call | tf_op jit(solution)/shard_map/pallas_call | solution.py:54
  73.1 13.2 %collective-permute-done.refs_0_.refs_2_ = bf16[128,4096]{1,0:T(8,128)(2,1)S(1)} collective-permute-done((bf16[128,4096]{1,0:T(8,128)(2,1)}, bf16[128,4096]{1,0:T(8,128)(2,1)S(1)}, u32[]{:S(2)}, u32[]{:S(2)}) %collective-permute-start) | collective-permute-done | bytes 1048608 | tf_op jit(solution)/shard_map/ppermute | solution.py:406
  88.7 6.8 %collective-permute-done.4.refs_4_.refs_5_ = bf16[128,4096]{1,0:T(8,128)(2,1)S(1)} collective-permute-done((bf16[128,4096]{1,0:T(8,128)(2,1)}, bf16[128,4096]{1,0:T(8,128)(2,1)S(1)}, u32[]{:S(2)}, u32[]{:S(2)}) %collective-permute-start.4) | collective-permute-done | bytes 1048608 | tf_op jit(solution)/shard_map/ppermute | solution.py:407
  97.3 11.5 %collective-permute-done.9.refs_1_.refs_3_ = bf16[128,4096]{1,0:T(8,128)(2,1)} collective-permute-done((bf16[128,4096]{1,0:T(8,128)(2,1)}, bf16[128,4096]{1,0:T(8,128)(2,1)}, u32[]{:S(2)}, u32[]{:S(2)}) %collective-permute-start.9) | collective-permute-done | bytes 1048608 | tf_op jit(solution)/shard_map/ppermute | solution.py:406
  108.8 2.5 collective-permute-start.24
  111.3 6.8 %collective-permute-done.11.refs_3_.refs_4_ = bf16[128,4096]{1,0:T(8,128)(2,1)} collective-permute-done((bf16[128,4096]{1,0:T(8,128)(2,1)S(1)}, bf16[128,4096]{1,0:T(8,128)(2,1)}, u32[]{:S(2)}, u32[]{:S(2)}) %collective-permute-start.11) | collective-permute-done | bytes 1048608 | tf_op jit(solution)/shard_map/ppermute | solution.py:407
  135.2 2.5 shard_map.97
  137.7 2.4 collective-permute-start.14
  142.3 17.0 %collective-permute-done.24.refs_1_.refs_7_ = bf16[128,4096]{1,0:T(8,128)(2,1)} collective-permute-done((bf16[128,4096]{1,0:T(8,128)(2,1)}, bf16[128,4096]{1,0:T(8,128)(2,1)}, u32[]{:S(2)}, u32[]{:S(2)}) %collective-permute-start.24) | collective-permute-done | bytes 1048608 | tf_op jit(solution)/shard_map/ppermute | solution.py:406
  159.3 2.5 collective-permute-start.29
  166.4 2.4 shard_map.98.refs_14_.refs_8_.refs_10_
  168.8 5.0 %collective-permute-start.18 = (bf16[1,2,128,512]{3,2,1,0:T(8,128)(2,1)}, bf16[1,2,128,512]{3,2,1,0:T(8,128)(2,1)}, u32[]{:S(2)}, u32[]{:S(2)}) collective-permute-start(bf16[1,2,128,512]{3,2,1,0:T(8,128)(2,1)} %shard_map.98.refs_14_.refs_8_.refs_10_), channel_id=1, source_target_pairs={{0,16},{8,24},{16,0},{24,8},{1,17},{9,25},{17,1},{25,9},{2,18},{10... | collective-permute-start | bytes 786440 | tf_op jit(solution)/shard_map/ppermute | solution.py:387
  173.8 6.2 %collective-permute-done.18.refs_15_.refs_9_.refs_11_ = bf16[1,2,128,512]{3,2,1,0:T(8,128)(2,1)} collective-permute-done((bf16[1,2,128,512]{3,2,1,0:T(8,128)(2,1)}, bf16[1,2,128,512]{3,2,1,0:T(8,128)(2,1)}, u32[]{:S(2)}, u32[]{:S(2)}) %collective-permute-start.18) | collective-permute-done | bytes 262176 | tf_op jit(solution)/shard_map/ppermute | solution.py:387
  182.7 2.8 shard_map.99.refs_18_.refs_12_.refs_14_
  185.5 4.0 %collective-permute-done.15.refs_11_.refs_5_.refs_7_ = bf16[1,2,128,512]{3,2,1,0:T(8,128)(2,1)} collective-permute-done((bf16[1,2,128,512]{3,2,1,0:T(8,128)(2,1)}, bf16[1,2,128,512]{3,2,1,0:T(8,128)(2,1)}, u32[]{:S(2)}, u32[]{:S(2)}) %collective-permute-start.15) | collective-permute-done | bytes 262176 | tf_op jit(solution)/shard_map/ppermute | solution.py:387
  190.3 6.3 %collective-permute-done.6.refs_4_.refs_3_ = bf16[128,4096]{1,0:T(8,128)(2,1)} collective-permute-done((bf16[128,4096]{1,0:T(8,128)(2,1)}, bf16[128,4096]{1,0:T(8,128)(2,1)}, u32[]{:S(2)}, u32[]{:S(2)}) %collective-permute-start.6) | collective-permute-done | bytes 1048608 | tf_op jit(solution)/shard_map/ppermute | solution.py:407
  196.7 12.7 %collective-permute-done.29.refs_1_ = bf16[128,4096]{1,0:T(8,128)(2,1)} collective-permute-done((bf16[128,4096]{1,0:T(8,128)(2,1)}, bf16[128,4096]{1,0:T(8,128)(2,1)}, u32[]{:S(2)}, u32[]{:S(2)}) %collective-permute-start.29) | collective-permute-done | bytes 1048608 | tf_op jit(solution)/shard_map/ppermute | solution.py:406
  209.3 9.0 %collective-permute-done.30.refs_3_.refs_2_ = bf16[128,4096]{1,0:T(8,128)(2,1)} collective-permute-done((bf16[128,4096]{1,0:T(8,128)(2,1)S(1)}, bf16[128,4096]{1,0:T(8,128)(2,1)}, u32[]{:S(2)}, u32[]{:S(2)}) %collective-permute-start.30) | collective-permute-done | bytes 1048608 | tf_op jit(solution)/shard_map/ppermute | solution.py:407
  221.9 2.8 shard_map.100.refs_22_.refs_16_.refs_18_
  224.7 3.0 shard_map.101.refs_10_.refs_20_.refs_22_
  239.4 3.8 %collective-permute-done.26.refs_23_.refs_17_.refs_19_ = bf16[2,2,128,512]{3,2,1,0:T(8,128)(2,1)} collective-permute-done((bf16[2,2,128,512]{3,2,1,0:T(8,128)(2,1)S(1)}, bf16[2,2,128,512]{3,2,1,0:T(8,128)(2,1)}, u32[]{:S(2)}, u32[]{:S(2)}) %collective-permute-start.26) | collective-permute-done | bytes 524320 | tf_op jit(solution)/shard_map/ppermute | solution.py:387
  243.7 9.7 %collective-permute-done.31.refs_11_.refs_21_.refs_23_ = bf16[2,2,128,512]{3,2,1,0:T(8,128)(2,1)S(1)} collective-permute-done((bf16[2,2,128,512]{3,2,1,0:T(8,128)(2,1)}, bf16[2,2,128,512]{3,2,1,0:T(8,128)(2,1)S(1)}, u32[]{:S(2)}, u32[]{:S(2)}) %collective-permute-start.31) | collective-permute-done | bytes 524320 | tf_op jit(solution)/shard_map/ppermute | solution.py:387
  258.6 3.7 %collective-permute-start.12 = (bf16[128,4096]{1,0:T(8,128)(2,1)}, bf16[128,4096]{1,0:T(8,128)(2,1)}, u32[]{:S(2)}, u32[]{:S(2)}) collective-permute-start(bf16[128,4096]{1,0:T(8,128)(2,1)} %collective-permute-done.11.refs_3_.refs_4_), channel_id=1, source_target_pairs={{5,4},{2,3},{13,12},{10,11},{21,20},{18,19},{29,28},{26,27}} | collective-permute-start | bytes 3145736 | tf_op jit(solution)/shard_map/ppermute | solution.py:439
  269.8 20.7 %shard_map.102.refs_14_ = f32[2,1024,512]{2,1,0:T(8,128)} custom-call(s32[37]{0:T(128)} %stack.128.plan_ref, s32[2,8]{1,0:T(2,128)} %convert_element_type.3.used_ref, bf16[128,4096]{1,0:T(8,128)(2,1)} %shard_map.95.refs_0_, bf16[128,4096]{1,0:T(8,128)(2,1)} %shard_map.96.refs_1_, bf16[128,4096]{1,0:T(8,128)(2,1)} %copy-done.7, ...), custom_call_target="tpu_custom_call" | custom-call | flops 10737418240 | bytes 21495808 | tf_op jit(solution)/shard_map/pallas_call | solution.py:307
  290.5 8.8 %shard_map.103.refs_24_ = f32[2,1024,512]{2,1,0:T(8,128)} custom-call(s32[13]{0:T(128)} %stack.127.plan_ref, s32[2,8]{1,0:T(2,128)} %convert_element_type.3.used_ref, bf16[128,4096]{1,0:T(8,128)(2,1)} %shard_map.95.refs_0_, bf16[128,4096]{1,0:T(8,128)(2,1)} %shard_map.96.refs_1_, bf16[128,4096]{1,0:T(8,128)(2,1)} %copy-done.7, ...), custom_call_target="tpu_custom_call", output_to_operand_aliasing={{}: (16, {})} | custom-call | flops 2684354560 | bytes 7340032 | tf_op jit(solution)/shard_map/pallas_call | solution.py:307
  299.3 11.4 %shard_map.104.refs_26_ = f32[2,1024,512]{2,1,0:T(8,128)} custom-call(s32[34]{0:T(128)} %stack.126.plan_ref, s32[2,8]{1,0:T(2,128)} %convert_element_type.3.used_ref, bf16[128,4096]{1,0:T(8,128)(2,1)} %collective-permute-done.2.refs_0_, bf16[128,4096]{1,0:T(8,128)(2,1)} %collective-permute-done.29.refs_1_, ...), custom_call_target="tpu_custom_call", output_to_operand_aliasing={{}: (26, {})} | custom-call | flops 4294967296 | bytes 13631488 | tf_op jit(solution)/shard_map/pallas_call | solution.py:307
  310.8 8.3 %shard_map.105 = f32[2,1024,512]{2,1,0:T(8,128)} custom-call(s32[34]{0:T(128)} %stack.119.plan_ref, s32[2,8]{1,0:T(2,128)} %convert_element_type.3.used_ref, bf16[128,4096]{1,0:T(8,128)(2,1)} %collective-permute-done.3.refs_0_, bf16[128,4096]{1,0:T(8,128)(2,1)} %collective-permute-done.7.refs_1_, ...), custom_call_target="tpu_custom_call", output_to_operand_aliasing={{}: (28, {})} | custom-call | flops 2147483648 | bytes 11010048 | tf_op jit(solution)/shard_map/pallas_call | solution.py:307
  (108 shorter events, 47.9 us)
Async XLA Ops:
  33.9 30.3 %all-to-all-start.1 = ((bf16[32,128,128]{2,1,0:T(8,128)(2,1)}), bf16[32,128,128]{2,1,0:T(8,128)(2,1)S(1)}, u32[]{:S(2)}, u32[]{:S(2)}) async-start(bf16[32,128,128]{2,1,0:T(8,128)(2,1)} %get-tuple-element.8), calls=%async_computation.1 | async-start | bytes 2097152 | tf_op jit(solution)/shard_map/all_to_all | solution.py:352
  44.2 42.1 %collective-permute-start = (bf16[128,4096]{1,0:T(8,128)(2,1)}, bf16[128,4096]{1,0:T(8,128)(2,1)S(1)}, u32[]{:S(2)}, u32[]{:S(2)}) collective-permute-start(bf16[128,4096]{1,0:T(8,128)(2,1)} %shard_map.95.refs_0_), channel_id=1, source_target_pairs={{0,2},{2,4},{4,6},{6,7},{7,5},{5,3},{3,1},{1,0},{8,10},{10,12},{12... | collective-permute-start | bytes 3145736 | tf_op jit(solution)/shard_map/ppermute | solution.py:406
  69.2 26.2 %collective-permute-start.4 = (bf16[128,4096]{1,0:T(8,128)(2,1)}, bf16[128,4096]{1,0:T(8,128)(2,1)S(1)}, u32[]{:S(2)}, u32[]{:S(2)}) collective-permute-start(bf16[128,4096]{1,0:T(8,128)(2,1)} %shard_map.96.refs_1_), channel_id=1, source_target_pairs={{2,0},{4,2},{6,4},{7,6},{5,7},{3,5},{1,3},{0,1},{10,8},{12,10},{14... | collective-permute-start | bytes 3145736 | tf_op jit(solution)/shard_map/ppermute | solution.py:407
  71.1 37.7 %collective-permute-start.9 = (bf16[128,4096]{1,0:T(8,128)(2,1)}, bf16[128,4096]{1,0:T(8,128)(2,1)}, u32[]{:S(2)}, u32[]{:S(2)}) collective-permute-start(bf16[128,4096]{1,0:T(8,128)(2,1)} %shard_map.96.refs_1_), channel_id=1, source_target_pairs={{0,2},{2,4},{4,6},{6,7},{7,5},{5,3},{3,1},{1,0},{8,10},{10,12},{12... | collective-permute-start | bytes 3145736 | tf_op jit(solution)/shard_map/ppermute | solution.py:406
  71.2 46.8 %collective-permute-start.11 = (bf16[128,4096]{1,0:T(8,128)(2,1)S(1)}, bf16[128,4096]{1,0:T(8,128)(2,1)}, u32[]{:S(2)}, u32[]{:S(2)}) collective-permute-start(bf16[128,4096]{1,0:T(8,128)(2,1)S(1)} %copy-done.1), channel_id=1, source_target_pairs={{2,0},{4,2},{6,4},{7,6},{5,7},{3,5},{1,3},{0,1},{10,8},{12,10},{14... | collective-permute-start | bytes 3145736 | tf_op jit(solution)/shard_map/ppermute | solution.py:407
  86.3 53.7 %collective-permute-start.1 = (bf16[128,4096]{1,0:T(8,128)(2,1)S(1)}, bf16[128,4096]{1,0:T(8,128)(2,1)}, u32[]{:S(2)}, u32[]{:S(2)}) collective-permute-start(bf16[128,4096]{1,0:T(8,128)(2,1)S(1)} %collective-permute-done.refs_0_.refs_2_), channel_id=1, source_target_pairs={{0,2},{2,4},{4,6},{6,7},{7,5},{5,3},{3,1},{1,0},{8,10},{10,12},{12... | collective-permute-start | bytes 3145736 | tf_op jit(solution)/shard_map/ppermute | solution.py:406
  95.5 45.0 %collective-permute-start.5 = (bf16[128,4096]{1,0:T(8,128)(2,1)S(1)}, bf16[128,4096]{1,0:T(8,128)(2,1)}, u32[]{:S(2)}, u32[]{:S(2)}) collective-permute-start(bf16[128,4096]{1,0:T(8,128)(2,1)S(1)} %collective-permute-done.4.refs_4_.refs_5_), channel_id=1, source_target_pairs={{2,0},{4,2},{6,4},{7,6},{5,7},{3,5},{1,3},{0,1},{10,8},{12,10},{14... | collective-permute-start | bytes 3145736 | tf_op jit(solution)/shard_map/ppermute | solution.py:407
  108.8 50.6 %collective-permute-start.24 = (bf16[128,4096]{1,0:T(8,128)(2,1)}, bf16[128,4096]{1,0:T(8,128)(2,1)}, u32[]{:S(2)}, u32[]{:S(2)}) collective-permute-start(bf16[128,4096]{1,0:T(8,128)(2,1)} %collective-permute-done.9.refs_1_.refs_3_), channel_id=1, source_target_pairs={{0,2},{2,4},{4,6},{6,7},{7,5},{5,3},{3,1},{1,0},{8,10},{10,12},{12... | collective-permute-start | bytes 3145736 | tf_op jit(solution)/shard_map/ppermute | solution.py:406
  118.0 44.9 %collective-permute-start.25 = (bf16[128,4096]{1,0:T(8,128)(2,1)}, bf16[128,4096]{1,0:T(8,128)(2,1)S(1)}, u32[]{:S(2)}, u32[]{:S(2)}) collective-permute-start(bf16[128,4096]{1,0:T(8,128)(2,1)} %collective-permute-done.11.refs_3_.refs_4_), channel_id=1, source_target_pairs={{2,0},{4,2},{6,4},{7,6},{5,7},{3,5},{1,3},{0,1},{10,8},{12,10},{14... | collective-permute-start | bytes 3145736 | tf_op jit(solution)/shard_map/ppermute | solution.py:407
  137.7 31.2 %collective-permute-start.14 = (bf16[1,2,128,512]{3,2,1,0:T(8,128)(2,1)}, bf16[1,2,128,512]{3,2,1,0:T(8,128)(2,1)}, u32[]{:S(2)}, u32[]{:S(2)}) collective-permute-start(bf16[1,2,128,512]{3,2,1,0:T(8,128)(2,1)} %shard_map.97), channel_id=1, source_target_pairs={{0,7},{2,5},{4,3},{6,1},{7,0},{5,2},{3,4},{1,6},{8,15},{10,13},{12... | collective-permute-start | bytes 786440 | tf_op jit(solution)/shard_map/ppermute | solution.py:401
  140.1 50.3 %collective-permute-start.2 = (bf16[128,4096]{1,0:T(8,128)(2,1)}, bf16[128,4096]{1,0:T(8,128)(2,1)}, u32[]{:S(2)}, u32[]{:S(2)}) collective-permute-start(bf16[128,4096]{1,0:T(8,128)(2,1)} %collective-permute-done.1.refs_0_.refs_6_), channel_id=1, source_target_pairs={{0,2},{2,4},{4,6},{6,7},{7,5},{5,3},{3,1},{1,0},{8,10},{10,12},{12... | collective-permute-start | bytes 3145736 | tf_op jit(solution)/shard_map/ppermute | solution.py:406
  140.5 56.2 %collective-permute-start.6 = (bf16[128,4096]{1,0:T(8,128)(2,1)}, bf16[128,4096]{1,0:T(8,128)(2,1)}, u32[]{:S(2)}, u32[]{:S(2)}) collective-permute-start(bf16[128,4096]{1,0:T(8,128)(2,1)} %collective-permute-done.5.refs_4_.refs_9_), channel_id=1, source_target_pairs={{2,0},{4,2},{6,4},{7,6},{5,7},{3,5},{1,3},{0,1},{10,8},{12,10},{14... | collective-permute-start | bytes 3145736 | tf_op jit(solution)/shard_map/ppermute | solution.py:407
  159.3 50.0 %collective-permute-start.29 = (bf16[128,4096]{1,0:T(8,128)(2,1)}, bf16[128,4096]{1,0:T(8,128)(2,1)}, u32[]{:S(2)}, u32[]{:S(2)}) collective-permute-start(bf16[128,4096]{1,0:T(8,128)(2,1)} %collective-permute-done.24.refs_1_.refs_7_), channel_id=1, source_target_pairs={{0,2},{2,4},{4,6},{6,7},{7,5},{5,3},{3,1},{1,0},{8,10},{10,12},{12... | collective-permute-start | bytes 3145736 | tf_op jit(solution)/shard_map/ppermute | solution.py:406
  162.9 55.4 %collective-permute-start.30 = (bf16[128,4096]{1,0:T(8,128)(2,1)S(1)}, bf16[128,4096]{1,0:T(8,128)(2,1)}, u32[]{:S(2)}, u32[]{:S(2)}) collective-permute-start(bf16[128,4096]{1,0:T(8,128)(2,1)S(1)} %collective-permute-done.25.refs_3_.refs_8_), channel_id=1, source_target_pairs={{2,0},{4,2},{6,4},{7,6},{5,7},{3,5},{1,3},{0,1},{10,8},{12,10},{14... | collective-permute-start | bytes 3145736 | tf_op jit(solution)/shard_map/ppermute | solution.py:407
  189.5 40.0 %collective-permute-start.21 = (bf16[2,2,128,512]{3,2,1,0:T(8,128)(2,1)}, bf16[2,2,128,512]{3,2,1,0:T(8,128)(2,1)S(1)}, u32[]{:S(2)}, u32[]{:S(2)}) collective-permute-start(bf16[2,2,128,512]{3,2,1,0:T(8,128)(2,1)} %shard_map.99.refs_18_.refs_12_.refs_14_), channel_id=1, source_target_pairs={{0,16},{8,24},{16,0},{24,8},{1,17},{9,25},{17,1},{25,9},{2,18},{10... | collective-permute-start | bytes 1572872 | tf_op jit(solution)/shard_map/ppermute | solution.py:387
  190.3 37.4 %collective-permute-start.19 = (bf16[1,2,128,512]{3,2,1,0:T(8,128)(2,1)S(1)}, bf16[1,2,128,512]{3,2,1,0:T(8,128)(2,1)}, u32[]{:S(2)}, u32[]{:S(2)}) collective-permute-start(bf16[1,2,128,512]{3,2,1,0:T(8,128)(2,1)S(1)} %copy-done.12), channel_id=1, source_target_pairs={{0,8},{8,0},{16,24},{24,16},{1,9},{9,1},{17,25},{25,17},{2,10},{10... | collective-permute-start | bytes 786440 | tf_op jit(solution)/shard_map/ppermute | solution.py:387
  196.7 31.6 %collective-permute-start.16 = (bf16[1,2,128,512]{3,2,1,0:T(8,128)(2,1)}, bf16[1,2,128,512]{3,2,1,0:T(8,128)(2,1)}, u32[]{:S(2)}, u32[]{:S(2)}) collective-permute-start(bf16[1,2,128,512]{3,2,1,0:T(8,128)(2,1)} %collective-permute-done.14.refs_10_.refs_4_.refs_6_), channel_id=1, source_target_pairs={{0,8},{8,0},{16,24},{24,16},{1,9},{9,1},{17,25},{25,17},{2,10},{10... | collective-permute-start | bytes 786440 | tf_op jit(solution)/shard_map/ppermute | solution.py:387
  209.3 20.1 %collective-permute-start.20 = (bf16[1,2,128,512]{3,2,1,0:T(8,128)(2,1)}, bf16[1,2,128,512]{3,2,1,0:T(8,128)(2,1)}, u32[]{:S(2)}, u32[]{:S(2)}) collective-permute-start(bf16[1,2,128,512]{3,2,1,0:T(8,128)(2,1)} %collective-permute-done.18.refs_15_.refs_9_.refs_11_), channel_id=1, source_target_pairs={{0,8},{8,0},{16,24},{24,16},{1,9},{9,1},{17,25},{25,17},{2,10},{10... | collective-permute-start | bytes 786440 | tf_op jit(solution)/shard_map/ppermute | solution.py:387
  218.3 12.1 %collective-permute-start.17 = (bf16[1,2,128,512]{3,2,1,0:T(8,128)(2,1)}, bf16[1,2,128,512]{3,2,1,0:T(8,128)(2,1)}, u32[]{:S(2)}, u32[]{:S(2)}) collective-permute-start(bf16[1,2,128,512]{3,2,1,0:T(8,128)(2,1)} %collective-permute-done.15.refs_11_.refs_5_.refs_7_), channel_id=1, source_target_pairs={{0,8},{8,0},{16,24},{24,16},{1,9},{9,1},{17,25},{25,17},{2,10},{10... | collective-permute-start | bytes 786440 | tf_op jit(solution)/shard_map/ppermute | solution.py:387
  228.3 14.9 %collective-permute-start.26 = (bf16[2,2,128,512]{3,2,1,0:T(8,128)(2,1)S(1)}, bf16[2,2,128,512]{3,2,1,0:T(8,128)(2,1)}, u32[]{:S(2)}, u32[]{:S(2)}) collective-permute-start(bf16[2,2,128,512]{3,2,1,0:T(8,128)(2,1)S(1)} %copy-done.3), channel_id=1, source_target_pairs={{0,16},{8,24},{16,0},{24,8},{1,17},{9,25},{17,1},{25,9},{2,18},{10... | collective-permute-start | bytes 1572872 | tf_op jit(solution)/shard_map/ppermute | solution.py:387
  229.4 13.8 %collective-permute-start.23 = (bf16[2,2,128,512]{3,2,1,0:T(8,128)(2,1)S(1)}, bf16[2,2,128,512]{3,2,1,0:T(8,128)(2,1)}, u32[]{:S(2)}, u32[]{:S(2)}) collective-permute-start(bf16[2,2,128,512]{3,2,1,0:T(8,128)(2,1)S(1)} %collective-permute-done.21.refs_19_.refs_13_.refs_15_), channel_id=1, source_target_pairs={{0,8},{8,0},{16,24},{24,16},{1,9},{9,1},{17,25},{25,17},{2,10},{10... | collective-permute-start | bytes 1572872 | tf_op jit(solution)/shard_map/ppermute | solution.py:387
  229.4 24.0 %collective-permute-start.31 = (bf16[2,2,128,512]{3,2,1,0:T(8,128)(2,1)}, bf16[2,2,128,512]{3,2,1,0:T(8,128)(2,1)S(1)}, u32[]{:S(2)}, u32[]{:S(2)}) collective-permute-start(bf16[2,2,128,512]{3,2,1,0:T(8,128)(2,1)} %shard_map.101.refs_10_.refs_20_.refs_22_), channel_id=1, source_target_pairs={{0,16},{8,24},{16,0},{24,8},{1,17},{9,25},{17,1},{25,9},{2,18},{10... | collective-permute-start | bytes 1572872 | tf_op jit(solution)/shard_map/ppermute | solution.py:387
  230.4 28.2 %collective-permute-start.10 = (bf16[128,4096]{1,0:T(8,128)(2,1)}, bf16[128,4096]{1,0:T(8,128)(2,1)}, u32[]{:S(2)}, u32[]{:S(2)}) collective-permute-start(bf16[128,4096]{1,0:T(8,128)(2,1)} %collective-permute-done.9.refs_1_.refs_3_), channel_id=1, source_target_pairs={{3,2},{4,5},{11,10},{12,13},{19,18},{20,21},{27,26},{28,29}} | collective-permute-start | bytes 3145736 | tf_op jit(solution)/shard_map/ppermute | solution.py:439
  239.1 23.2 %collective-permute-start.27 = (bf16[2,2,128,512]{3,2,1,0:T(8,128)(2,1)S(1)}, bf16[2,2,128,512]{3,2,1,0:T(8,128)(2,1)}, u32[]{:S(2)}, u32[]{:S(2)}) collective-permute-start(bf16[2,2,128,512]{3,2,1,0:T(8,128)(2,1)S(1)} %copy-done.3), channel_id=1, source_target_pairs={{0,8},{8,0},{16,24},{24,16},{1,9},{9,1},{17,25},{25,17},{2,10},{10... | collective-permute-start | bytes 1572872 | tf_op jit(solution)/shard_map/ppermute | solution.py:387
  243.2 21.4 %collective-permute-start.28 = (bf16[2,2,128,512]{3,2,1,0:T(8,128)(2,1)}, bf16[2,2,128,512]{3,2,1,0:T(8,128)(2,1)}, u32[]{:S(2)}, u32[]{:S(2)}) collective-permute-start(bf16[2,2,128,512]{3,2,1,0:T(8,128)(2,1)} %collective-permute-done.26.refs_23_.refs_17_.refs_19_), channel_id=1, source_target_pairs={{0,8},{8,0},{16,24},{24,16},{1,9},{9,1},{17,25},{25,17},{2,10},{10... | collective-permute-start | bytes 1572872 | tf_op jit(solution)/shard_map/ppermute | solution.py:387
  243.2 22.7 %collective-permute-start.32 = (bf16[2,2,128,512]{3,2,1,0:T(8,128)(2,1)}, bf16[2,2,128,512]{3,2,1,0:T(8,128)(2,1)S(1)}, u32[]{:S(2)}, u32[]{:S(2)}) collective-permute-start(bf16[2,2,128,512]{3,2,1,0:T(8,128)(2,1)} %shard_map.101.refs_10_.refs_20_.refs_22_), channel_id=1, source_target_pairs={{0,8},{8,0},{16,24},{24,16},{1,9},{9,1},{17,25},{25,17},{2,10},{10... | collective-permute-start | bytes 1572872 | tf_op jit(solution)/shard_map/ppermute | solution.py:387
  253.4 14.1 %collective-permute-start.33 = (bf16[2,2,128,512]{3,2,1,0:T(8,128)(2,1)S(1)}, bf16[2,2,128,512]{3,2,1,0:T(8,128)(2,1)S(1)}, u32[]{:S(2)}, u32[]{:S(2)}) collective-permute-start(bf16[2,2,128,512]{3,2,1,0:T(8,128)(2,1)S(1)} %collective-permute-done.31.refs_11_.refs_21_.refs_23_), channel_id=1, source_target_pairs={{0,8},{8,0},{16,24},{24,16},{1,9},{9,1},{17,25},{25,17},{2,10},{10... | collective-permute-start | bytes 1572872 | tf_op jit(solution)/shard_map/ppermute | solution.py:387
  258.6 52.2 %collective-permute-start.12 = (bf16[128,4096]{1,0:T(8,128)(2,1)}, bf16[128,4096]{1,0:T(8,128)(2,1)}, u32[]{:S(2)}, u32[]{:S(2)}) collective-permute-start(bf16[128,4096]{1,0:T(8,128)(2,1)} %collective-permute-done.11.refs_3_.refs_4_), channel_id=1, source_target_pairs={{5,4},{2,3},{13,12},{10,11},{21,20},{18,19},{29,28},{26,27}} | collective-permute-start | bytes 3145736 | tf_op jit(solution)/shard_map/ppermute | solution.py:439
  262.3 48.4 %collective-permute-start.13 = (bf16[128,4096]{1,0:T(8,128)(2,1)}, bf16[128,4096]{1,0:T(8,128)(2,1)}, u32[]{:S(2)}, u32[]{:S(2)}) collective-permute-start(bf16[128,4096]{1,0:T(8,128)(2,1)} %copy-done.9), channel_id=1, source_target_pairs={{5,4},{2,3},{13,12},{10,11},{21,20},{18,19},{29,28},{26,27}} | collective-permute-start | bytes 3145736 | tf_op jit(solution)/shard_map/ppermute | solution.py:439
  264.6 46.2 %collective-permute-start.8 = (bf16[128,4096]{1,0:T(8,128)(2,1)S(1)}, bf16[128,4096]{1,0:T(8,128)(2,1)}, u32[]{:S(2)}, u32[]{:S(2)}) collective-permute-start(bf16[128,4096]{1,0:T(8,128)(2,1)S(1)} %copy-done.8), channel_id=1, source_target_pairs={{3,2},{4,5},{11,10},{12,13},{19,18},{20,21},{27,26},{28,29}} | collective-permute-start | bytes 3145736 | tf_op jit(solution)/shard_map/ppermute | solution.py:439
  265.9 44.9 %collective-permute-start.3 = (bf16[128,4096]{1,0:T(8,128)(2,1)}, bf16[128,4096]{1,0:T(8,128)(2,1)}, u32[]{:S(2)}, u32[]{:S(2)}) collective-permute-start(bf16[128,4096]{1,0:T(8,128)(2,1)} %collective-permute-done.2.refs_0_), channel_id=1, source_target_pairs={{1,0},{4,6},{6,7},{3,1},{9,8},{12,14},{14,15},{11,9},{17,16},{20,2... | collective-permute-start | bytes 3145736 | tf_op jit(solution)/shard_map/ppermute | solution.py:429
  267.6 43.2 %collective-permute-start.7 = (bf16[128,4096]{1,0:T(8,128)(2,1)}, bf16[128,4096]{1,0:T(8,128)(2,1)}, u32[]{:S(2)}, u32[]{:S(2)}) collective-permute-start(bf16[128,4096]{1,0:T(8,128)(2,1)} %collective-permute-done.6.refs_4_.refs_3_), channel_id=1, source_target_pairs={{2,0},{7,6},{5,7},{0,1},{10,8},{15,14},{13,15},{8,9},{18,16},{23,2... | collective-permute-start | bytes 3145736 | tf_op jit(solution)/shard_map/ppermute | solution.py:429
  (22 other events, 941.1 us)
where the time goes:
time: 323 us; the launch traced here: 319 us
  waiting for transfers between devices  128 us (40%)
  Pallas kernels  74.7 us (23%)
  starting transfers between devices  51.2 us (16%)
  blocking collectives  29.9 us (9%)
  between operations  18.2 us (6%)
  other arithmetic  11.1 us (3%)
  local copies, waits for them, and re-layouts  6.54 us (2%)
    ppermute x6, waiting for transfers between devices, local(): ahead = tuple((lax.ppermute(p, 'rcv', forward) for p in ahead))  54.4 us
    pallas_call x4, Pallas kernels, job(): pl.pallas_call(kernel, out_shape=jax.ShapeDtypeStruct((2, span, TILE_SIZE...  49.1 us
    ppermute x6, waiting for transfers between devices, local(): behind = tuple((lax.ppermute(p, 'rcv', backward) for p in behind))  30.1 us
    all_to_all x1, blocking collectives, local(): lax.all_to_all(b, ('src', 'rcv'), split_axis=0, concat_axis=0, tiled=True)  29.9 us
    ppermute x15, waiting for transfers between devices, spread(): lax.ppermute(x, 'src', swap)  23.7 us
    all_to_all x1, waiting for transfers between devices, local(): lax.all_to_all(b, ('src', 'rcv'), split_axis=0, concat_axis=0, tiled=True)  19.4 us
    pallas_call x5, Pallas kernels, cut(): pl.pallas_call(cut_kernel, out_shape=jax.ShapeDtypeStruct(shape, jnp.bflo...  13.4 us
    ppermute x6, starting transfers between devices, local(): behind = tuple((lax.ppermute(p, 'rcv', backward) for p in behind))  11.4 us
  transfers between devices with their start and end apart: 35, of which 15 were waited for; matrix products, arithmetic and copies ran while one was open for 5% of the time, Pallas kernels for 20%

commit v1 on v0

--- a/solution.py
+++ b/solution.py
@@ -1,11 +1,11 @@
-import functools
-
 import jax
 import jax.numpy as jnp
+import numpy as np
 from jax import lax
 from jax.experimental import pallas as pl
 from jax.experimental.pallas import tpu as pltpu
 from jax.sharding import PartitionSpec as P
+
 
 TILE_SIZE = 512
 
@@ -22,7 +22,7 @@
 
 
 def transposed_blocks(data, devices):
-    _, rows, total = data.shape
+    _, rows, _ = data.shape
     if rows % 128:
         return tuple(jnp.transpose(p.reshape(rows, devices, rows), (1, 0, 2)) for p in data)
     group = 8
@@ -64,7 +64,7 @@
     )(data, mask, arrived)
 
 
-def product_kernel(rows, src_count, plan_ref, used_ref, *refs):
+def product_kernel(rows, plan_ref, used_ref, *refs):
     (row_refs, piece_refs), out_ref, scratch = refs[0], refs[1], refs[2:]
     left, right, row_sem, piece_sem = scratch
     inner_tiles = right.shape[0]
@@ -138,7 +138,7 @@
         ins = refs[: len(arrays)]
         row_refs = list(zip(ins[: len(parts)], parts))
         product_kernel(
-            rows, None, plan_ref, used_ref, (row_refs, ins[len(parts) :]), *refs[len(arrays) :]
+            rows, plan_ref, used_ref, (row_refs, ins[len(parts) :]), *refs[len(arrays) :]
         )
 
     inner_tiles = total // TILE_SIZE
@@ -161,7 +161,7 @@
     )(plan, used, *arrays)
 
 
-def cut_kernel(place_ref, *refs):
+def cut_kernel(device_ref, place_ref, *refs):
     planes, out_ref = refs[:-1], refs[-1]
     for block in range(out_ref.shape[0]):
         first, second, gain = planes[3 * block : 3 * block + 3]
@@ -169,39 +169,42 @@
             out_ref[block, part] = (ref[...].astype(jnp.float32) * gain[...]).astype(jnp.bfloat16)
 
 
-def cut(blocks, column, gains):
+def cut(blocks, column, gains, device):
     rows = blocks[0][0][0].shape[0]
-    place = jnp.stack([column] + [first for _, first in blocks]).astype(jnp.int32)
+    place = np.stack([column] + [first for _, first in blocks], axis=1).astype(np.int32)
     specs, operands = [], []
     for index, (planes, _) in enumerate(blocks):
-        specs += [pl.BlockSpec((rows, TILE_SIZE), lambda i, place: (0, place[0]))] * 2
-        specs.append(pl.BlockSpec((None, rows, 1), lambda i, place, at=index + 1: (place[at], 0, 0)))
+        specs += [pl.BlockSpec((rows, TILE_SIZE), lambda i, me, place: (0, place[me[0], 0]))] * 2
+        specs.append(
+            pl.BlockSpec((None, rows, 1), lambda i, me, place, at=index + 1: (place[me[0], at], 0, 0))
+        )
         operands += [planes[0], planes[1], gains]
     shape = (len(blocks), 2, rows, TILE_SIZE)
     return pl.pallas_call(
         cut_kernel,
         out_shape=jax.ShapeDtypeStruct(shape, jnp.bfloat16),
         grid_spec=pltpu.PrefetchScalarGridSpec(
-            num_scalar_prefetch=1,
+            num_scalar_prefetch=2,
             grid=(1,),
             in_specs=specs,
-            out_specs=pl.BlockSpec(shape, lambda i, place: (0, 0, 0, 0)),
+            out_specs=pl.BlockSpec(shape, lambda i, me, place: (0, 0, 0, 0)),
         ),
-    )(place, *operands)
-
-
-def job(base, row_blocks, columns, absent, used, span, total, full, accumulate, choice=()):
+    )(device, jnp.asarray(place), *operands)
+
+
+def job(device, base, row_blocks, columns, absent, used, span, total, full, accumulate, choice=()):
     rows = row_blocks[0][0][0].shape[0]
     count, height = len(row_blocks), len(row_blocks) * rows
     chunks = 1 + max(column[3] for column in columns)
     depth = total if full else len(columns) * rows
     span_depth = depth // chunks
-    plan = jnp.stack(
+    plan = np.stack(
         [first for _, first in row_blocks]
         + [column[2] for column in columns]
         + list(absent)
-        + list(choice)
-    ).astype(jnp.int32)
+        + list(choice),
+        axis=1,
+    ).astype(np.int32)
     planes = [plane for block, _ in row_blocks for plane in block]
     sources, source_at = [], []
     for pieces, *_ in columns:
@@ -210,13 +213,14 @@
         source_at.append([source is pieces for source in sources].index(True))
     given = [] if base is None else [base]
 
-    def kernel(plan_ref, used_ref, *refs):
+    def kernel(device_ref, plan_ref, used_ref, *refs):
         plane_refs = refs[: len(planes)]
         source_refs = refs[len(planes) : len(planes) + len(sources)]
         out_ref, left, right, held, left_sem, right_sem, held_sem = refs[-7:]
+        me = device_ref[0]
 
         def first_of(at):
-            return pl.multiple_of(plan_ref[at], rows)
+            return pl.multiple_of(plan_ref[me, at], rows)
 
         def held_copy(block, part, out):
             here = held.at[part, pl.ds(block * rows, rows), :]
@@ -247,7 +251,7 @@
                 if full and choice:
                     for at in range(len(planes) // 2):
 
-                        @pl.when(plan_ref[plan.shape[0] - 1] == at)
+                        @pl.when(plan_ref[me, plan.shape[1] - 1] == at)
                         def _():
                             pltpu.make_async_copy(
                                 plane_refs[2 * at + part], left.at[part, here, :], left_sem
@@ -272,16 +276,16 @@
             bytes_view = right.at[pl.ds(0, 2), pl.ds(0, len(members) * rows), :]
             pltpu.make_async_copy(bytes_view, bytes_view, right_sem.at[chunk]).wait()
             if full:
-                base_row = plan_ref[count + members[0]] // span_depth * span_depth
+                base_row = plan_ref[me, count + members[0]] // span_depth * span_depth
                 inner = pl.ds(pl.multiple_of(base_row, span_depth), span_depth)
                 pieces = [(base_row + t * TILE_SIZE, TILE_SIZE) for t in range(span_depth // TILE_SIZE)]
                 spots = [pl.ds(pl.multiple_of(p, TILE_SIZE), n) for p, n in pieces]
             else:
                 inner = slice(None)
-                pieces = [(plan_ref[count + at], rows) for at in members]
+                pieces = [(plan_ref[me, count + at], rows) for at in members]
                 spots = [pl.ds(at * rows, rows) for at in members]
             for block in range(count):
-                own_tile = plan_ref[block] // TILE_SIZE
+                own_tile = plan_ref[me, block] // TILE_SIZE
                 for (first, size), spot in zip(pieces, spots):
 
                     @pl.when(used_ref[own_tile, first // TILE_SIZE] == 0)
@@ -308,7 +312,7 @@
         kernel,
         out_shape=jax.ShapeDtypeStruct((2, span, TILE_SIZE), jnp.float32),
         grid_spec=pltpu.PrefetchScalarGridSpec(
-            num_scalar_prefetch=2,
+            num_scalar_prefetch=3,
             grid=(1,),
             in_specs=[pl.BlockSpec(memory_space=pl.ANY)] * len(operands),
             out_specs=pl.BlockSpec(memory_space=pl.ANY),
@@ -321,12 +325,12 @@
                 pltpu.SemaphoreType.DMA,
             ],
         ),
-        input_output_aliases={} if base is None else {2 + len(operands) - 1: 0},
+        input_output_aliases={} if base is None else {3 + len(operands) - 1: 0},
         cost_estimate=pl.CostEstimate(
             flops=8 * height * depth * TILE_SIZE, bytes_accessed=moved, transcendentals=0
         ),
         compiler_params=pltpu.CompilerParams(vmem_limit_bytes=60 * 1024 * 1024),
-    )(plan, used, *operands)
+    )(device, jnp.asarray(plan), used, *operands)
 
 
 def used_tiles(aperture, lengths, rcv_index, total):
@@ -345,35 +349,39 @@
     rcv_index = lax.axis_index("rcv")
     devices = src_count * rcv_count
     span = rows * rcv_count
+    device = (src_index * rcv_count + rcv_index).reshape(1)
     phased = rows % 128 == 0 and rcv_count % 4 == 0 and rcv_count > 4
 
-    blocks = transposed_blocks(data, devices)
-    arrived = [
-        lax.all_to_all(b, ("src", "rcv"), split_axis=0, concat_axis=0, tiled=True) for b in blocks
-    ]
-    own = tuple(fill(data, fill_mask, a, part) for part, a in enumerate(arrived))
-    used = used_tiles(aperture, lengths, rcv_index, total)
-
     order = ring_order(rcv_count)
+    owner, mine = np.divmod(np.arange(devices), rcv_count)
+    place = np.asarray([order.index(i) for i in range(rcv_count)])[mine]
+    half = rcv_count // 2
+    steps = (rcv_count - 1) // 2
+
+    def origin(offset):
+        return np.asarray(order)[(place + offset) % rcv_count]
+
+    def here(numbers):
+        return jnp.asarray(numbers, jnp.int32)[device[0]]
+
     forward = [(order[i], order[(i + 1) % rcv_count]) for i in range(rcv_count)]
     backward = [(b, a) for a, b in forward]
-    place = jnp.asarray([order.index(i) for i in range(rcv_count)], jnp.int32)[rcv_index]
-    table = jnp.asarray(order + order, jnp.int32)
-    half = rcv_count // 2
-
-    def origin(offset):
-        return lax.dynamic_index_in_dim(table, place + offset % rcv_count, keepdims=False)
-
+
+    def hop(planes, pairs):
+        return tuple(lax.ppermute(p, "rcv", pairs) for p in planes)
+
+    used = used_tiles(aperture, lengths, rcv_index, total)
     my_gains = -lax.dynamic_slice_in_dim(obliquity, src_index * span, span)
     gains = my_gains.reshape(rcv_count, rows, 1)
 
     def tiles_of(blocks, column):
-        if rows % 128 == 0:
-            return cut(blocks, column, gains)
+        if phased:
+            return cut(blocks, column, gains, device)
         out = []
         for planes, first in blocks:
-            cuts = [lax.dynamic_slice_in_dim(p, column * TILE_SIZE, TILE_SIZE, 1) for p in planes]
-            gain = lax.dynamic_index_in_dim(gains, first, 0, keepdims=True)
+            start = here(column) * TILE_SIZE
+            cuts = [lax.dynamic_slice_in_dim(p, start, TILE_SIZE, 1) for p in planes]
+            gain = lax.dynamic_index_in_dim(gains, here(first), 0, keepdims=True)
             out.append((jnp.stack(cuts).astype(jnp.float32) * gain).astype(jnp.bfloat16))
         return jnp.stack(out)
 
@@ -388,75 +396,99 @@
             bit //= 2
         for pieces, mask in held_by:
             for index, first in enumerate(origins):
-                columns.append((pieces, index, (src_index ^ mask) * span + first * rows, mask))
+                columns.append((pieces, index, (owner ^ mask) * span + first * rows, mask))
 
     def collect(blocks):
-        spread(tiles_of(blocks, rcv_index), [first for _, first in blocks])
-
-    steps = (rcv_count - 1) // 2
-    rows_of = {0: (own, origin(0))}
+        tiles = tiles_of(blocks, mine)
+        spread(tiles, [first for _, first in blocks])
+
+    blocks = transposed_blocks(data, devices)
+    arrived = [
+        lax.all_to_all(b, ("src", "rcv"), split_axis=0, concat_axis=0, tiled=True) for b in blocks
+    ]
+    own, ahead, behind = [], [], []
+    for part in range(2):
+        own.append(fill(data, fill_mask, arrived[part], part))
+        ahead.append(lax.ppermute(own[part], "rcv", forward))
+        behind.append(lax.ppermute(own[part], "rcv", backward))
+
+    rows_of = {0: (own, origin(0)), -1: (ahead, origin(-1)), 1: (behind, origin(1))}
     far = origin(half)
-    if phased:
-        across = [(order[i], order[(i + half) % rcv_count]) for i in range(rcv_count)]
-        spread(lax.ppermute(tiles_of([(own, origin(0))], far), "rcv", across), [far])
-    collect([rows_of[0]])
-    ahead, behind = own, own
-    trail = {}
-    for step in range(1, steps + 1):
-        ahead = tuple(lax.ppermute(p, "rcv", forward) for p in ahead)
-        behind = tuple(lax.ppermute(p, "rcv", backward) for p in behind)
-        rows_of[-step], rows_of[step] = (ahead, origin(-step)), (behind, origin(step))
-        trail[step] = len(columns)
-        collect([rows_of[-step], rows_of[step]])
     if not phased:
+        collect([rows_of[0]])
+        collect([rows_of[-1], rows_of[1]])
+        for step in range(2, steps + 1):
+            ahead, behind = hop(ahead, forward), hop(behind, backward)
+            rows_of[-step], rows_of[step] = (ahead, origin(-step)), (behind, origin(step))
+            collect([rows_of[-step], rows_of[step]])
         if rcv_count % 2 == 0:
-            last = (lax.ppermute(ahead[0], "rcv", forward), lax.ppermute(behind[1], "rcv", backward))
+            last = hop(ahead[:1], forward) + hop(behind[1:], backward)
             rows_of[half] = (last, far)
             collect([rows_of[half]])
         row_buffers, row_starts, pieces, starts = [], [], [], []
         for planes, first in rows_of.values():
             row_buffers += [(planes[0], 0), (planes[1], 1)]
-            row_starts += [first * rows] * 2
+            row_starts += [here(first * rows)] * 2
         for array, index, first, _ in columns:
             if index == 0:
                 pieces.append(array)
-            starts.append(first)
+            starts.append(here(first))
         return product(row_buffers, row_starts, pieces, starts, used, span, total)
 
     quarter = rcv_count // 4
     near = [quarter - 1, quarter, rcv_count - 1 - quarter, rcv_count - quarter]
-    last = [
-        lax.ppermute(p, "rcv", [(order[(i + d) % rcv_count], order[i]) for i in range(rcv_count) if i not in near])
-        for p, d in ((ahead[0], -1), (behind[1], 1))
-    ]
-    taken = []
-    for offset in (-1, 1):
+
+    def from_mate(offset):
         pairs = []
         for i in near:
             mate = rcv_count - 1 - i
             if (mate + offset) % rcv_count == (i + half) % rcv_count:
                 pairs.append((order[mate], order[i]))
-        taken.append([lax.ppermute(p, "rcv", pairs) for p in rows_of[offset][0]])
-    is_near = jnp.any(place == jnp.asarray(near, jnp.int32))
-    side = jnp.any(jnp.asarray([(rcv_count - 2 - i - i - half) % rcv_count == 0 for i in range(rcv_count)])[None, place])
-    chosen = jnp.where(is_near, jnp.where(side, 1, 2), 0)
+        return pairs
+
+    across = [(order[i], order[(i + half) % rcv_count]) for i in range(rcv_count)]
+    far_pieces = cut([(own, origin(0))], far, gains, device)
+    far_pieces = lax.ppermute(far_pieces, "rcv", across)
+    spread(far_pieces, [far])
+    collect([rows_of[0]])
+    inside = [0] + [o for step in range(1, steps) for o in (-step, step)]
+    outside = [-steps, steps]
 
     def as_rows(offsets):
         return [(rows_of[o][0], rows_of[o][1] * rows) for o in offsets]
 
-    inside = [0] + [o for step in range(1, steps) for o in (-step, step)]
-    outside = [-steps, steps]
-    early, late = columns[: trail[steps]], columns[trail[steps] :]
+    for step in range(2, steps + 1):
+        collect([rows_of[1 - step], rows_of[step - 1]])
+        moved = []
+        for part in range(2):
+            moved.append(lax.ppermute(ahead[part], "rcv", forward))
+            moved.append(lax.ppermute(behind[part], "rcv", backward))
+        ahead, behind = moved[0::2], moved[1::2]
+        rows_of[-step], rows_of[step] = (ahead, origin(-step)), (behind, origin(step))
+    taken = [hop(rows_of[offset][0], from_mate(offset)) for offset in (-1, 1)]
+    late_from = len(columns)
+    collect([rows_of[-steps], rows_of[steps]])
+    early, late = columns[:late_from], columns[late_from:]
     out = job(
-        None, as_rows(inside), early, [c[2] for c in late], used, span, total, True, False
+        device, None, as_rows(inside), early, [c[2] for c in late], used, span, total, True, False
     )
+    turns = [
+        [(order[(i + d) % rcv_count], order[i]) for i in range(rcv_count) if i not in near]
+        for d in (-1, 1)
+    ]
+    last = []
+    for part, plane in enumerate((ahead[0], behind[1])):
+        last.append(lax.ppermute(plane, "rcv", turns[part]))
     packed = [(array, index, first, 0) for array, index, first, _ in late]
-    out = job(out, as_rows(inside), packed, [], used, span, total, False, True)
-    out = job(out, as_rows(outside), columns, [], used, span, total, True, False)
-    candidates = (*last, *taken[0], *taken[1])
-    return job(
-        out, [(candidates, far * rows)], columns, [], used, span, total, True, False, [chosen]
-    )
+    out = job(device, out, as_rows(inside), packed, [], used, span, total, False, True)
+    out = job(device, out, as_rows(outside), columns, [], used, span, total, True, False)
+    chosen = np.zeros(devices)
+    for number, offset in enumerate((-1, 1), start=1):
+        for _, target in from_mate(offset):
+            chosen[mine == target] = number
+    candidates = [(*last, *taken[0], *taken[1])]
+    rows_far = [(candidates[0], far * rows)]
+    return job(device, out, rows_far, columns, [], used, span, total, True, False, [chosen])
 
 
 def solution(mesh):
@@ -467,6 +499,7 @@
         P("src", None, None),
         P("src", "rcv"),
     )
+
     return jax.shard_map(
         local, mesh=mesh, in_specs=placed, out_specs=P(None, "src", "rcv"), check_vma=False
     )

time: 323 us -> 323 us (level)
  waiting for transfers between devices: 128 us -> 148 us
  between operations: 18.2 us -> 0.41 us
  other arithmetic: 11.1 us -> 1.43 us
  starting transfers between devices: 51.2 us -> 57.5 us
  local copies, waits for them, and re-layouts: 6.54 us -> 2.07 us
    ppermute x19, waiting for transfers between devices: 84.5 us -> 95.4 us  [the longest x4 34.1 us: local(): moved.append(lax.ppermute(ahead[part], 'rcv', forward))]
    ppermute x15, waiting for transfers between devices: 23.7 us -> 33.6 us  [spread(): lax.ppermute(x, 'src', swap)]
    another operation x5 -> x0, other arithmetic: 8.39 us -> none  [cut(): jnp.stack([column] + [first for _, first in blocks]).astype(jnp.int32)]
    ppermute x19, starting transfers between devices: 34.7 us -> 39.6 us  [the longest x4 11.2 us: hop(): return tuple((lax.ppermute(p, 'rcv', pairs) for p in planes))]
  transfers between devices with their start and end apart: 35 -> 35, of which waited for: 15 -> 16; matrix products, arithmetic and copies ran while one was open for 5% -> 1% of each run, Pallas kernels for 20% -> 20%
where the time goes in v1:
time: 323 us; the launch traced here: 317 us
  waiting for transfers between devices  148 us (46%)
  Pallas kernels  77.1 us (24%)
  starting transfers between devices  57.5 us (18%)
  blocking collectives  29.9 us (9%)
    pallas_call x4, Pallas kernels, job(): pl.pallas_call(kernel, out_shape=jax.ShapeDtypeStruct((2, span, TILE_SIZE...  50.3 us
    ppermute x4, waiting for transfers between devices, local(): moved.append(lax.ppermute(ahead[part], 'rcv', forward))  34.1 us
    ppermute x15, waiting for transfers between devices, spread(): lax.ppermute(x, 'src', swap)  33.6 us
    all_to_all x1, blocking collectives, local(): lax.all_to_all(b, ('src', 'rcv'), split_axis=0, concat_axis=0, tiled=True)  29.9 us
    ppermute x2, waiting for transfers between devices, local(): ahead.append(lax.ppermute(own[part], 'rcv', forward))  24.7 us
    ppermute x4, waiting for transfers between devices, local(): moved.append(lax.ppermute(behind[part], 'rcv', backward))  23 us
    all_to_all x1, waiting for transfers between devices, local(): lax.all_to_all(b, ('src', 'rcv'), split_axis=0, concat_axis=0, tiled=True)  19.4 us
    pallas_call x5, Pallas kernels, cut(): pl.pallas_call(cut_kernel, out_shape=jax.ShapeDtypeStruct(shape, jnp.bflo...  14.6 us
  transfers between devices with their start and end apart: 35, of which 16 were waited for; matrix products, arithmetic and copies ran while one was open for 1% of the time, Pallas kernels for 20%

profile of v1, /device:TPU:18, one launch (start us, length us, event | category | flops | bytes accessed | tf_op | source)
XLA Modules:
  0.0 316.9 jit_solution(7674529256660162024)
XLA Ops:
  0.0 4.0 %shard_map.139 = (bf16[32,128,128]{2,1,0:T(8,128)(2,1)}, bf16[32,128,128]{2,1,0:T(8,128)(2,1)}) custom-call(bf16[2,128,4096]{2,1,0:T(8,128)(2,1)} %data_ref.5), custom_call_target="tpu_custom_call" | custom-call | tf_op jit(solution)/shard_map/pallas_call | solution.py:29
  4.0 29.9 %all_to_all.10.arrived_ref = bf16[32,128,128]{2,1,0:T(8,128)(2,1)} all-to-all(bf16[32,128,128]{2,1,0:T(8,128)(2,1)} %get-tuple-element.7), channel_id=1, replica_groups=mesh['src'=4,'rcv'=8] {'src','rcv'}, dimensions={0} | all-to-all | bytes 2097152 | tf_op jit(solution)/shard_map/all_to_all | solution.py:407
  33.9 6.2 %all-to-all-start.1 = ((bf16[32,128,128]{2,1,0:T(8,128)(2,1)}), bf16[32,128,128]{2,1,0:T(8,128)(2,1)S(1)}, u32[]{:S(2)}, u32[]{:S(2)}) async-start(bf16[32,128,128]{2,1,0:T(8,128)(2,1)} %get-tuple-element.8), calls=%async_computation.1 | async-start | bytes 2097152 | tf_op jit(solution)/shard_map/all_to_all | solution.py:407
  40.1 4.1 %shard_map.140.refs_0_ = bf16[128,4096]{1,0:T(8,128)(2,1)} custom-call(bf16[2,128,4096]{2,1,0:T(8,128)(2,1)} %data_ref.5, s32[128,4096]{1,0:T(8,128)} %mask_ref.3, bf16[32,128,128]{2,1,0:T(8,128)(2,1)} %all_to_all.10.arrived_ref), custom_call_target="tpu_custom_call" | custom-call | tf_op jit(solution)/shard_map/pallas_call | solution.py:54
  44.7 19.4 %all-to-all-done.1.arrived_ref = bf16[32,128,128]{2,1,0:T(8,128)(2,1)S(1)} async-done(((bf16[32,128,128]{2,1,0:T(8,128)(2,1)}), bf16[32,128,128]{2,1,0:T(8,128)(2,1)S(1)}, u32[]{:S(2)}, u32[]{:S(2)}) %all-to-all-start.1) | async-done | bytes 1048608 | tf_op jit(solution)/shard_map/all_to_all | solution.py:407
  65.1 4.1 %shard_map.141.refs_1_ = bf16[128,4096]{1,0:T(8,128)(2,1)} custom-call(bf16[2,128,4096]{2,1,0:T(8,128)(2,1)} %data_ref.5, s32[128,4096]{1,0:T(8,128)} %mask_ref.3, bf16[32,128,128]{2,1,0:T(8,128)(2,1)} %copy-done.7), custom_call_target="tpu_custom_call" | custom-call | tf_op jit(solution)/shard_map/pallas_call | solution.py:54
  73.1 13.2 %collective-permute-done.refs_0_.refs_2_ = bf16[128,4096]{1,0:T(8,128)(2,1)S(1)} collective-permute-done((bf16[128,4096]{1,0:T(8,128)(2,1)}, bf16[128,4096]{1,0:T(8,128)(2,1)S(1)}, u32[]{:S(2)}, u32[]{:S(2)}) %collective-permute-start) | collective-permute-done | bytes 1048608 | tf_op jit(solution)/shard_map/ppermute | solution.py:412
  88.7 6.8 %collective-permute-done.4.refs_4_.refs_5_ = bf16[128,4096]{1,0:T(8,128)(2,1)S(1)} collective-permute-done((bf16[128,4096]{1,0:T(8,128)(2,1)}, bf16[128,4096]{1,0:T(8,128)(2,1)S(1)}, u32[]{:S(2)}, u32[]{:S(2)}) %collective-permute-start.4) | collective-permute-done | bytes 1048608 | tf_op jit(solution)/shard_map/ppermute | solution.py:413
  97.3 11.5 %collective-permute-done.9.refs_1_.refs_3_ = bf16[128,4096]{1,0:T(8,128)(2,1)} collective-permute-done((bf16[128,4096]{1,0:T(8,128)(2,1)}, bf16[128,4096]{1,0:T(8,128)(2,1)}, u32[]{:S(2)}, u32[]{:S(2)}) %collective-permute-start.9) | collective-permute-done | bytes 1048608 | tf_op jit(solution)/shard_map/ppermute | solution.py:412
  111.3 6.8 %collective-permute-done.11.refs_3_.refs_4_ = bf16[128,4096]{1,0:T(8,128)(2,1)} collective-permute-done((bf16[128,4096]{1,0:T(8,128)(2,1)S(1)}, bf16[128,4096]{1,0:T(8,128)(2,1)}, u32[]{:S(2)}, u32[]{:S(2)}) %collective-permute-start.11) | collective-permute-done | bytes 1048608 | tf_op jit(solution)/shard_map/ppermute | solution.py:413
  121.6 2.7 shard_map.142
  126.7 4.4 %collective-permute-done.1.refs_0_.refs_6_ = bf16[128,4096]{1,0:T(8,128)(2,1)} collective-permute-done((bf16[128,4096]{1,0:T(8,128)(2,1)S(1)}, bf16[128,4096]{1,0:T(8,128)(2,1)}, u32[]{:S(2)}, u32[]{:S(2)}) %collective-permute-start.1) | collective-permute-done | bytes 1048608 | tf_op jit(solution)/shard_map/ppermute | solution.py:464
  131.2 2.6 collective-permute-start.2
  133.7 6.8 %collective-permute-done.5.refs_4_.refs_9_ = bf16[128,4096]{1,0:T(8,128)(2,1)} collective-permute-done((bf16[128,4096]{1,0:T(8,128)(2,1)S(1)}, bf16[128,4096]{1,0:T(8,128)(2,1)}, u32[]{:S(2)}, u32[]{:S(2)}) %collective-permute-start.5) | collective-permute-done | bytes 1048608 | tf_op jit(solution)/shard_map/ppermute | solution.py:465
  142.3 17.0 %collective-permute-done.24.refs_1_.refs_7_ = bf16[128,4096]{1,0:T(8,128)(2,1)} collective-permute-done((bf16[128,4096]{1,0:T(8,128)(2,1)}, bf16[128,4096]{1,0:T(8,128)(2,1)}, u32[]{:S(2)}, u32[]{:S(2)}) %collective-permute-start.24) | collective-permute-done | bytes 1048608 | tf_op jit(solution)/shard_map/ppermute | solution.py:464
  165.2 2.7 shard_map.143.refs_14_.refs_8_.refs_10_
  167.9 5.0 %collective-permute-start.18 = (bf16[1,2,128,512]{3,2,1,0:T(8,128)(2,1)}, bf16[1,2,128,512]{3,2,1,0:T(8,128)(2,1)}, u32[]{:S(2)}, u32[]{:S(2)}) collective-permute-start(bf16[1,2,128,512]{3,2,1,0:T(8,128)(2,1)} %shard_map.143.refs_14_.refs_8_.refs_10_), channel_id=1, source_target_pairs={{0,16},{8,24},{16,0},{24,8},{1,17},{9,25},{17,1},{25,9},{2,18},{10... | collective-permute-start | bytes 786440 | tf_op jit(solution)/shard_map/ppermute | solution.py:395
  172.8 6.5 %collective-permute-done.18.refs_15_.refs_9_.refs_11_ = bf16[1,2,128,512]{3,2,1,0:T(8,128)(2,1)} collective-permute-done((bf16[1,2,128,512]{3,2,1,0:T(8,128)(2,1)}, bf16[1,2,128,512]{3,2,1,0:T(8,128)(2,1)}, u32[]{:S(2)}, u32[]{:S(2)}) %collective-permute-start.18) | collective-permute-done | bytes 262176 | tf_op jit(solution)/shard_map/ppermute | solution.py:395
  181.0 3.0 shard_map.144.refs_18_.refs_12_.refs_14_
  184.0 4.8 %collective-permute-done.15.refs_11_.refs_5_.refs_7_ = bf16[1,2,128,512]{3,2,1,0:T(8,128)(2,1)} collective-permute-done((bf16[1,2,128,512]{3,2,1,0:T(8,128)(2,1)}, bf16[1,2,128,512]{3,2,1,0:T(8,128)(2,1)}, u32[]{:S(2)}, u32[]{:S(2)}) %collective-permute-start.15) | collective-permute-done | bytes 262176 | tf_op jit(solution)/shard_map/ppermute | solution.py:395
  190.5 6.2 %collective-permute-done.6.refs_4_.refs_3_ = bf16[128,4096]{1,0:T(8,128)(2,1)} collective-permute-done((bf16[128,4096]{1,0:T(8,128)(2,1)}, bf16[128,4096]{1,0:T(8,128)(2,1)}, u32[]{:S(2)}, u32[]{:S(2)}) %collective-permute-start.6) | collective-permute-done | bytes 1048608 | tf_op jit(solution)/shard_map/ppermute | solution.py:465
  196.7 12.7 %collective-permute-done.29.refs_1_ = bf16[128,4096]{1,0:T(8,128)(2,1)} collective-permute-done((bf16[128,4096]{1,0:T(8,128)(2,1)}, bf16[128,4096]{1,0:T(8,128)(2,1)}, u32[]{:S(2)}, u32[]{:S(2)}) %collective-permute-start.29) | collective-permute-done | bytes 1048608 | tf_op jit(solution)/shard_map/ppermute | solution.py:464
  209.3 9.0 %collective-permute-done.30.refs_3_.refs_2_ = bf16[128,4096]{1,0:T(8,128)(2,1)} collective-permute-done((bf16[128,4096]{1,0:T(8,128)(2,1)S(1)}, bf16[128,4096]{1,0:T(8,128)(2,1)}, u32[]{:S(2)}, u32[]{:S(2)}) %collective-permute-start.30) | collective-permute-done | bytes 1048608 | tf_op jit(solution)/shard_map/ppermute | solution.py:465
  218.3 3.0 shard_map.145.refs_22_.refs_16_.refs_18_
  221.3 3.2 shard_map.146.refs_10_.refs_20_.refs_22_
  228.7 12.6 %collective-permute-done.26.refs_23_.refs_17_.refs_19_ = bf16[2,2,128,512]{3,2,1,0:T(8,128)(2,1)} collective-permute-done((bf16[2,2,128,512]{3,2,1,0:T(8,128)(2,1)S(1)}, bf16[2,2,128,512]{3,2,1,0:T(8,128)(2,1)}, u32[]{:S(2)}, u32[]{:S(2)}) %collective-permute-start.26) | collective-permute-done | bytes 524320 | tf_op jit(solution)/shard_map/ppermute | solution.py:395
  241.8 9.7 %collective-permute-done.31.refs_11_.refs_21_.refs_23_ = bf16[2,2,128,512]{3,2,1,0:T(8,128)(2,1)S(1)} collective-permute-done((bf16[2,2,128,512]{3,2,1,0:T(8,128)(2,1)}, bf16[2,2,128,512]{3,2,1,0:T(8,128)(2,1)S(1)}, u32[]{:S(2)}, u32[]{:S(2)}) %collective-permute-start.31) | collective-permute-done | bytes 524320 | tf_op jit(solution)/shard_map/ppermute | solution.py:395
  252.4 6.3 %collective-permute-start.12 = (bf16[128,4096]{1,0:T(8,128)(2,1)}, bf16[128,4096]{1,0:T(8,128)(2,1)}, u32[]{:S(2)}, u32[]{:S(2)}) collective-permute-start(bf16[128,4096]{1,0:T(8,128)(2,1)} %collective-permute-done.11.refs_3_.refs_4_), channel_id=1, source_target_pairs={{5,4},{2,3},{13,12},{10,11},{21,20},{18,19},{29,28},{26,27}} | collective-permute-start | bytes 3145736 | tf_op jit(solution)/shard_map/ppermute | solution.py:371
  266.3 20.9 %shard_map.147.refs_14_ = f32[2,1024,512]{2,1,0:T(8,128)} custom-call(s32[1]{0:T(128)} %bitcast.device_ref, s32[32,37]{1,0:T(8,128)} %constant.45.clone.plan_ref, s32[2,8]{1,0:T(2,128)} %convert_element_type.3.used_ref, bf16[128,4096]{1,0:T(8,128)(2,1)} %shard_map.140.refs_0_, bf16[128,4096]{1,0:T(8,128)(2,1)} %shard_map.141.refs_1_, ...), custom_call_target="tpu_custom_call" | custom-call | flops 10737418240 | bytes 21495808 | tf_op jit(solution)/shard_map/pallas_call | solution.py:311
  287.3 9.1 %shard_map.148.refs_24_ = f32[2,1024,512]{2,1,0:T(8,128)} custom-call(s32[1]{0:T(128)} %bitcast.device_ref, s32[32,13]{1,0:T(8,128)} %constant.46.clone.plan_ref, s32[2,8]{1,0:T(2,128)} %convert_element_type.3.used_ref, bf16[128,4096]{1,0:T(8,128)(2,1)} %shard_map.140.refs_0_, ...), custom_call_target="tpu_custom_call", output_to_operand_aliasing={{}: (17, {})} | custom-call | flops 2684354560 | bytes 7340032 | tf_op jit(solution)/shard_map/pallas_call | solution.py:311
  296.4 11.6 %shard_map.149.refs_26_ = f32[2,1024,512]{2,1,0:T(8,128)} custom-call(s32[1]{0:T(128)} %bitcast.device_ref, s32[32,34]{1,0:T(8,128)} %constant.47.clone.plan_ref, s32[2,8]{1,0:T(2,128)} %convert_element_type.3.used_ref, bf16[128,4096]{1,0:T(8,128)(2,1)} %collective-permute-done.2.refs_0_, ...), custom_call_target="tpu_custom_call", output_to_operand_aliasing={{}: (27, {})} | custom-call | flops 4294967296 | bytes 13631488 | tf_op jit(solution)/shard_map/pallas_call | solution.py:311
  308.1 8.7 %shard_map.150 = f32[2,1024,512]{2,1,0:T(8,128)} custom-call(s32[1]{0:T(128)} %bitcast.device_ref, s32[32,34]{1,0:T(8,128)} %constant.48.clone.plan_ref, s32[2,8]{1,0:T(2,128)} %convert_element_type.3.used_ref, bf16[128,4096]{1,0:T(8,128)(2,1)} %collective-permute-done.3.refs_0_, ...), custom_call_target="tpu_custom_call", output_to_operand_aliasing={{}: (29, {})} | custom-call | flops 2147483648 | bytes 11010048 | tf_op jit(solution)/shard_map/pallas_call | solution.py:311
  (91 shorter events, 42.1 us)
Async XLA Ops:
  33.9 30.3 %all-to-all-start.1 = ((bf16[32,128,128]{2,1,0:T(8,128)(2,1)}), bf16[32,128,128]{2,1,0:T(8,128)(2,1)S(1)}, u32[]{:S(2)}, u32[]{:S(2)}) async-start(bf16[32,128,128]{2,1,0:T(8,128)(2,1)} %get-tuple-element.8), calls=%async_computation.1 | async-start | bytes 2097152 | tf_op jit(solution)/shard_map/all_to_all | solution.py:407
  44.2 42.1 %collective-permute-start = (bf16[128,4096]{1,0:T(8,128)(2,1)}, bf16[128,4096]{1,0:T(8,128)(2,1)S(1)}, u32[]{:S(2)}, u32[]{:S(2)}) collective-permute-start(bf16[128,4096]{1,0:T(8,128)(2,1)} %shard_map.140.refs_0_), channel_id=1, source_target_pairs={{0,2},{2,4},{4,6},{6,7},{7,5},{5,3},{3,1},{1,0},{8,10},{10,12},{12... | collective-permute-start | bytes 3145736 | tf_op jit(solution)/shard_map/ppermute | solution.py:412
  69.2 26.2 %collective-permute-start.4 = (bf16[128,4096]{1,0:T(8,128)(2,1)}, bf16[128,4096]{1,0:T(8,128)(2,1)S(1)}, u32[]{:S(2)}, u32[]{:S(2)}) collective-permute-start(bf16[128,4096]{1,0:T(8,128)(2,1)} %shard_map.141.refs_1_), channel_id=1, source_target_pairs={{2,0},{4,2},{6,4},{7,6},{5,7},{3,5},{1,3},{0,1},{10,8},{12,10},{14... | collective-permute-start | bytes 3145736 | tf_op jit(solution)/shard_map/ppermute | solution.py:413
  71.1 37.7 %collective-permute-start.9 = (bf16[128,4096]{1,0:T(8,128)(2,1)}, bf16[128,4096]{1,0:T(8,128)(2,1)}, u32[]{:S(2)}, u32[]{:S(2)}) collective-permute-start(bf16[128,4096]{1,0:T(8,128)(2,1)} %shard_map.141.refs_1_), channel_id=1, source_target_pairs={{0,2},{2,4},{4,6},{6,7},{7,5},{5,3},{3,1},{1,0},{8,10},{10,12},{12... | collective-permute-start | bytes 3145736 | tf_op jit(solution)/shard_map/ppermute | solution.py:412
  71.2 46.8 %collective-permute-start.11 = (bf16[128,4096]{1,0:T(8,128)(2,1)S(1)}, bf16[128,4096]{1,0:T(8,128)(2,1)}, u32[]{:S(2)}, u32[]{:S(2)}) collective-permute-start(bf16[128,4096]{1,0:T(8,128)(2,1)S(1)} %copy-done.1), channel_id=1, source_target_pairs={{2,0},{4,2},{6,4},{7,6},{5,7},{3,5},{1,3},{0,1},{10,8},{12,10},{14... | collective-permute-start | bytes 3145736 | tf_op jit(solution)/shard_map/ppermute | solution.py:413
  86.3 44.8 %collective-permute-start.1 = (bf16[128,4096]{1,0:T(8,128)(2,1)S(1)}, bf16[128,4096]{1,0:T(8,128)(2,1)}, u32[]{:S(2)}, u32[]{:S(2)}) collective-permute-start(bf16[128,4096]{1,0:T(8,128)(2,1)S(1)} %collective-permute-done.refs_0_.refs_2_), channel_id=1, source_target_pairs={{0,2},{2,4},{4,6},{6,7},{7,5},{5,3},{3,1},{1,0},{8,10},{10,12},{12... | collective-permute-start | bytes 3145736 | tf_op jit(solution)/shard_map/ppermute | solution.py:464
  95.5 45.0 %collective-permute-start.5 = (bf16[128,4096]{1,0:T(8,128)(2,1)S(1)}, bf16[128,4096]{1,0:T(8,128)(2,1)}, u32[]{:S(2)}, u32[]{:S(2)}) collective-permute-start(bf16[128,4096]{1,0:T(8,128)(2,1)S(1)} %collective-permute-done.4.refs_4_.refs_5_), channel_id=1, source_target_pairs={{2,0},{4,2},{6,4},{7,6},{5,7},{3,5},{1,3},{0,1},{10,8},{12,10},{14... | collective-permute-start | bytes 3145736 | tf_op jit(solution)/shard_map/ppermute | solution.py:465
  108.8 50.6 %collective-permute-start.24 = (bf16[128,4096]{1,0:T(8,128)(2,1)}, bf16[128,4096]{1,0:T(8,128)(2,1)}, u32[]{:S(2)}, u32[]{:S(2)}) collective-permute-start(bf16[128,4096]{1,0:T(8,128)(2,1)} %collective-permute-done.9.refs_1_.refs_3_), channel_id=1, source_target_pairs={{0,2},{2,4},{4,6},{6,7},{7,5},{5,3},{3,1},{1,0},{8,10},{10,12},{12... | collective-permute-start | bytes 3145736 | tf_op jit(solution)/shard_map/ppermute | solution.py:464
  118.0 44.9 %collective-permute-start.25 = (bf16[128,4096]{1,0:T(8,128)(2,1)}, bf16[128,4096]{1,0:T(8,128)(2,1)S(1)}, u32[]{:S(2)}, u32[]{:S(2)}) collective-permute-start(bf16[128,4096]{1,0:T(8,128)(2,1)} %collective-permute-done.11.refs_3_.refs_4_), channel_id=1, source_target_pairs={{2,0},{4,2},{6,4},{7,6},{5,7},{3,5},{1,3},{0,1},{10,8},{12,10},{14... | collective-permute-start | bytes 3145736 | tf_op jit(solution)/shard_map/ppermute | solution.py:465
  124.3 43.6 %collective-permute-start.14 = (bf16[1,2,128,512]{3,2,1,0:T(8,128)(2,1)}, bf16[1,2,128,512]{3,2,1,0:T(8,128)(2,1)}, u32[]{:S(2)}, u32[]{:S(2)}) collective-permute-start(bf16[1,2,128,512]{3,2,1,0:T(8,128)(2,1)} %shard_map.142), channel_id=1, source_target_pairs={{0,7},{2,5},{4,3},{6,1},{7,0},{5,2},{3,4},{1,6},{8,15},{10,13},{12... | collective-permute-start | bytes 786440 | tf_op jit(solution)/shard_map/ppermute | solution.py:451
  131.2 59.3 %collective-permute-start.2 = (bf16[128,4096]{1,0:T(8,128)(2,1)}, bf16[128,4096]{1,0:T(8,128)(2,1)}, u32[]{:S(2)}, u32[]{:S(2)}) collective-permute-start(bf16[128,4096]{1,0:T(8,128)(2,1)} %collective-permute-done.1.refs_0_.refs_6_), channel_id=1, source_target_pairs={{0,2},{2,4},{4,6},{6,7},{7,5},{5,3},{3,1},{1,0},{8,10},{10,12},{12... | collective-permute-start | bytes 3145736 | tf_op jit(solution)/shard_map/ppermute | solution.py:464
  140.5 56.2 %collective-permute-start.6 = (bf16[128,4096]{1,0:T(8,128)(2,1)}, bf16[128,4096]{1,0:T(8,128)(2,1)}, u32[]{:S(2)}, u32[]{:S(2)}) collective-permute-start(bf16[128,4096]{1,0:T(8,128)(2,1)} %collective-permute-done.5.refs_4_.refs_9_), channel_id=1, source_target_pairs={{2,0},{4,2},{6,4},{7,6},{5,7},{3,5},{1,3},{0,1},{10,8},{12,10},{14... | collective-permute-start | bytes 3145736 | tf_op jit(solution)/shard_map/ppermute | solution.py:465
  159.3 50.0 %collective-permute-start.29 = (bf16[128,4096]{1,0:T(8,128)(2,1)}, bf16[128,4096]{1,0:T(8,128)(2,1)}, u32[]{:S(2)}, u32[]{:S(2)}) collective-permute-start(bf16[128,4096]{1,0:T(8,128)(2,1)} %collective-permute-done.24.refs_1_.refs_7_), channel_id=1, source_target_pairs={{0,2},{2,4},{4,6},{6,7},{7,5},{5,3},{3,1},{1,0},{8,10},{10,12},{12... | collective-permute-start | bytes 3145736 | tf_op jit(solution)/shard_map/ppermute | solution.py:464
  162.9 55.4 %collective-permute-start.30 = (bf16[128,4096]{1,0:T(8,128)(2,1)S(1)}, bf16[128,4096]{1,0:T(8,128)(2,1)}, u32[]{:S(2)}, u32[]{:S(2)}) collective-permute-start(bf16[128,4096]{1,0:T(8,128)(2,1)S(1)} %collective-permute-done.25.refs_3_.refs_8_), channel_id=1, source_target_pairs={{2,0},{4,2},{6,4},{7,6},{5,7},{3,5},{1,3},{0,1},{10,8},{12,10},{14... | collective-permute-start | bytes 3145736 | tf_op jit(solution)/shard_map/ppermute | solution.py:465
  167.9 11.4 %collective-permute-start.18 = (bf16[1,2,128,512]{3,2,1,0:T(8,128)(2,1)}, bf16[1,2,128,512]{3,2,1,0:T(8,128)(2,1)}, u32[]{:S(2)}, u32[]{:S(2)}) collective-permute-start(bf16[1,2,128,512]{3,2,1,0:T(8,128)(2,1)} %shard_map.143.refs_14_.refs_8_.refs_10_), channel_id=1, source_target_pairs={{0,16},{8,24},{16,0},{24,8},{1,17},{9,25},{17,1},{25,9},{2,18},{10... | collective-permute-start | bytes 786440 | tf_op jit(solution)/shard_map/ppermute | solution.py:395
  188.8 38.7 %collective-permute-start.21 = (bf16[2,2,128,512]{3,2,1,0:T(8,128)(2,1)}, bf16[2,2,128,512]{3,2,1,0:T(8,128)(2,1)S(1)}, u32[]{:S(2)}, u32[]{:S(2)}) collective-permute-start(bf16[2,2,128,512]{3,2,1,0:T(8,128)(2,1)} %shard_map.144.refs_18_.refs_12_.refs_14_), channel_id=1, source_target_pairs={{0,16},{8,24},{16,0},{24,8},{1,17},{9,25},{17,1},{25,9},{2,18},{10... | collective-permute-start | bytes 1572872 | tf_op jit(solution)/shard_map/ppermute | solution.py:395
  190.5 34.0 %collective-permute-start.19 = (bf16[1,2,128,512]{3,2,1,0:T(8,128)(2,1)S(1)}, bf16[1,2,128,512]{3,2,1,0:T(8,128)(2,1)}, u32[]{:S(2)}, u32[]{:S(2)}) collective-permute-start(bf16[1,2,128,512]{3,2,1,0:T(8,128)(2,1)S(1)} %copy-done.12), channel_id=1, source_target_pairs={{0,8},{8,0},{16,24},{24,16},{1,9},{9,1},{17,25},{25,17},{2,10},{10... | collective-permute-start | bytes 786440 | tf_op jit(solution)/shard_map/ppermute | solution.py:395
  196.7 29.1 %collective-permute-start.20 = (bf16[1,2,128,512]{3,2,1,0:T(8,128)(2,1)}, bf16[1,2,128,512]{3,2,1,0:T(8,128)(2,1)}, u32[]{:S(2)}, u32[]{:S(2)}) collective-permute-start(bf16[1,2,128,512]{3,2,1,0:T(8,128)(2,1)} %collective-permute-done.18.refs_15_.refs_9_.refs_11_), channel_id=1, source_target_pairs={{0,8},{8,0},{16,24},{24,16},{1,9},{9,1},{17,25},{25,17},{2,10},{10... | collective-permute-start | bytes 786440 | tf_op jit(solution)/shard_map/ppermute | solution.py:395
  209.3 17.0 %collective-permute-start.16 = (bf16[1,2,128,512]{3,2,1,0:T(8,128)(2,1)}, bf16[1,2,128,512]{3,2,1,0:T(8,128)(2,1)}, u32[]{:S(2)}, u32[]{:S(2)}) collective-permute-start(bf16[1,2,128,512]{3,2,1,0:T(8,128)(2,1)} %collective-permute-done.14.refs_10_.refs_4_.refs_6_), channel_id=1, source_target_pairs={{0,8},{8,0},{16,24},{24,16},{1,9},{9,1},{17,25},{25,17},{2,10},{10... | collective-permute-start | bytes 786440 | tf_op jit(solution)/shard_map/ppermute | solution.py:395
  224.5 27.9 %collective-permute-start.10 = (bf16[128,4096]{1,0:T(8,128)(2,1)}, bf16[128,4096]{1,0:T(8,128)(2,1)}, u32[]{:S(2)}, u32[]{:S(2)}) collective-permute-start(bf16[128,4096]{1,0:T(8,128)(2,1)} %collective-permute-done.9.refs_1_.refs_3_), channel_id=1, source_target_pairs={{3,2},{4,5},{11,10},{12,13},{19,18},{20,21},{27,26},{28,29}} | collective-permute-start | bytes 3145736 | tf_op jit(solution)/shard_map/ppermute | solution.py:371
  226.4 14.9 %collective-permute-start.26 = (bf16[2,2,128,512]{3,2,1,0:T(8,128)(2,1)S(1)}, bf16[2,2,128,512]{3,2,1,0:T(8,128)(2,1)}, u32[]{:S(2)}, u32[]{:S(2)}) collective-permute-start(bf16[2,2,128,512]{3,2,1,0:T(8,128)(2,1)S(1)} %copy-done.3), channel_id=1, source_target_pairs={{0,16},{8,24},{16,0},{24,8},{1,17},{9,25},{17,1},{25,9},{2,18},{10... | collective-permute-start | bytes 1572872 | tf_op jit(solution)/shard_map/ppermute | solution.py:395
  227.5 13.8 %collective-permute-start.23 = (bf16[2,2,128,512]{3,2,1,0:T(8,128)(2,1)S(1)}, bf16[2,2,128,512]{3,2,1,0:T(8,128)(2,1)S(1)}, u32[]{:S(2)}, u32[]{:S(2)}) collective-permute-start(bf16[2,2,128,512]{3,2,1,0:T(8,128)(2,1)S(1)} %collective-permute-done.21.refs_19_.refs_13_.refs_15_), channel_id=1, source_target_pairs={{0,8},{8,0},{16,24},{24,16},{1,9},{9,1},{17,25},{25,17},{2,10},{10... | collective-permute-start | bytes 1572872 | tf_op jit(solution)/shard_map/ppermute | solution.py:395
  227.6 24.0 %collective-permute-start.31 = (bf16[2,2,128,512]{3,2,1,0:T(8,128)(2,1)}, bf16[2,2,128,512]{3,2,1,0:T(8,128)(2,1)S(1)}, u32[]{:S(2)}, u32[]{:S(2)}) collective-permute-start(bf16[2,2,128,512]{3,2,1,0:T(8,128)(2,1)} %shard_map.146.refs_10_.refs_20_.refs_22_), channel_id=1, source_target_pairs={{0,16},{8,24},{16,0},{24,8},{1,17},{9,25},{17,1},{25,9},{2,18},{10... | collective-permute-start | bytes 1572872 | tf_op jit(solution)/shard_map/ppermute | solution.py:395
  228.5 30.2 %collective-permute-start.27 = (bf16[2,2,128,512]{3,2,1,0:T(8,128)(2,1)S(1)}, bf16[2,2,128,512]{3,2,1,0:T(8,128)(2,1)}, u32[]{:S(2)}, u32[]{:S(2)}) collective-permute-start(bf16[2,2,128,512]{3,2,1,0:T(8,128)(2,1)S(1)} %copy-done.3), channel_id=1, source_target_pairs={{0,8},{8,0},{16,24},{24,16},{1,9},{9,1},{17,25},{25,17},{2,10},{10... | collective-permute-start | bytes 1572872 | tf_op jit(solution)/shard_map/ppermute | solution.py:395
  241.3 19.7 %collective-permute-start.28 = (bf16[2,2,128,512]{3,2,1,0:T(8,128)(2,1)}, bf16[2,2,128,512]{3,2,1,0:T(8,128)(2,1)}, u32[]{:S(2)}, u32[]{:S(2)}) collective-permute-start(bf16[2,2,128,512]{3,2,1,0:T(8,128)(2,1)} %collective-permute-done.26.refs_23_.refs_17_.refs_19_), channel_id=1, source_target_pairs={{0,8},{8,0},{16,24},{24,16},{1,9},{9,1},{17,25},{25,17},{2,10},{10... | collective-permute-start | bytes 1572872 | tf_op jit(solution)/shard_map/ppermute | solution.py:395
  241.3 21.0 %collective-permute-start.32 = (bf16[2,2,128,512]{3,2,1,0:T(8,128)(2,1)}, bf16[2,2,128,512]{3,2,1,0:T(8,128)(2,1)S(1)}, u32[]{:S(2)}, u32[]{:S(2)}) collective-permute-start(bf16[2,2,128,512]{3,2,1,0:T(8,128)(2,1)} %shard_map.146.refs_10_.refs_20_.refs_22_), channel_id=1, source_target_pairs={{0,8},{8,0},{16,24},{24,16},{1,9},{9,1},{17,25},{25,17},{2,10},{10... | collective-permute-start | bytes 1572872 | tf_op jit(solution)/shard_map/ppermute | solution.py:395
  251.6 12.4 %collective-permute-start.33 = (bf16[2,2,128,512]{3,2,1,0:T(8,128)(2,1)S(1)}, bf16[2,2,128,512]{3,2,1,0:T(8,128)(2,1)S(1)}, u32[]{:S(2)}, u32[]{:S(2)}) collective-permute-start(bf16[2,2,128,512]{3,2,1,0:T(8,128)(2,1)S(1)} %collective-permute-done.31.refs_11_.refs_21_.refs_23_), channel_id=1, source_target_pairs={{0,8},{8,0},{16,24},{24,16},{1,9},{9,1},{17,25},{25,17},{2,10},{10... | collective-permute-start | bytes 1572872 | tf_op jit(solution)/shard_map/ppermute | solution.py:395
  252.4 55.6 %collective-permute-start.12 = (bf16[128,4096]{1,0:T(8,128)(2,1)}, bf16[128,4096]{1,0:T(8,128)(2,1)}, u32[]{:S(2)}, u32[]{:S(2)}) collective-permute-start(bf16[128,4096]{1,0:T(8,128)(2,1)} %collective-permute-done.11.refs_3_.refs_4_), channel_id=1, source_target_pairs={{5,4},{2,3},{13,12},{10,11},{21,20},{18,19},{29,28},{26,27}} | collective-permute-start | bytes 3145736 | tf_op jit(solution)/shard_map/ppermute | solution.py:371
  258.8 49.3 %collective-permute-start.13 = (bf16[128,4096]{1,0:T(8,128)(2,1)}, bf16[128,4096]{1,0:T(8,128)(2,1)}, u32[]{:S(2)}, u32[]{:S(2)}) collective-permute-start(bf16[128,4096]{1,0:T(8,128)(2,1)} %copy-done.10), channel_id=1, source_target_pairs={{5,4},{2,3},{13,12},{10,11},{21,20},{18,19},{29,28},{26,27}} | collective-permute-start | bytes 3145736 | tf_op jit(solution)/shard_map/ppermute | solution.py:371
  261.0 47.0 %collective-permute-start.8 = (bf16[128,4096]{1,0:T(8,128)(2,1)S(1)}, bf16[128,4096]{1,0:T(8,128)(2,1)}, u32[]{:S(2)}, u32[]{:S(2)}) collective-permute-start(bf16[128,4096]{1,0:T(8,128)(2,1)S(1)} %copy-done.9), channel_id=1, source_target_pairs={{3,2},{4,5},{11,10},{12,13},{19,18},{20,21},{27,26},{28,29}} | collective-permute-start | bytes 3145736 | tf_op jit(solution)/shard_map/ppermute | solution.py:371
  262.3 45.7 %collective-permute-start.3 = (bf16[128,4096]{1,0:T(8,128)(2,1)}, bf16[128,4096]{1,0:T(8,128)(2,1)}, u32[]{:S(2)}, u32[]{:S(2)}) collective-permute-start(bf16[128,4096]{1,0:T(8,128)(2,1)} %collective-permute-done.2.refs_0_), channel_id=1, source_target_pairs={{1,0},{4,6},{6,7},{3,1},{9,8},{12,14},{14,15},{11,9},{17,16},{20,2... | collective-permute-start | bytes 3145736 | tf_op jit(solution)/shard_map/ppermute | solution.py:481
  264.0 44.1 %collective-permute-start.7 = (bf16[128,4096]{1,0:T(8,128)(2,1)}, bf16[128,4096]{1,0:T(8,128)(2,1)}, u32[]{:S(2)}, u32[]{:S(2)}) collective-permute-start(bf16[128,4096]{1,0:T(8,128)(2,1)} %collective-permute-done.6.refs_4_.refs_3_), channel_id=1, source_target_pairs={{2,0},{7,6},{5,7},{0,1},{10,8},{15,14},{13,15},{8,9},{18,16},{23,2... | collective-permute-start | bytes 3145736 | tf_op jit(solution)/shard_map/ppermute | solution.py:481
  (20 other events, 736.1 us)

commit v2 on v1

--- a/solution.py
+++ b/solution.py
@@ -192,12 +192,12 @@
     )(device, jnp.asarray(place), *operands)
 
 
-def job(device, base, row_blocks, columns, absent, used, span, total, full, accumulate, choice=()):
+def job(device, base, row_blocks, columns, absent, used, span, total, full, accumulate, choice=(), groups=1):
     rows = row_blocks[0][0][0].shape[0]
     count, height = len(row_blocks), len(row_blocks) * rows
     chunks = 1 + max(column[3] for column in columns)
     depth = total if full else len(columns) * rows
-    span_depth = depth // chunks
+    chunk_depth = depth // chunks
     plan = np.stack(
         [first for _, first in row_blocks]
         + [column[2] for column in columns]
@@ -212,6 +212,9 @@
             sources.append(pieces)
         source_at.append([source is pieces for source in sources].index(True))
     given = [] if base is None else [base]
+    bounds = [count * turn // groups for turn in range(groups + 1)]
+    turns = list(zip(bounds[:-1], bounds[1:]))
+    members = [[at for at, column in enumerate(columns) if column[3] == c] for c in range(chunks)]
 
     def kernel(device_ref, plan_ref, used_ref, *refs):
         plane_refs = refs[: len(planes)]
@@ -222,89 +225,107 @@
         def first_of(at):
             return pl.multiple_of(plan_ref[me, at], rows)
 
-        def held_copy(block, part, out):
+        def inner_of(chunk):
+            if not full:
+                return slice(None)
+            start = plan_ref[me, count + members[chunk][0]] // chunk_depth * chunk_depth
+            return pl.ds(pl.multiple_of(start, chunk_depth), chunk_depth)
+
+        def held_copy(block, part, out, sem):
             here = held.at[part, pl.ds(block * rows, rows), :]
             there = out_ref.at[part, pl.ds(first_of(block), rows), :]
             pair = (here, there) if out else (there, here)
-            return pltpu.make_async_copy(*pair, held_sem)
-
+            return pltpu.make_async_copy(*pair, sem)
+
+        def start_left(turn, chunk):
+            sem, inner = left_sem.at[turn, chunk], inner_of(chunk)
+            for block in range(*turns[turn]):
+                for part in range(2):
+                    here = pl.ds(block * rows, rows)
+                    if not full:
+                        for at in range(len(columns)):
+                            pltpu.make_async_copy(
+                                plane_refs[2 * block + part].at[:, pl.ds(first_of(count + at), rows)],
+                                left.at[part, here, pl.ds(at * rows, rows)],
+                                sem,
+                            ).start()
+                        continue
+                    for at in range(len(planes) // 2 if choice else 1):
+                        ref = plane_refs[2 * (block + at) + part]
+                        copy = pltpu.make_async_copy(ref.at[:, inner], left.at[part, here, inner], sem)
+                        if choice:
+                            pl.when(plan_ref[me, plan.shape[1] - 1] == at)(copy.start)
+                        else:
+                            copy.start()
+
+        def start_right(chunk):
+            for at in members[chunk]:
+                row = first_of(count + at) if full else at * rows
+                for part in range(2):
+                    pltpu.make_async_copy(
+                        source_refs[source_at[at]].at[columns[at][1], part],
+                        right.at[part, pl.ds(row, rows), :],
+                        right_sem.at[chunk],
+                    ).start()
+
+        for chunk in range(chunks):
+            start_right(chunk)
+            start_left(0, chunk)
+        for turn in range(1, groups):
+            for chunk in range(chunks):
+                start_left(turn, chunk)
         if accumulate:
-            for block in range(count):
-                for part in range(2):
-                    held_copy(block, part, False).start()
-        else:
-            held[...] = jnp.zeros_like(held)
+            for turn in range(groups):
+                for block in range(*turns[turn]):
+                    for part in range(2):
+                        held_copy(block, part, False, held_sem.at[turn]).start()
         for at in range(len(absent)):
             row = first_of(count + len(columns) + at)
             right[:, pl.ds(row, rows), :] = jnp.zeros((3, rows, TILE_SIZE), jnp.bfloat16)
-        for at, (_, index, _, chunk) in enumerate(columns):
-            row = first_of(count + at) if full else at * rows
-            for part in range(2):
-                pltpu.make_async_copy(
-                    source_refs[source_at[at]].at[index, part],
-                    right.at[part, pl.ds(row, rows), :],
-                    right_sem.at[chunk],
-                ).start()
-        for block in range(count):
-            for part in range(2):
-                ref, here = plane_refs[2 * block + part], pl.ds(block * rows, rows)
-                if full and choice:
-                    for at in range(len(planes) // 2):
-
-                        @pl.when(plan_ref[me, plan.shape[1] - 1] == at)
+
+        for turn, (first, end) in enumerate(turns):
+            band = slice(first * rows, end * rows)
+            if accumulate:
+                view = held.at[:, pl.ds(first * rows, (end - first) * rows), :]
+                pltpu.make_async_copy(view, view, held_sem.at[turn]).wait()
+            for chunk in range(chunks):
+                inner = inner_of(chunk)
+                if turn == 0:
+                    view = right.at[pl.ds(0, 2), pl.ds(0, len(members[chunk]) * rows), :]
+                    pltpu.make_async_copy(view, view, right_sem.at[chunk]).wait()
+                    right[2, inner, :] = -right[1, inner, :]
+                view = left.at[:, pl.ds(0, (end - first) * rows), pl.ds(0, chunk_depth)]
+                pltpu.make_async_copy(view, view, left_sem.at[turn, chunk]).wait()
+                if full:
+                    start = plan_ref[me, count + members[chunk][0]] // chunk_depth * chunk_depth
+                    tiles = [(start + t, TILE_SIZE) for t in range(0, chunk_depth, TILE_SIZE)]
+                    spots = [pl.ds(pl.multiple_of(p, TILE_SIZE), n) for p, n in tiles]
+                else:
+                    tiles = [(plan_ref[me, count + at], rows) for at in members[chunk]]
+                    spots = [pl.ds(at * rows, rows) for at in members[chunk]]
+                for block in range(first, end):
+                    own_tile = plan_ref[me, block] // TILE_SIZE
+                    for (inner_row, size), spot in zip(tiles, spots):
+
+                        @pl.when(used_ref[own_tile, inner_row // TILE_SIZE] == 0)
                         def _():
-                            pltpu.make_async_copy(
-                                plane_refs[2 * at + part], left.at[part, here, :], left_sem
-                            ).start()
-
-                    continue
-                if full:
-                    pltpu.make_async_copy(ref, left.at[part, here, :], left_sem).start()
-                    continue
-                for at in range(len(columns)):
-                    pltpu.make_async_copy(
-                        ref.at[:, pl.ds(first_of(count + at), rows)],
-                        left.at[part, here, pl.ds(at * rows, rows)],
-                        left_sem,
-                    ).start()
-        pltpu.make_async_copy(left, left, left_sem).wait()
-        if accumulate:
-            pltpu.make_async_copy(held, held, held_sem).wait()
-
-        for chunk in range(chunks):
-            members = [at for at, column in enumerate(columns) if column[3] == chunk]
-            bytes_view = right.at[pl.ds(0, 2), pl.ds(0, len(members) * rows), :]
-            pltpu.make_async_copy(bytes_view, bytes_view, right_sem.at[chunk]).wait()
-            if full:
-                base_row = plan_ref[me, count + members[0]] // span_depth * span_depth
-                inner = pl.ds(pl.multiple_of(base_row, span_depth), span_depth)
-                pieces = [(base_row + t * TILE_SIZE, TILE_SIZE) for t in range(span_depth // TILE_SIZE)]
-                spots = [pl.ds(pl.multiple_of(p, TILE_SIZE), n) for p, n in pieces]
-            else:
-                inner = slice(None)
-                pieces = [(plan_ref[me, count + at], rows) for at in members]
-                spots = [pl.ds(at * rows, rows) for at in members]
-            for block in range(count):
-                own_tile = plan_ref[me, block] // TILE_SIZE
-                for (first, size), spot in zip(pieces, spots):
-
-                    @pl.when(used_ref[own_tile, first // TILE_SIZE] == 0)
-                    def _():
-                        left[:, block * rows : (block + 1) * rows, spot] = jnp.zeros(
-                            (2, rows, size), jnp.bfloat16
-                        )
-
-            right[2, inner, :] = -right[1, inner, :]
-            lead, trail = left[0, :, inner], left[1, :, inner]
-            for part, (upper, lower) in enumerate(((0, 2), (1, 0))):
-                held[part] += jnp.dot(
-                    lead, right[upper, inner, :], preferred_element_type=jnp.float32
-                ) + jnp.dot(trail, right[lower, inner, :], preferred_element_type=jnp.float32)
-
-        for block in range(count):
-            for part in range(2):
-                held_copy(block, part, True).start()
-        pltpu.make_async_copy(held, held, held_sem).wait()
+                            left[:, block * rows : (block + 1) * rows, spot] = jnp.zeros(
+                                (2, rows, size), jnp.bfloat16
+                            )
+
+                lead, trail = left[0, band, inner], left[1, band, inner]
+                for part, (upper, lower) in enumerate(((0, 2), (1, 0))):
+                    both = jnp.dot(
+                        lead, right[upper, inner, :], preferred_element_type=jnp.float32
+                    ) + jnp.dot(trail, right[lower, inner, :], preferred_element_type=jnp.float32)
+                    if chunk == 0 and not accumulate:
+                        held[part, band] = both
+                    else:
+                        held[part, band] += both
+                    if chunk == chunks - 1:
+                        for block in range(first, end):
+                            held_copy(block, part, True, held_sem.at[groups]).start()
+        pltpu.make_async_copy(held, held, held_sem.at[groups]).wait()
 
     operands = planes + sources + given
     moved = 4 * height * depth + 4 * depth * TILE_SIZE + 8 * height * TILE_SIZE
@@ -320,9 +341,9 @@
                 pltpu.VMEM((2, height, depth), jnp.bfloat16),
                 pltpu.VMEM((3, depth, TILE_SIZE), jnp.bfloat16),
                 pltpu.VMEM((2, height, TILE_SIZE), jnp.float32),
-                pltpu.SemaphoreType.DMA,
+                pltpu.SemaphoreType.DMA((groups, chunks)),
                 pltpu.SemaphoreType.DMA((chunks,)),
-                pltpu.SemaphoreType.DMA,
+                pltpu.SemaphoreType.DMA((groups + 1,)),
             ],
         ),
         input_output_aliases={} if base is None else {3 + len(operands) - 1: 0},
@@ -479,9 +500,11 @@
     last = []
     for part, plane in enumerate((ahead[0], behind[1])):
         last.append(lax.ppermute(plane, "rcv", turns[part]))
+    absent = [c[2] for c in late]
+    out = job(device, out, as_rows(outside), early, absent, used, span, total, True, False)
     packed = [(array, index, first, 0) for array, index, first, _ in late]
-    out = job(device, out, as_rows(inside), packed, [], used, span, total, False, True)
-    out = job(device, out, as_rows(outside), columns, [], used, span, total, True, False)
+    nearer = as_rows(inside + outside)
+    out = job(device, out, nearer, packed, [], used, span, total, False, True, groups=3)
     chosen = np.zeros(devices)
     for number, offset in enumerate((-1, 1), start=1):
         for _, target in from_mate(offset):

time: 323 us -> 319 us (0.988)
  Pallas kernels: 77.1 us -> 72.9 us
    pallas_call x4, Pallas kernels: 50.3 us -> 46.1 us  [job(): pl.pallas_call(kernel, out_shape=jax.ShapeDtypeStruct((2, span, TILE_SIZE...]
where the time goes in v2:
time: 319 us; the launch traced here: 313 us
  waiting for transfers between devices  149 us (47%)
  Pallas kernels  72.9 us (23%)
  starting transfers between devices  57.6 us (18%)
  blocking collectives  29.9 us (9%)
    pallas_call x4, Pallas kernels, job(): pl.pallas_call(kernel, out_shape=jax.ShapeDtypeStruct((2, span, TILE_SIZE...  46.1 us
    ppermute x4, waiting for transfers between devices, local(): moved.append(lax.ppermute(ahead[part], 'rcv', forward))  34.1 us
    ppermute x15, waiting for transfers between devices, spread(): lax.ppermute(x, 'src', swap)  33.6 us
    all_to_all x1, blocking collectives, local(): lax.all_to_all(b, ('src', 'rcv'), split_axis=0, concat_axis=0, tiled=True)  29.9 us
    ppermute x2, waiting for transfers between devices, local(): ahead.append(lax.ppermute(own[part], 'rcv', forward))  24.7 us
    ppermute x4, waiting for transfers between devices, local(): moved.append(lax.ppermute(behind[part], 'rcv', backward))  23.1 us
    all_to_all x1, waiting for transfers between devices, local(): lax.all_to_all(b, ('src', 'rcv'), split_axis=0, concat_axis=0, tiled=True)  19.4 us
    pallas_call x5, Pallas kernels, cut(): pl.pallas_call(cut_kernel, out_shape=jax.ShapeDtypeStruct(shape, jnp.bflo...  14.6 us
  transfers between devices with their start and end apart: 35, of which 16 were waited for; matrix products, arithmetic and copies ran while one was open for 1% of the time, Pallas kernels for 20%

profile of v2, /device:TPU:18, one launch (start us, length us, event | category | flops | bytes accessed | tf_op | source)
XLA Modules:
  0.0 312.8 jit_solution(9963797198007711843)
XLA Ops:
  0.0 3.9 %shard_map.139 = (bf16[32,128,128]{2,1,0:T(8,128)(2,1)}, bf16[32,128,128]{2,1,0:T(8,128)(2,1)}) custom-call(bf16[2,128,4096]{2,1,0:T(8,128)(2,1)} %data_ref.5), custom_call_target="tpu_custom_call" | custom-call | tf_op jit(solution)/shard_map/pallas_call | solution.py:29
  4.0 29.9 %all_to_all.10.arrived_ref = bf16[32,128,128]{2,1,0:T(8,128)(2,1)} all-to-all(bf16[32,128,128]{2,1,0:T(8,128)(2,1)} %get-tuple-element.7), channel_id=1, replica_groups=mesh['src'=4,'rcv'=8] {'src','rcv'}, dimensions={0} | all-to-all | bytes 2097152 | tf_op jit(solution)/shard_map/all_to_all | solution.py:428
  33.9 6.2 %all-to-all-start.1 = ((bf16[32,128,128]{2,1,0:T(8,128)(2,1)}), bf16[32,128,128]{2,1,0:T(8,128)(2,1)S(1)}, u32[]{:S(2)}, u32[]{:S(2)}) async-start(bf16[32,128,128]{2,1,0:T(8,128)(2,1)} %get-tuple-element.8), calls=%async_computation.1 | async-start | bytes 2097152 | tf_op jit(solution)/shard_map/all_to_all | solution.py:428
  40.1 4.1 %shard_map.140.refs_0_ = bf16[128,4096]{1,0:T(8,128)(2,1)} custom-call(bf16[2,128,4096]{2,1,0:T(8,128)(2,1)} %data_ref.5, s32[128,4096]{1,0:T(8,128)} %mask_ref.3, bf16[32,128,128]{2,1,0:T(8,128)(2,1)} %all_to_all.10.arrived_ref), custom_call_target="tpu_custom_call" | custom-call | tf_op jit(solution)/shard_map/pallas_call | solution.py:54
  44.7 19.4 %all-to-all-done.1.arrived_ref = bf16[32,128,128]{2,1,0:T(8,128)(2,1)S(1)} async-done(((bf16[32,128,128]{2,1,0:T(8,128)(2,1)}), bf16[32,128,128]{2,1,0:T(8,128)(2,1)S(1)}, u32[]{:S(2)}, u32[]{:S(2)}) %all-to-all-start.1) | async-done | bytes 1048608 | tf_op jit(solution)/shard_map/all_to_all | solution.py:428
  65.1 4.1 %shard_map.141.refs_1_ = bf16[128,4096]{1,0:T(8,128)(2,1)} custom-call(bf16[2,128,4096]{2,1,0:T(8,128)(2,1)} %data_ref.5, s32[128,4096]{1,0:T(8,128)} %mask_ref.3, bf16[32,128,128]{2,1,0:T(8,128)(2,1)} %copy-done.7), custom_call_target="tpu_custom_call" | custom-call | tf_op jit(solution)/shard_map/pallas_call | solution.py:54
  73.1 13.2 %collective-permute-done.refs_0_.refs_2_ = bf16[128,4096]{1,0:T(8,128)(2,1)S(1)} collective-permute-done((bf16[128,4096]{1,0:T(8,128)(2,1)}, bf16[128,4096]{1,0:T(8,128)(2,1)S(1)}, u32[]{:S(2)}, u32[]{:S(2)}) %collective-permute-start) | collective-permute-done | bytes 1048608 | tf_op jit(solution)/shard_map/ppermute | solution.py:433
  88.7 6.8 %collective-permute-done.4.refs_4_.refs_5_ = bf16[128,4096]{1,0:T(8,128)(2,1)S(1)} collective-permute-done((bf16[128,4096]{1,0:T(8,128)(2,1)}, bf16[128,4096]{1,0:T(8,128)(2,1)S(1)}, u32[]{:S(2)}, u32[]{:S(2)}) %collective-permute-start.4) | collective-permute-done | bytes 1048608 | tf_op jit(solution)/shard_map/ppermute | solution.py:434
  97.3 11.5 %collective-permute-done.9.refs_1_.refs_3_ = bf16[128,4096]{1,0:T(8,128)(2,1)} collective-permute-done((bf16[128,4096]{1,0:T(8,128)(2,1)}, bf16[128,4096]{1,0:T(8,128)(2,1)}, u32[]{:S(2)}, u32[]{:S(2)}) %collective-permute-start.9) | collective-permute-done | bytes 1048608 | tf_op jit(solution)/shard_map/ppermute | solution.py:433
  111.3 6.8 %collective-permute-done.11.refs_3_.refs_4_ = bf16[128,4096]{1,0:T(8,128)(2,1)} collective-permute-done((bf16[128,4096]{1,0:T(8,128)(2,1)S(1)}, bf16[128,4096]{1,0:T(8,128)(2,1)}, u32[]{:S(2)}, u32[]{:S(2)}) %collective-permute-start.11) | collective-permute-done | bytes 1048608 | tf_op jit(solution)/shard_map/ppermute | solution.py:434
  121.6 2.7 shard_map.142
  126.8 4.4 %collective-permute-done.1.refs_0_.refs_6_ = bf16[128,4096]{1,0:T(8,128)(2,1)} collective-permute-done((bf16[128,4096]{1,0:T(8,128)(2,1)S(1)}, bf16[128,4096]{1,0:T(8,128)(2,1)}, u32[]{:S(2)}, u32[]{:S(2)}) %collective-permute-start.1) | collective-permute-done | bytes 1048608 | tf_op jit(solution)/shard_map/ppermute | solution.py:485
  131.2 2.6 collective-permute-start.2
  133.7 6.8 %collective-permute-done.5.refs_4_.refs_9_ = bf16[128,4096]{1,0:T(8,128)(2,1)} collective-permute-done((bf16[128,4096]{1,0:T(8,128)(2,1)S(1)}, bf16[128,4096]{1,0:T(8,128)(2,1)}, u32[]{:S(2)}, u32[]{:S(2)}) %collective-permute-start.5) | collective-permute-done | bytes 1048608 | tf_op jit(solution)/shard_map/ppermute | solution.py:486
  142.4 17.0 %collective-permute-done.24.refs_1_.refs_7_ = bf16[128,4096]{1,0:T(8,128)(2,1)} collective-permute-done((bf16[128,4096]{1,0:T(8,128)(2,1)}, bf16[128,4096]{1,0:T(8,128)(2,1)}, u32[]{:S(2)}, u32[]{:S(2)}) %collective-permute-start.24) | collective-permute-done | bytes 1048608 | tf_op jit(solution)/shard_map/ppermute | solution.py:485
  165.3 2.7 shard_map.143.refs_14_.refs_8_.refs_10_
  168.0 5.0 %collective-permute-start.18 = (bf16[1,2,128,512]{3,2,1,0:T(8,128)(2,1)}, bf16[1,2,128,512]{3,2,1,0:T(8,128)(2,1)}, u32[]{:S(2)}, u32[]{:S(2)}) collective-permute-start(bf16[1,2,128,512]{3,2,1,0:T(8,128)(2,1)} %shard_map.143.refs_14_.refs_8_.refs_10_), channel_id=1, source_target_pairs={{0,16},{8,24},{16,0},{24,8},{1,17},{9,25},{17,1},{25,9},{2,18},{10... | collective-permute-start | bytes 786440 | tf_op jit(solution)/shard_map/ppermute | solution.py:416
  173.0 6.2 %collective-permute-done.18.refs_15_.refs_9_.refs_11_ = bf16[1,2,128,512]{3,2,1,0:T(8,128)(2,1)} collective-permute-done((bf16[1,2,128,512]{3,2,1,0:T(8,128)(2,1)}, bf16[1,2,128,512]{3,2,1,0:T(8,128)(2,1)}, u32[]{:S(2)}, u32[]{:S(2)}) %collective-permute-start.18) | collective-permute-done | bytes 262176 | tf_op jit(solution)/shard_map/ppermute | solution.py:416
  180.9 3.0 shard_map.144.refs_18_.refs_12_.refs_14_
  183.9 4.8 %collective-permute-done.15.refs_11_.refs_5_.refs_7_ = bf16[1,2,128,512]{3,2,1,0:T(8,128)(2,1)} collective-permute-done((bf16[1,2,128,512]{3,2,1,0:T(8,128)(2,1)}, bf16[1,2,128,512]{3,2,1,0:T(8,128)(2,1)}, u32[]{:S(2)}, u32[]{:S(2)}) %collective-permute-start.15) | collective-permute-done | bytes 262176 | tf_op jit(solution)/shard_map/ppermute | solution.py:416
  190.5 6.1 %collective-permute-done.6.refs_4_.refs_3_.refs_13_ = bf16[128,4096]{1,0:T(8,128)(2,1)S(1)} collective-permute-done((bf16[128,4096]{1,0:T(8,128)(2,1)}, bf16[128,4096]{1,0:T(8,128)(2,1)S(1)}, u32[]{:S(2)}, u32[]{:S(2)}) %collective-permute-start.6) | collective-permute-done | bytes 1048608 | tf_op jit(solution)/shard_map/ppermute | solution.py:486
  196.6 12.7 %collective-permute-done.29.refs_1_.refs_11_ = bf16[128,4096]{1,0:T(8,128)(2,1)S(1)} collective-permute-done((bf16[128,4096]{1,0:T(8,128)(2,1)}, bf16[128,4096]{1,0:T(8,128)(2,1)S(1)}, u32[]{:S(2)}, u32[]{:S(2)}) %collective-permute-start.29) | collective-permute-done | bytes 1048608 | tf_op jit(solution)/shard_map/ppermute | solution.py:485
  209.3 9.0 %collective-permute-done.30.refs_3_.refs_2_.refs_12_ = bf16[128,4096]{1,0:T(8,128)(2,1)} collective-permute-done((bf16[128,4096]{1,0:T(8,128)(2,1)}, bf16[128,4096]{1,0:T(8,128)(2,1)}, u32[]{:S(2)}, u32[]{:S(2)}) %collective-permute-start.30) | collective-permute-done | bytes 1048608 | tf_op jit(solution)/shard_map/ppermute | solution.py:486
  218.3 3.0 shard_map.145.refs_22_.refs_16_.refs_18_
  221.3 3.2 %shard_map.146.refs_14_.refs_22_ = bf16[2,2,128,512]{3,2,1,0:T(8,128)(2,1)} custom-call(s32[1]{0:T(128)} %bitcast.device_ref, s32[32,3]{1,0:T(8,128)} %constant.44.clone.place_ref, bf16[128,4096]{1,0:T(8,128)(2,1)} %copy-done.2, bf16[128,4096]{1,0:T(8,128)(2,1)} %copy-done.4, f32[8,128,1]{2,1,0:T(8,128)} %copy.26.refs_2_.refs_5_, ...), custom_call_target="tpu_custom_call" | custom-call | tf_op jit(solution)/shard_map/pallas_call | solution.py:183
  228.7 12.7 %collective-permute-done.26.refs_23_.refs_17_.refs_19_ = bf16[2,2,128,512]{3,2,1,0:T(8,128)(2,1)S(1)} collective-permute-done((bf16[2,2,128,512]{3,2,1,0:T(8,128)(2,1)}, bf16[2,2,128,512]{3,2,1,0:T(8,128)(2,1)S(1)}, u32[]{:S(2)}, u32[]{:S(2)}) %collective-permute-start.26) | collective-permute-done | bytes 524320 | tf_op jit(solution)/shard_map/ppermute | solution.py:416
  241.9 9.8 %collective-permute-done.31.refs_15_.refs_23_ = bf16[2,2,128,512]{3,2,1,0:T(8,128)(2,1)S(1)} collective-permute-done((bf16[2,2,128,512]{3,2,1,0:T(8,128)(2,1)}, bf16[2,2,128,512]{3,2,1,0:T(8,128)(2,1)S(1)}, u32[]{:S(2)}, u32[]{:S(2)}) %collective-permute-start.31) | collective-permute-done | bytes 524320 | tf_op jit(solution)/shard_map/ppermute | solution.py:416
  252.5 6.4 %collective-permute-start.12 = (bf16[128,4096]{1,0:T(8,128)(2,1)}, bf16[128,4096]{1,0:T(8,128)(2,1)}, u32[]{:S(2)}, u32[]{:S(2)}) collective-permute-start(bf16[128,4096]{1,0:T(8,128)(2,1)} %collective-permute-done.11.refs_3_.refs_4_), channel_id=1, source_target_pairs={{5,4},{2,3},{13,12},{10,11},{21,20},{18,19},{29,28},{26,27}} | collective-permute-start | bytes 3145736 | tf_op jit(solution)/shard_map/ppermute | solution.py:392
  266.5 17.4 %shard_map.147.refs_20_ = f32[2,1024,512]{2,1,0:T(8,128)} custom-call(s32[1]{0:T(128)} %bitcast.device_ref, s32[32,37]{1,0:T(8,128)} %constant.45.clone.plan_ref, s32[2,8]{1,0:T(2,128)} %convert_element_type.3.used_ref, bf16[128,4096]{1,0:T(8,128)(2,1)} %shard_map.140.refs_0_, bf16[128,4096]{1,0:T(8,128)(2,1)} %shard_map.141.refs_1_, ...), custom_call_target="tpu_custom_call" | custom-call | flops 10737418240 | bytes 21495808 | tf_op jit(solution)/shard_map/pallas_call | solution.py:332
  284.0 10.1 %shard_map.148.refs_18_ = f32[2,1024,512]{2,1,0:T(8,128)} custom-call(s32[1]{0:T(128)} %bitcast.device_ref, s32[32,34]{1,0:T(8,128)} %constant.46.clone.plan_ref, s32[2,8]{1,0:T(2,128)} %convert_element_type.3.used_ref, bf16[128,4096]{1,0:T(8,128)(2,1)} %copy-done.2, bf16[128,4096]{1,0:T(8,128)(2,1)} %copy-done.4, ...), custom_call_target="tpu_custom_call", output_to_operand_aliasing={{}: (23, {})} | custom-call | flops 4294967296 | bytes 13631488 | tf_op jit(solution)/shard_map/pallas_call | solution.py:332
  294.0 10.9 %shard_map.149.refs_26_ = f32[2,1024,512]{2,1,0:T(8,128)} custom-call(s32[1]{0:T(128)} %bitcast.device_ref, s32[32,15]{1,0:T(8,128)} %constant.47.clone.plan_ref, s32[2,8]{1,0:T(2,128)} %convert_element_type.3.used_ref, bf16[128,4096]{1,0:T(8,128)(2,1)} %shard_map.140.refs_0_, ...), custom_call_target="tpu_custom_call", output_to_operand_aliasing={{}: (21, {})} | custom-call | flops 3758096384 | bytes 9437184 | tf_op jit(solution)/shard_map/pallas_call | solution.py:332
  305.0 7.6 %shard_map.150 = f32[2,1024,512]{2,1,0:T(8,128)} custom-call(s32[1]{0:T(128)} %bitcast.device_ref, s32[32,34]{1,0:T(8,128)} %constant.48.clone.plan_ref, s32[2,8]{1,0:T(2,128)} %convert_element_type.3.used_ref, bf16[128,4096]{1,0:T(8,128)(2,1)} %collective-permute-done.3.refs_0_, ...), custom_call_target="tpu_custom_call", output_to_operand_aliasing={{}: (29, {})} | custom-call | flops 2147483648 | bytes 11010048 | tf_op jit(solution)/shard_map/pallas_call | solution.py:332
  (89 shorter events, 42.2 us)
Async XLA Ops:
  33.9 30.3 %all-to-all-start.1 = ((bf16[32,128,128]{2,1,0:T(8,128)(2,1)}), bf16[32,128,128]{2,1,0:T(8,128)(2,1)S(1)}, u32[]{:S(2)}, u32[]{:S(2)}) async-start(bf16[32,128,128]{2,1,0:T(8,128)(2,1)} %get-tuple-element.8), calls=%async_computation.1 | async-start | bytes 2097152 | tf_op jit(solution)/shard_map/all_to_all | solution.py:428
  44.2 42.1 %collective-permute-start = (bf16[128,4096]{1,0:T(8,128)(2,1)}, bf16[128,4096]{1,0:T(8,128)(2,1)S(1)}, u32[]{:S(2)}, u32[]{:S(2)}) collective-permute-start(bf16[128,4096]{1,0:T(8,128)(2,1)} %shard_map.140.refs_0_), channel_id=1, source_target_pairs={{0,2},{2,4},{4,6},{6,7},{7,5},{5,3},{3,1},{1,0},{8,10},{10,12},{12... | collective-permute-start | bytes 3145736 | tf_op jit(solution)/shard_map/ppermute | solution.py:433
  69.2 26.2 %collective-permute-start.4 = (bf16[128,4096]{1,0:T(8,128)(2,1)}, bf16[128,4096]{1,0:T(8,128)(2,1)S(1)}, u32[]{:S(2)}, u32[]{:S(2)}) collective-permute-start(bf16[128,4096]{1,0:T(8,128)(2,1)} %shard_map.141.refs_1_), channel_id=1, source_target_pairs={{2,0},{4,2},{6,4},{7,6},{5,7},{3,5},{1,3},{0,1},{10,8},{12,10},{14... | collective-permute-start | bytes 3145736 | tf_op jit(solution)/shard_map/ppermute | solution.py:434
  71.1 37.7 %collective-permute-start.9 = (bf16[128,4096]{1,0:T(8,128)(2,1)}, bf16[128,4096]{1,0:T(8,128)(2,1)}, u32[]{:S(2)}, u32[]{:S(2)}) collective-permute-start(bf16[128,4096]{1,0:T(8,128)(2,1)} %shard_map.141.refs_1_), channel_id=1, source_target_pairs={{0,2},{2,4},{4,6},{6,7},{7,5},{5,3},{3,1},{1,0},{8,10},{10,12},{12... | collective-permute-start | bytes 3145736 | tf_op jit(solution)/shard_map/ppermute | solution.py:433
  71.3 46.8 %collective-permute-start.11 = (bf16[128,4096]{1,0:T(8,128)(2,1)S(1)}, bf16[128,4096]{1,0:T(8,128)(2,1)}, u32[]{:S(2)}, u32[]{:S(2)}) collective-permute-start(bf16[128,4096]{1,0:T(8,128)(2,1)S(1)} %copy-done.1), channel_id=1, source_target_pairs={{2,0},{4,2},{6,4},{7,6},{5,7},{3,5},{1,3},{0,1},{10,8},{12,10},{14... | collective-permute-start | bytes 3145736 | tf_op jit(solution)/shard_map/ppermute | solution.py:434
  86.3 44.8 %collective-permute-start.1 = (bf16[128,4096]{1,0:T(8,128)(2,1)S(1)}, bf16[128,4096]{1,0:T(8,128)(2,1)}, u32[]{:S(2)}, u32[]{:S(2)}) collective-permute-start(bf16[128,4096]{1,0:T(8,128)(2,1)S(1)} %collective-permute-done.refs_0_.refs_2_), channel_id=1, source_target_pairs={{0,2},{2,4},{4,6},{6,7},{7,5},{5,3},{3,1},{1,0},{8,10},{10,12},{12... | collective-permute-start | bytes 3145736 | tf_op jit(solution)/shard_map/ppermute | solution.py:485
  95.5 45.0 %collective-permute-start.5 = (bf16[128,4096]{1,0:T(8,128)(2,1)S(1)}, bf16[128,4096]{1,0:T(8,128)(2,1)}, u32[]{:S(2)}, u32[]{:S(2)}) collective-permute-start(bf16[128,4096]{1,0:T(8,128)(2,1)S(1)} %collective-permute-done.4.refs_4_.refs_5_), channel_id=1, source_target_pairs={{2,0},{4,2},{6,4},{7,6},{5,7},{3,5},{1,3},{0,1},{10,8},{12,10},{14... | collective-permute-start | bytes 3145736 | tf_op jit(solution)/shard_map/ppermute | solution.py:486
  108.8 50.6 %collective-permute-start.24 = (bf16[128,4096]{1,0:T(8,128)(2,1)}, bf16[128,4096]{1,0:T(8,128)(2,1)}, u32[]{:S(2)}, u32[]{:S(2)}) collective-permute-start(bf16[128,4096]{1,0:T(8,128)(2,1)} %collective-permute-done.9.refs_1_.refs_3_), channel_id=1, source_target_pairs={{0,2},{2,4},{4,6},{6,7},{7,5},{5,3},{3,1},{1,0},{8,10},{10,12},{12... | collective-permute-start | bytes 3145736 | tf_op jit(solution)/shard_map/ppermute | solution.py:485
  118.1 45.0 %collective-permute-start.25 = (bf16[128,4096]{1,0:T(8,128)(2,1)}, bf16[128,4096]{1,0:T(8,128)(2,1)}, u32[]{:S(2)}, u32[]{:S(2)}) collective-permute-start(bf16[128,4096]{1,0:T(8,128)(2,1)} %collective-permute-done.11.refs_3_.refs_4_), channel_id=1, source_target_pairs={{2,0},{4,2},{6,4},{7,6},{5,7},{3,5},{1,3},{0,1},{10,8},{12,10},{14... | collective-permute-start | bytes 3145736 | tf_op jit(solution)/shard_map/ppermute | solution.py:486
  124.4 43.6 %collective-permute-start.14 = (bf16[1,2,128,512]{3,2,1,0:T(8,128)(2,1)}, bf16[1,2,128,512]{3,2,1,0:T(8,128)(2,1)}, u32[]{:S(2)}, u32[]{:S(2)}) collective-permute-start(bf16[1,2,128,512]{3,2,1,0:T(8,128)(2,1)} %shard_map.142), channel_id=1, source_target_pairs={{0,7},{2,5},{4,3},{6,1},{7,0},{5,2},{3,4},{1,6},{8,15},{10,13},{12... | collective-permute-start | bytes 786440 | tf_op jit(solution)/shard_map/ppermute | solution.py:472
  131.2 59.2 %collective-permute-start.2 = (bf16[128,4096]{1,0:T(8,128)(2,1)}, bf16[128,4096]{1,0:T(8,128)(2,1)S(1)}, u32[]{:S(2)}, u32[]{:S(2)}) collective-permute-start(bf16[128,4096]{1,0:T(8,128)(2,1)} %collective-permute-done.1.refs_0_.refs_6_), channel_id=1, source_target_pairs={{0,2},{2,4},{4,6},{6,7},{7,5},{5,3},{3,1},{1,0},{8,10},{10,12},{12... | collective-permute-start | bytes 3145736 | tf_op jit(solution)/shard_map/ppermute | solution.py:485
  140.5 56.1 %collective-permute-start.6 = (bf16[128,4096]{1,0:T(8,128)(2,1)}, bf16[128,4096]{1,0:T(8,128)(2,1)S(1)}, u32[]{:S(2)}, u32[]{:S(2)}) collective-permute-start(bf16[128,4096]{1,0:T(8,128)(2,1)} %collective-permute-done.5.refs_4_.refs_9_), channel_id=1, source_target_pairs={{2,0},{4,2},{6,4},{7,6},{5,7},{3,5},{1,3},{0,1},{10,8},{12,10},{14... | collective-permute-start | bytes 3145736 | tf_op jit(solution)/shard_map/ppermute | solution.py:486
  159.3 50.0 %collective-permute-start.29 = (bf16[128,4096]{1,0:T(8,128)(2,1)}, bf16[128,4096]{1,0:T(8,128)(2,1)S(1)}, u32[]{:S(2)}, u32[]{:S(2)}) collective-permute-start(bf16[128,4096]{1,0:T(8,128)(2,1)} %collective-permute-done.24.refs_1_.refs_7_), channel_id=1, source_target_pairs={{0,2},{2,4},{4,6},{6,7},{7,5},{5,3},{3,1},{1,0},{8,10},{10,12},{12... | collective-permute-start | bytes 3145736 | tf_op jit(solution)/shard_map/ppermute | solution.py:485
  163.1 55.3 %collective-permute-start.30 = (bf16[128,4096]{1,0:T(8,128)(2,1)}, bf16[128,4096]{1,0:T(8,128)(2,1)}, u32[]{:S(2)}, u32[]{:S(2)}) collective-permute-start(bf16[128,4096]{1,0:T(8,128)(2,1)} %collective-permute-done.25.refs_3_.refs_8_), channel_id=1, source_target_pairs={{2,0},{4,2},{6,4},{7,6},{5,7},{3,5},{1,3},{0,1},{10,8},{12,10},{14... | collective-permute-start | bytes 3145736 | tf_op jit(solution)/shard_map/ppermute | solution.py:486
  168.0 11.2 %collective-permute-start.18 = (bf16[1,2,128,512]{3,2,1,0:T(8,128)(2,1)}, bf16[1,2,128,512]{3,2,1,0:T(8,128)(2,1)}, u32[]{:S(2)}, u32[]{:S(2)}) collective-permute-start(bf16[1,2,128,512]{3,2,1,0:T(8,128)(2,1)} %shard_map.143.refs_14_.refs_8_.refs_10_), channel_id=1, source_target_pairs={{0,16},{8,24},{16,0},{24,8},{1,17},{9,25},{17,1},{25,9},{2,18},{10... | collective-permute-start | bytes 786440 | tf_op jit(solution)/shard_map/ppermute | solution.py:416
  188.7 38.8 %collective-permute-start.21 = (bf16[2,2,128,512]{3,2,1,0:T(8,128)(2,1)}, bf16[2,2,128,512]{3,2,1,0:T(8,128)(2,1)}, u32[]{:S(2)}, u32[]{:S(2)}) collective-permute-start(bf16[2,2,128,512]{3,2,1,0:T(8,128)(2,1)} %shard_map.144.refs_18_.refs_12_.refs_14_), channel_id=1, source_target_pairs={{0,16},{8,24},{16,0},{24,8},{1,17},{9,25},{17,1},{25,9},{2,18},{10... | collective-permute-start | bytes 1572872 | tf_op jit(solution)/shard_map/ppermute | solution.py:416
  190.4 34.1 %collective-permute-start.19 = (bf16[1,2,128,512]{3,2,1,0:T(8,128)(2,1)S(1)}, bf16[1,2,128,512]{3,2,1,0:T(8,128)(2,1)}, u32[]{:S(2)}, u32[]{:S(2)}) collective-permute-start(bf16[1,2,128,512]{3,2,1,0:T(8,128)(2,1)S(1)} %copy-done.8), channel_id=1, source_target_pairs={{0,8},{8,0},{16,24},{24,16},{1,9},{9,1},{17,25},{25,17},{2,10},{10... | collective-permute-start | bytes 786440 | tf_op jit(solution)/shard_map/ppermute | solution.py:416
  196.6 29.2 %collective-permute-start.20 = (bf16[1,2,128,512]{3,2,1,0:T(8,128)(2,1)}, bf16[1,2,128,512]{3,2,1,0:T(8,128)(2,1)}, u32[]{:S(2)}, u32[]{:S(2)}) collective-permute-start(bf16[1,2,128,512]{3,2,1,0:T(8,128)(2,1)} %collective-permute-done.18.refs_15_.refs_9_.refs_11_), channel_id=1, source_target_pairs={{0,8},{8,0},{16,24},{24,16},{1,9},{9,1},{17,25},{25,17},{2,10},{10... | collective-permute-start | bytes 786440 | tf_op jit(solution)/shard_map/ppermute | solution.py:416
  209.3 17.0 %collective-permute-start.16 = (bf16[1,2,128,512]{3,2,1,0:T(8,128)(2,1)}, bf16[1,2,128,512]{3,2,1,0:T(8,128)(2,1)}, u32[]{:S(2)}, u32[]{:S(2)}) collective-permute-start(bf16[1,2,128,512]{3,2,1,0:T(8,128)(2,1)} %collective-permute-done.14.refs_10_.refs_4_.refs_6_), channel_id=1, source_target_pairs={{0,8},{8,0},{16,24},{24,16},{1,9},{9,1},{17,25},{25,17},{2,10},{10... | collective-permute-start | bytes 786440 | tf_op jit(solution)/shard_map/ppermute | solution.py:416
  224.5 28.0 %collective-permute-start.10 = (bf16[128,4096]{1,0:T(8,128)(2,1)}, bf16[128,4096]{1,0:T(8,128)(2,1)}, u32[]{:S(2)}, u32[]{:S(2)}) collective-permute-start(bf16[128,4096]{1,0:T(8,128)(2,1)} %collective-permute-done.9.refs_1_.refs_3_), channel_id=1, source_target_pairs={{3,2},{4,5},{11,10},{12,13},{19,18},{20,21},{27,26},{28,29}} | collective-permute-start | bytes 3145736 | tf_op jit(solution)/shard_map/ppermute | solution.py:392
  226.4 15.0 %collective-permute-start.26 = (bf16[2,2,128,512]{3,2,1,0:T(8,128)(2,1)}, bf16[2,2,128,512]{3,2,1,0:T(8,128)(2,1)S(1)}, u32[]{:S(2)}, u32[]{:S(2)}) collective-permute-start(bf16[2,2,128,512]{3,2,1,0:T(8,128)(2,1)} %shard_map.145.refs_22_.refs_16_.refs_18_), channel_id=1, source_target_pairs={{0,16},{8,24},{16,0},{24,8},{1,17},{9,25},{17,1},{25,9},{2,18},{10... | collective-permute-start | bytes 1572872 | tf_op jit(solution)/shard_map/ppermute | solution.py:416
  227.5 13.9 %collective-permute-start.23 = (bf16[2,2,128,512]{3,2,1,0:T(8,128)(2,1)}, bf16[2,2,128,512]{3,2,1,0:T(8,128)(2,1)S(1)}, u32[]{:S(2)}, u32[]{:S(2)}) collective-permute-start(bf16[2,2,128,512]{3,2,1,0:T(8,128)(2,1)} %collective-permute-done.21.refs_19_.refs_13_.refs_15_), channel_id=1, source_target_pairs={{0,8},{8,0},{16,24},{24,16},{1,9},{9,1},{17,25},{25,17},{2,10},{10... | collective-permute-start | bytes 1572872 | tf_op jit(solution)/shard_map/ppermute | solution.py:416
  227.5 24.2 %collective-permute-start.31 = (bf16[2,2,128,512]{3,2,1,0:T(8,128)(2,1)}, bf16[2,2,128,512]{3,2,1,0:T(8,128)(2,1)S(1)}, u32[]{:S(2)}, u32[]{:S(2)}) collective-permute-start(bf16[2,2,128,512]{3,2,1,0:T(8,128)(2,1)} %shard_map.146.refs_14_.refs_22_), channel_id=1, source_target_pairs={{0,16},{8,24},{16,0},{24,8},{1,17},{9,25},{17,1},{25,9},{2,18},{10... | collective-permute-start | bytes 1572872 | tf_op jit(solution)/shard_map/ppermute | solution.py:416
  228.5 30.4 %collective-permute-start.27 = (bf16[2,2,128,512]{3,2,1,0:T(8,128)(2,1)}, bf16[2,2,128,512]{3,2,1,0:T(8,128)(2,1)S(1)}, u32[]{:S(2)}, u32[]{:S(2)}) collective-permute-start(bf16[2,2,128,512]{3,2,1,0:T(8,128)(2,1)} %shard_map.145.refs_22_.refs_16_.refs_18_), channel_id=1, source_target_pairs={{0,8},{8,0},{16,24},{24,16},{1,9},{9,1},{17,25},{25,17},{2,10},{10... | collective-permute-start | bytes 1572872 | tf_op jit(solution)/shard_map/ppermute | solution.py:416
  241.4 19.8 %collective-permute-start.28 = (bf16[2,2,128,512]{3,2,1,0:T(8,128)(2,1)S(1)}, bf16[2,2,128,512]{3,2,1,0:T(8,128)(2,1)S(1)}, u32[]{:S(2)}, u32[]{:S(2)}) collective-permute-start(bf16[2,2,128,512]{3,2,1,0:T(8,128)(2,1)S(1)} %collective-permute-done.26.refs_23_.refs_17_.refs_19_), channel_id=1, source_target_pairs={{0,8},{8,0},{16,24},{24,16},{1,9},{9,1},{17,25},{25,17},{2,10},{10... | collective-permute-start | bytes 1572872 | tf_op jit(solution)/shard_map/ppermute | solution.py:416
  241.4 21.1 %collective-permute-start.32 = (bf16[2,2,128,512]{3,2,1,0:T(8,128)(2,1)}, bf16[2,2,128,512]{3,2,1,0:T(8,128)(2,1)}, u32[]{:S(2)}, u32[]{:S(2)}) collective-permute-start(bf16[2,2,128,512]{3,2,1,0:T(8,128)(2,1)} %shard_map.146.refs_14_.refs_22_), channel_id=1, source_target_pairs={{0,8},{8,0},{16,24},{24,16},{1,9},{9,1},{17,25},{25,17},{2,10},{10... | collective-permute-start | bytes 1572872 | tf_op jit(solution)/shard_map/ppermute | solution.py:416
  251.7 12.5 %collective-permute-start.33 = (bf16[2,2,128,512]{3,2,1,0:T(8,128)(2,1)S(1)}, bf16[2,2,128,512]{3,2,1,0:T(8,128)(2,1)}, u32[]{:S(2)}, u32[]{:S(2)}) collective-permute-start(bf16[2,2,128,512]{3,2,1,0:T(8,128)(2,1)S(1)} %collective-permute-done.31.refs_15_.refs_23_), channel_id=1, source_target_pairs={{0,8},{8,0},{16,24},{24,16},{1,9},{9,1},{17,25},{25,17},{2,10},{10... | collective-permute-start | bytes 1572872 | tf_op jit(solution)/shard_map/ppermute | solution.py:416
  252.5 52.5 %collective-permute-start.12 = (bf16[128,4096]{1,0:T(8,128)(2,1)}, bf16[128,4096]{1,0:T(8,128)(2,1)}, u32[]{:S(2)}, u32[]{:S(2)}) collective-permute-start(bf16[128,4096]{1,0:T(8,128)(2,1)} %collective-permute-done.11.refs_3_.refs_4_), channel_id=1, source_target_pairs={{5,4},{2,3},{13,12},{10,11},{21,20},{18,19},{29,28},{26,27}} | collective-permute-start | bytes 3145736 | tf_op jit(solution)/shard_map/ppermute | solution.py:392
  258.9 46.1 %collective-permute-start.13 = (bf16[128,4096]{1,0:T(8,128)(2,1)}, bf16[128,4096]{1,0:T(8,128)(2,1)}, u32[]{:S(2)}, u32[]{:S(2)}) collective-permute-start(bf16[128,4096]{1,0:T(8,128)(2,1)} %copy-done.6), channel_id=1, source_target_pairs={{5,4},{2,3},{13,12},{10,11},{21,20},{18,19},{29,28},{26,27}} | collective-permute-start | bytes 3145736 | tf_op jit(solution)/shard_map/ppermute | solution.py:392
  261.2 43.8 %collective-permute-start.8 = (bf16[128,4096]{1,0:T(8,128)(2,1)}, bf16[128,4096]{1,0:T(8,128)(2,1)}, u32[]{:S(2)}, u32[]{:S(2)}) collective-permute-start(bf16[128,4096]{1,0:T(8,128)(2,1)} %copy-done.5), channel_id=1, source_target_pairs={{3,2},{4,5},{11,10},{12,13},{19,18},{20,21},{27,26},{28,29}} | collective-permute-start | bytes 3145736 | tf_op jit(solution)/shard_map/ppermute | solution.py:392
  262.5 42.5 %collective-permute-start.3 = (bf16[128,4096]{1,0:T(8,128)(2,1)}, bf16[128,4096]{1,0:T(8,128)(2,1)}, u32[]{:S(2)}, u32[]{:S(2)}) collective-permute-start(bf16[128,4096]{1,0:T(8,128)(2,1)} %copy-done.2), channel_id=1, source_target_pairs={{1,0},{4,6},{6,7},{3,1},{9,8},{12,14},{14,15},{11,9},{17,16},{20,2... | collective-permute-start | bytes 3145736 | tf_op jit(solution)/shard_map/ppermute | solution.py:502
  264.2 40.8 %collective-permute-start.7 = (bf16[128,4096]{1,0:T(8,128)(2,1)}, bf16[128,4096]{1,0:T(8,128)(2,1)}, u32[]{:S(2)}, u32[]{:S(2)}) collective-permute-start(bf16[128,4096]{1,0:T(8,128)(2,1)} %copy-done.3), channel_id=1, source_target_pairs={{2,0},{7,6},{5,7},{0,1},{10,8},{15,14},{13,15},{8,9},{18,16},{23,2... | collective-permute-start | bytes 3145736 | tf_op jit(solution)/shard_map/ppermute | solution.py:502
  (19 other events, 649.2 us)

commit v3 on v2

--- a/solution.py
+++ b/solution.py
@@ -192,164 +192,234 @@
     )(device, jnp.asarray(place), *operands)
 
 
-def job(device, base, row_blocks, columns, absent, used, span, total, full, accumulate, choice=(), groups=1):
-    rows = row_blocks[0][0][0].shape[0]
-    count, height = len(row_blocks), len(row_blocks) * rows
-    chunks = 1 + max(column[3] for column in columns)
-    depth = total if full else len(columns) * rows
-    chunk_depth = depth // chunks
-    plan = np.stack(
-        [first for _, first in row_blocks]
-        + [column[2] for column in columns]
-        + list(absent)
-        + list(choice),
-        axis=1,
-    ).astype(np.int32)
-    planes = [plane for block, _ in row_blocks for plane in block]
-    sources, source_at = [], []
-    for pieces, *_ in columns:
-        if not any(pieces is source for source in sources):
-            sources.append(pieces)
-        source_at.append([source is pieces for source in sources].index(True))
-    given = [] if base is None else [base]
-    bounds = [count * turn // groups for turn in range(groups + 1)]
-    turns = list(zip(bounds[:-1], bounds[1:]))
-    members = [[at for at, column in enumerate(columns) if column[3] == c] for c in range(chunks)]
-
-    def kernel(device_ref, plan_ref, used_ref, *refs):
-        plane_refs = refs[: len(planes)]
-        source_refs = refs[len(planes) : len(planes) + len(sources)]
-        out_ref, left, right, held, left_sem, right_sem, held_sem = refs[-7:]
-        me = device_ref[0]
-
-        def first_of(at):
-            return pl.multiple_of(plan_ref[me, at], rows)
-
-        def inner_of(chunk):
-            if not full:
-                return slice(None)
-            start = plan_ref[me, count + members[chunk][0]] // chunk_depth * chunk_depth
-            return pl.ds(pl.multiple_of(start, chunk_depth), chunk_depth)
-
-        def held_copy(block, part, out, sem):
-            here = held.at[part, pl.ds(block * rows, rows), :]
-            there = out_ref.at[part, pl.ds(first_of(block), rows), :]
-            pair = (here, there) if out else (there, here)
-            return pltpu.make_async_copy(*pair, sem)
-
-        def start_left(turn, chunk):
-            sem, inner = left_sem.at[turn, chunk], inner_of(chunk)
-            for block in range(*turns[turn]):
-                for part in range(2):
-                    here = pl.ds(block * rows, rows)
-                    if not full:
-                        for at in range(len(columns)):
-                            pltpu.make_async_copy(
-                                plane_refs[2 * block + part].at[:, pl.ds(first_of(count + at), rows)],
-                                left.at[part, here, pl.ds(at * rows, rows)],
-                                sem,
-                            ).start()
-                        continue
-                    for at in range(len(planes) // 2 if choice else 1):
-                        ref = plane_refs[2 * (block + at) + part]
-                        copy = pltpu.make_async_copy(ref.at[:, inner], left.at[part, here, inner], sem)
-                        if choice:
-                            pl.when(plan_ref[me, plan.shape[1] - 1] == at)(copy.start)
-                        else:
-                            copy.start()
-
-        def start_right(chunk):
-            for at in members[chunk]:
-                row = first_of(count + at) if full else at * rows
-                for part in range(2):
-                    pltpu.make_async_copy(
-                        source_refs[source_at[at]].at[columns[at][1], part],
-                        right.at[part, pl.ds(row, rows), :],
-                        right_sem.at[chunk],
-                    ).start()
-
-        for chunk in range(chunks):
-            start_right(chunk)
-            start_left(0, chunk)
-        for turn in range(1, groups):
-            for chunk in range(chunks):
-                start_left(turn, chunk)
-        if accumulate:
-            for turn in range(groups):
-                for block in range(*turns[turn]):
+class Job:
+    def __init__(self, row_blocks, columns, absent=(), choice=None, pack=(), packed=(), splits=()):
+        self.row_blocks, self.columns, self.absent = row_blocks, columns, list(absent)
+        self.choice, self.pack, self.packed = choice, list(pack), list(packed)
+        self.planes = [] if packed else [p for planes, _ in row_blocks for p in planes]
+        self.sources, self.source_at = [], []
+        for pieces, *_ in columns:
+            if not any(pieces is source for source in self.sources):
+                self.sources.append(pieces)
+            self.source_at.append([pieces is source for source in self.sources].index(True))
+        self.rows = columns[0][0].shape[2]
+        self.count = len(row_blocks)
+        self.chunks = 1 if packed else 1 + max(column[3] for column in columns)
+        bounds = [0, *splits, self.count]
+        self.turns = list(zip(bounds[:-1], bounds[1:]))
+
+    def numbers(self):
+        listed = [first for _, first in self.row_blocks] + [column[2] for column in self.columns]
+        listed += self.absent + [first for first, _ in self.pack]
+        return listed + ([] if self.choice is None else [self.choice])
+
+    def operands(self):
+        return self.planes + self.sources + [array for array, _ in self.packed]
+
+    def depth(self, total):
+        return len(self.columns) * self.rows if self.packed else total
+
+    def scratch(self, total):
+        height, depth = self.count * self.rows, self.depth(total)
+        shapes = [
+            pltpu.VMEM((2, height, depth), jnp.bfloat16),
+            pltpu.VMEM((3, depth, TILE_SIZE), jnp.bfloat16),
+            pltpu.VMEM((2, height, TILE_SIZE), jnp.float32),
+            pltpu.SemaphoreType.DMA((len(self.turns), self.chunks)),
+            pltpu.SemaphoreType.DMA((self.chunks,)),
+            pltpu.SemaphoreType.DMA((len(self.turns) + 1,)),
+        ]
+        if self.pack:
+            shapes.append(pltpu.VMEM((2, height, len(self.pack) * self.rows), jnp.bfloat16))
+            shapes.append(pltpu.SemaphoreType.DMA)
+        return shapes
+
+    def bind(self, number, used_ref, refs, out_ref, pack_ref, scratch, total):
+        self.number, self.used_ref, self.out_ref, self.pack_ref = number, used_ref, out_ref, pack_ref
+        self.plane_refs = refs[: len(self.planes)]
+        self.source_refs = refs[len(self.planes) : len(self.planes) + len(self.sources)]
+        self.packed_refs = refs[len(self.planes) + len(self.sources) :]
+        self.left, self.right, self.held, self.left_sem, self.right_sem, self.held_sem = scratch[:6]
+        self.packing = scratch[6:]
+        self.chunk_depth = self.depth(total) // self.chunks
+        self.members = [
+            [at for at, column in enumerate(self.columns) if self.packed or column[3] == chunk]
+            for chunk in range(self.chunks)
+        ]
+
+    def first_of(self, at):
+        return pl.multiple_of(self.number(at), self.rows)
+
+    def start_row(self, chunk):
+        return self.number(self.count + self.members[chunk][0]) // self.chunk_depth * self.chunk_depth
+
+    def inner_of(self, chunk):
+        if self.packed:
+            return slice(None)
+        return pl.ds(pl.multiple_of(self.start_row(chunk), self.chunk_depth), self.chunk_depth)
+
+    def held_copy(self, block, part, out, sem):
+        here = self.held.at[part, pl.ds(block * self.rows, self.rows), :]
+        there = self.out_ref.at[part, pl.ds(self.first_of(block), self.rows), :]
+        return pltpu.make_async_copy(*((here, there) if out else (there, here)), sem)
+
+    def start_right(self, chunk):
+        for at in self.members[chunk]:
+            row = at * self.rows if self.packed else self.first_of(self.count + at)
+            for part in range(2):
+                pltpu.make_async_copy(
+                    self.source_refs[self.source_at[at]].at[self.columns[at][1], part],
+                    self.right.at[part, pl.ds(row, self.rows), :],
+                    self.right_sem.at[chunk],
+                ).start()
+
+    def start_left(self, turn, chunk):
+        sem, inner = self.left_sem.at[turn, chunk], self.inner_of(chunk)
+        first, end = self.turns[turn]
+        rows, base = self.rows, 0
+        for ref, (_, blocks) in zip(self.packed_refs, self.packed):
+            low, high = max(first, base), min(end, base + blocks)
+            if low < high:
+                pltpu.make_async_copy(
+                    ref.at[:, pl.ds((low - base) * rows, (high - low) * rows), :],
+                    self.left.at[:, pl.ds(low * rows, (high - low) * rows), :],
+                    sem,
+                ).start()
+            base += blocks
+        if self.packed:
+            return
+        for block in range(first, end):
+            for part in range(2):
+                here = self.left.at[part, pl.ds(block * rows, rows), inner]
+                candidates = 1 if self.choice is None else len(self.planes) // 2
+                for at in range(candidates):
+                    ref = self.plane_refs[2 * (block + at) + part]
+                    copy = pltpu.make_async_copy(ref.at[:, inner], here, sem)
+                    if self.choice is None:
+                        copy.start()
+                    else:
+                        pl.when(self.number(len(self.numbers()) - 1) == at)(copy.start)
+
+    def start(self):
+        for chunk in range(self.chunks):
+            self.start_right(chunk)
+            self.start_left(0, chunk)
+        for turn in range(len(self.turns)):
+            if turn:
+                for chunk in range(self.chunks):
+                    self.start_left(turn, chunk)
+            if self.packed:
+                for block in range(*self.turns[turn]):
                     for part in range(2):
-                        held_copy(block, part, False, held_sem.at[turn]).start()
-        for at in range(len(absent)):
-            row = first_of(count + len(columns) + at)
+                        self.held_copy(block, part, False, self.held_sem.at[turn]).start()
+
+    def mask(self, chunk, first, end):
+        rows = self.rows
+        for block in range(first, end):
+            own_tile = self.number(block) // TILE_SIZE
+            for offset in range(0, self.chunk_depth, TILE_SIZE):
+                row = self.start_row(chunk) + offset
+                spot = pl.ds(pl.multiple_of(row, TILE_SIZE), TILE_SIZE)
+
+                @pl.when(self.used_ref[own_tile, row // TILE_SIZE] == 0)
+                def _():
+                    self.left[:, block * rows : (block + 1) * rows, spot] = jnp.zeros(
+                        (2, rows, TILE_SIZE), jnp.bfloat16
+                    )
+
+    def run(self):
+        rows, left, right, held = self.rows, self.left, self.right, self.held
+        for at in range(len(self.absent)):
+            row = self.first_of(self.count + len(self.columns) + at)
             right[:, pl.ds(row, rows), :] = jnp.zeros((3, rows, TILE_SIZE), jnp.bfloat16)
-
-        for turn, (first, end) in enumerate(turns):
+        pack_at = self.count + len(self.columns) + len(self.absent)
+        for turn, (first, end) in enumerate(self.turns):
             band = slice(first * rows, end * rows)
-            if accumulate:
+            if self.packed:
                 view = held.at[:, pl.ds(first * rows, (end - first) * rows), :]
-                pltpu.make_async_copy(view, view, held_sem.at[turn]).wait()
-            for chunk in range(chunks):
-                inner = inner_of(chunk)
+                pltpu.make_async_copy(view, view, self.held_sem.at[turn]).wait()
+            for chunk in range(self.chunks):
+                inner = self.inner_of(chunk)
                 if turn == 0:
-                    view = right.at[pl.ds(0, 2), pl.ds(0, len(members[chunk]) * rows), :]
-                    pltpu.make_async_copy(view, view, right_sem.at[chunk]).wait()
+                    view = right.at[pl.ds(0, 2), pl.ds(0, len(self.members[chunk]) * rows), :]
+                    pltpu.make_async_copy(view, view, self.right_sem.at[chunk]).wait()
                     right[2, inner, :] = -right[1, inner, :]
-                view = left.at[:, pl.ds(0, (end - first) * rows), pl.ds(0, chunk_depth)]
-                pltpu.make_async_copy(view, view, left_sem.at[turn, chunk]).wait()
-                if full:
-                    start = plan_ref[me, count + members[chunk][0]] // chunk_depth * chunk_depth
-                    tiles = [(start + t, TILE_SIZE) for t in range(0, chunk_depth, TILE_SIZE)]
-                    spots = [pl.ds(pl.multiple_of(p, TILE_SIZE), n) for p, n in tiles]
-                else:
-                    tiles = [(plan_ref[me, count + at], rows) for at in members[chunk]]
-                    spots = [pl.ds(at * rows, rows) for at in members[chunk]]
-                for block in range(first, end):
-                    own_tile = plan_ref[me, block] // TILE_SIZE
-                    for (inner_row, size), spot in zip(tiles, spots):
-
-                        @pl.when(used_ref[own_tile, inner_row // TILE_SIZE] == 0)
-                        def _():
-                            left[:, block * rows : (block + 1) * rows, spot] = jnp.zeros(
-                                (2, rows, size), jnp.bfloat16
-                            )
-
+                view = left.at[:, pl.ds(0, (end - first) * rows), pl.ds(0, self.chunk_depth)]
+                pltpu.make_async_copy(view, view, self.left_sem.at[turn, chunk]).wait()
+                if not self.packed:
+                    self.mask(chunk, first, end)
+                for at, (_, owner) in enumerate(self.pack):
+                    if owner == chunk:
+                        column = pl.ds(self.first_of(pack_at + at), rows)
+                        self.packing[0][:, band, at * rows : (at + 1) * rows] = left[:, band, column]
                 lead, trail = left[0, band, inner], left[1, band, inner]
                 for part, (upper, lower) in enumerate(((0, 2), (1, 0))):
                     both = jnp.dot(
                         lead, right[upper, inner, :], preferred_element_type=jnp.float32
                     ) + jnp.dot(trail, right[lower, inner, :], preferred_element_type=jnp.float32)
-                    if chunk == 0 and not accumulate:
+                    if chunk == 0 and not self.packed:
                         held[part, band] = both
                     else:
                         held[part, band] += both
-                    if chunk == chunks - 1:
+                    if chunk == self.chunks - 1:
                         for block in range(first, end):
-                            held_copy(block, part, True, held_sem.at[groups]).start()
-        pltpu.make_async_copy(held, held, held_sem.at[groups]).wait()
-
-    operands = planes + sources + given
-    moved = 4 * height * depth + 4 * depth * TILE_SIZE + 8 * height * TILE_SIZE
+                            self.held_copy(block, part, True, self.held_sem.at[len(self.turns)]).start()
+        if self.pack:
+            pltpu.make_async_copy(self.packing[0], self.pack_ref, self.packing[1]).start()
+
+    def finish(self):
+        if self.pack:
+            pltpu.make_async_copy(self.packing[0], self.pack_ref, self.packing[1]).wait()
+        pltpu.make_async_copy(self.held, self.held, self.held_sem.at[len(self.turns)]).wait()
+
+
+def launch(device, base, jobs, used, span, total):
+    plan = np.stack([n for job in jobs for n in job.numbers()], axis=1).astype(np.int32)
+    operands = [array for job in jobs for array in job.operands()]
+    operands += [] if base is None else [base]
+    packing = [job for job in jobs if job.pack]
+    scratch = [job.scratch(total) for job in jobs]
+    out_shape = [jax.ShapeDtypeStruct((2, span, TILE_SIZE), jnp.float32)]
+    for job in packing:
+        shape = (2, job.count * job.rows, len(job.pack) * job.rows)
+        out_shape.append(jax.ShapeDtypeStruct(shape, jnp.bfloat16))
+
+    def kernel(device_ref, plan_ref, used_ref, *refs):
+        outs = refs[len(operands) : len(operands) + len(out_shape)]
+        spare = refs[len(operands) + len(out_shape) :]
+        at, spare_at, plan_at = 0, 0, 0
+        for job, shapes in zip(jobs, scratch):
+            size = len(job.operands())
+            job.bind(
+                lambda n, plan_at=plan_at: plan_ref[device_ref[0], plan_at + n],
+                used_ref,
+                refs[at : at + size],
+                outs[0],
+                outs[1 + packing.index(job)] if job.pack else None,
+                spare[spare_at : spare_at + len(shapes)],
+                total,
+            )
+            at, spare_at, plan_at = at + size, spare_at + len(shapes), plan_at + len(job.numbers())
+        for job in jobs:
+            job.start()
+        for job in jobs:
+            job.run()
+        for job in jobs:
+            job.finish()
+
+    flops = sum(8 * job.count * job.rows * job.depth(total) * TILE_SIZE for job in jobs)
     return pl.pallas_call(
         kernel,
-        out_shape=jax.ShapeDtypeStruct((2, span, TILE_SIZE), jnp.float32),
+        out_shape=out_shape,
         grid_spec=pltpu.PrefetchScalarGridSpec(
             num_scalar_prefetch=3,
             grid=(1,),
             in_specs=[pl.BlockSpec(memory_space=pl.ANY)] * len(operands),
-            out_specs=pl.BlockSpec(memory_space=pl.ANY),
-            scratch_shapes=[
-                pltpu.VMEM((2, height, depth), jnp.bfloat16),
-                pltpu.VMEM((3, depth, TILE_SIZE), jnp.bfloat16),
-                pltpu.VMEM((2, height, TILE_SIZE), jnp.float32),
-                pltpu.SemaphoreType.DMA((groups, chunks)),
-                pltpu.SemaphoreType.DMA((chunks,)),
-                pltpu.SemaphoreType.DMA((groups + 1,)),
-            ],
+            out_specs=[pl.BlockSpec(memory_space=pl.ANY)] * len(out_shape),
+            scratch_shapes=[shape for shapes in scratch for shape in shapes],
         ),
         input_output_aliases={} if base is None else {3 + len(operands) - 1: 0},
-        cost_estimate=pl.CostEstimate(
-            flops=8 * height * depth * TILE_SIZE, bytes_accessed=moved, transcendentals=0
-        ),
+        cost_estimate=pl.CostEstimate(flops=flops, bytes_accessed=20 * span * total, transcendentals=0),
         compiler_params=pltpu.CompilerParams(vmem_limit_bytes=60 * 1024 * 1024),
     )(device, jnp.asarray(plan), used, *operands)
 
@@ -467,10 +537,6 @@
                 pairs.append((order[mate], order[i]))
         return pairs
 
-    across = [(order[i], order[(i + half) % rcv_count]) for i in range(rcv_count)]
-    far_pieces = cut([(own, origin(0))], far, gains, device)
-    far_pieces = lax.ppermute(far_pieces, "rcv", across)
-    spread(far_pieces, [far])
     collect([rows_of[0]])
     inside = [0] + [o for step in range(1, steps) for o in (-step, step)]
     outside = [-steps, steps]
@@ -489,10 +555,14 @@
     taken = [hop(rows_of[offset][0], from_mate(offset)) for offset in (-1, 1)]
     late_from = len(columns)
     collect([rows_of[-steps], rows_of[steps]])
+    across = [(order[i], order[(i + half) % rcv_count]) for i in range(rcv_count)]
+    far_pieces = cut([(own, origin(0))], far, gains, device)
+    far_pieces = lax.ppermute(far_pieces, "rcv", across)
+    spread(far_pieces, [far])
     early, late = columns[:late_from], columns[late_from:]
-    out = job(
-        device, None, as_rows(inside), early, [c[2] for c in late], used, span, total, True, False
-    )
+    absent, pack = [c[2] for c in late], [(c[2], c[3]) for c in late]
+    jobs = [Job(as_rows(inside), early, absent, pack=pack)]
+    out, packed_inside = launch(device, None, jobs, used, span, total)
     turns = [
         [(order[(i + d) % rcv_count], order[i]) for i in range(rcv_count) if i not in near]
         for d in (-1, 1)
@@ -500,18 +570,18 @@
     last = []
     for part, plane in enumerate((ahead[0], behind[1])):
         last.append(lax.ppermute(plane, "rcv", turns[part]))
-    absent = [c[2] for c in late]
-    out = job(device, out, as_rows(outside), early, absent, used, span, total, True, False)
-    packed = [(array, index, first, 0) for array, index, first, _ in late]
-    nearer = as_rows(inside + outside)
-    out = job(device, out, nearer, packed, [], used, span, total, False, True, groups=3)
+    jobs = [Job(as_rows(outside), early, absent, pack=pack)]
+    out, packed_outside = launch(device, out, jobs, used, span, total)
     chosen = np.zeros(devices)
     for number, offset in enumerate((-1, 1), start=1):
         for _, target in from_mate(offset):
             chosen[mine == target] = number
-    candidates = [(*last, *taken[0], *taken[1])]
-    rows_far = [(candidates[0], far * rows)]
-    return job(device, out, rows_far, columns, [], used, span, total, True, False, [chosen])
+    candidates = (*last, *taken[0], *taken[1])
+    packed = [(packed_inside, len(inside)), (packed_outside, len(outside))]
+    splits = [len(inside) // 2, len(inside)]
+    near_rows = Job(as_rows(inside + outside), late, packed=packed, splits=splits)
+    far_rows = Job([(candidates, far * rows)], columns, choice=chosen)
+    return launch(device, out, [near_rows, far_rows], used, span, total)[0]
 
 
 def solution(mesh):

time: 319 us -> 314 us (0.984)
  starting transfers between devices: 57.6 us -> 44.1 us
  waiting for transfers between devices: 149 us -> 154 us
  Pallas kernels: 72.9 us -> 76.5 us
    ppermute x1, waiting for transfers between devices: 0.01 us -> 46.5 us  [local(): far_pieces = lax.ppermute(far_pieces, 'rcv', across)]
    ppermute x2, waiting for transfers between devices: 24.7 us -> 0.01 us  [local(): ahead.append(lax.ppermute(own[part], 'rcv', forward))]
    ppermute x2, waiting for transfers between devices: 13.6 us -> 0.01 us  [local(): behind.append(lax.ppermute(own[part], 'rcv', backward))]
    ppermute x4, starting transfers between devices: 7.76 us -> 1.6 us  [local(): moved.append(lax.ppermute(behind[part], 'rcv', backward))]
    ppermute x15, starting transfers between devices: 11.7 us -> 6.32 us  [spread(): lax.ppermute(x, 'src', swap)]
    ppermute x15, waiting for transfers between devices: 33.6 us -> 28.6 us  [spread(): lax.ppermute(x, 'src', swap)]
    ppermute x4, waiting for transfers between devices: 23.1 us -> 27.1 us  [local(): moved.append(lax.ppermute(behind[part], 'rcv', backward))]
    pallas_call x4 -> x3, Pallas kernels: 46.1 us -> 49.8 us  [launch(): pl.pallas_call(kernel, out_shape=out_shape, grid_spec=pltpu.PrefetchScala...]
  transfers between devices with their start and end apart: 35 -> 35, of which waited for: 16 -> 14; matrix products, arithmetic and copies ran while one was open for 1% -> 1% of each run, Pallas kernels for 20% -> 15%
where the time goes in v3:
time: 314 us; the launch traced here: 310 us
  waiting for transfers between devices  154 us (49%)
  Pallas kernels  76.5 us (24%)
  starting transfers between devices  44.1 us (14%)
  blocking collectives  29.9 us (10%)
    pallas_call x3, Pallas kernels, launch(): pl.pallas_call(kernel, out_shape=out_shape, grid_spec=pltpu.PrefetchScala...  49.8 us
    ppermute x1, waiting for transfers between devices, local(): far_pieces = lax.ppermute(far_pieces, 'rcv', across)  46.5 us
    ppermute x4, waiting for transfers between devices, local(): moved.append(lax.ppermute(ahead[part], 'rcv', forward))  34.2 us
    all_to_all x1, blocking collectives, local(): lax.all_to_all(b, ('src', 'rcv'), split_axis=0, concat_axis=0, tiled=True)  29.9 us
    ppermute x15, waiting for transfers between devices, spread(): lax.ppermute(x, 'src', swap)  28.6 us
    ppermute x4, waiting for transfers between devices, local(): moved.append(lax.ppermute(behind[part], 'rcv', backward))  27.1 us
    all_to_all x1, waiting for transfers between devices, local(): lax.all_to_all(b, ('src', 'rcv'), split_axis=0, concat_axis=0, tiled=True)  17.9 us
    pallas_call x5, Pallas kernels, cut(): pl.pallas_call(cut_kernel, out_shape=jax.ShapeDtypeStruct(shape, jnp.bflo...  14.5 us
  transfers between devices with their start and end apart: 35, of which 14 were waited for; matrix products, arithmetic and copies ran while one was open for 1% of the time, Pallas kernels for 15%

profile of v3, /device:TPU:18, one launch (start us, length us, event | category | flops | bytes accessed | tf_op | source)
XLA Modules:
  0.0 309.7 jit_solution(189680859705065227)
XLA Ops:
  0.0 3.9 %shard_map.130 = (bf16[32,128,128]{2,1,0:T(8,128)(2,1)}, bf16[32,128,128]{2,1,0:T(8,128)(2,1)}) custom-call(bf16[2,128,4096]{2,1,0:T(8,128)(2,1)} %data_ref.5), custom_call_target="tpu_custom_call" | custom-call | tf_op jit(solution)/shard_map/pallas_call | solution.py:29
  3.9 29.9 %all_to_all.10.arrived_ref = bf16[32,128,128]{2,1,0:T(8,128)(2,1)} all-to-all(bf16[32,128,128]{2,1,0:T(8,128)(2,1)} %get-tuple-element.11), channel_id=1, replica_groups=mesh['src'=4,'rcv'=8] {'src','rcv'}, dimensions={0} | all-to-all | bytes 2097152 | tf_op jit(solution)/shard_map/all_to_all | solution.py:498
  33.9 6.2 %all-to-all-start.1 = ((bf16[32,128,128]{2,1,0:T(8,128)(2,1)}), bf16[32,128,128]{2,1,0:T(8,128)(2,1)S(1)}, u32[]{:S(2)}, u32[]{:S(2)}) async-start(bf16[32,128,128]{2,1,0:T(8,128)(2,1)} %get-tuple-element.12), calls=%async_computation.1 | async-start | bytes 2097152 | tf_op jit(solution)/shard_map/all_to_all | solution.py:498
  41.8 4.1 %shard_map.131.refs_0_ = bf16[128,4096]{1,0:T(8,128)(2,1)} custom-call(bf16[2,128,4096]{2,1,0:T(8,128)(2,1)} %data_ref.5, s32[128,4096]{1,0:T(8,128)} %mask_ref.3, bf16[32,128,128]{2,1,0:T(8,128)(2,1)} %all_to_all.10.arrived_ref), custom_call_target="tpu_custom_call" | custom-call | tf_op jit(solution)/shard_map/pallas_call | solution.py:54
  45.9 17.9 %all-to-all-done.1.arrived_ref = bf16[32,128,128]{2,1,0:T(8,128)(2,1)S(1)} async-done(((bf16[32,128,128]{2,1,0:T(8,128)(2,1)}), bf16[32,128,128]{2,1,0:T(8,128)(2,1)S(1)}, u32[]{:S(2)}, u32[]{:S(2)}) %all-to-all-start.1) | async-done | bytes 1048608 | tf_op jit(solution)/shard_map/all_to_all | solution.py:498
  64.8 4.1 %shard_map.132.refs_1_ = bf16[128,4096]{1,0:T(8,128)(2,1)} custom-call(bf16[2,128,4096]{2,1,0:T(8,128)(2,1)} %data_ref.5, s32[128,4096]{1,0:T(8,128)} %mask_ref.3, bf16[32,128,128]{2,1,0:T(8,128)(2,1)} %copy-done.2), custom_call_target="tpu_custom_call" | custom-call | tf_op jit(solution)/shard_map/pallas_call | solution.py:54
  68.9 2.7 shard_map.135.refs_10_.refs_4_.refs_16_
  71.6 1.7 collective-permute-start.19
  76.1 4.3 %collective-permute-done.19.refs_11_.refs_5_.refs_17_ = bf16[1,2,128,512]{3,2,1,0:T(8,128)(2,1)S(1)} collective-permute-done((bf16[1,2,128,512]{3,2,1,0:T(8,128)(2,1)}, bf16[1,2,128,512]{3,2,1,0:T(8,128)(2,1)S(1)}, u32[]{:S(2)}, u32[]{:S(2)}) %collective-permute-start.19) | collective-permute-done | bytes 262176 | tf_op jit(solution)/shard_map/ppermute | solution.py:486
  81.8 2.7 shard_map.134
  84.5 2.5 collective-permute-start.15
  87.0 46.5 %collective-permute-done.15.refs_4_.refs_32_ = bf16[1,2,128,512]{3,2,1,0:T(8,128)(2,1)S(1)} collective-permute-done((bf16[1,2,128,512]{3,2,1,0:T(8,128)(2,1)}, bf16[1,2,128,512]{3,2,1,0:T(8,128)(2,1)S(1)}, u32[]{:S(2)}, u32[]{:S(2)}) %collective-permute-start.15) | collective-permute-done | bytes 262176 | tf_op jit(solution)/shard_map/ppermute | solution.py:560
  136.6 2.0 collective-permute-start.1
  140.7 2.9 collective-permute-done.16.refs_5_.refs_33_
  145.3 3.0 shard_map.136.refs_14_.refs_8_.refs_20_
  149.7 13.2 %collective-permute-done.10.refs_4_.refs_9_ = bf16[128,4096]{1,0:T(8,128)(2,1)} collective-permute-done((bf16[128,4096]{1,0:T(8,128)(2,1)}, bf16[128,4096]{1,0:T(8,128)(2,1)}, u32[]{:S(2)}, u32[]{:S(2)}) %collective-permute-start.10) | collective-permute-done | bytes 1048608 | tf_op jit(solution)/shard_map/ppermute | solution.py:552
  163.0 2.0 collective-permute-start.2
  165.0 20.5 %collective-permute-done.4.refs_1_.refs_7_ = bf16[128,4096]{1,0:T(8,128)(2,1)} collective-permute-done((bf16[128,4096]{1,0:T(8,128)(2,1)}, bf16[128,4096]{1,0:T(8,128)(2,1)}, u32[]{:S(2)}, u32[]{:S(2)}) %collective-permute-start.4) | collective-permute-done | bytes 1048608 | tf_op jit(solution)/shard_map/ppermute | solution.py:551
  185.5 2.0 collective-permute-start.5
  187.6 2.1 collective-permute-done.23.refs_16_.refs_10_.refs_22_
  191.0 3.1 shard_map.137.refs_18_.refs_12_.refs_24_
  194.1 13.8 %collective-permute-done.11.refs_4_.refs_3_ = bf16[128,4096]{1,0:T(8,128)(2,1)} collective-permute-done((bf16[128,4096]{1,0:T(8,128)(2,1)}, bf16[128,4096]{1,0:T(8,128)(2,1)}, u32[]{:S(2)}, u32[]{:S(2)}) %collective-permute-start.11) | collective-permute-done | bytes 1048608 | tf_op jit(solution)/shard_map/ppermute | solution.py:552
  209.2 6.5 %collective-permute-start.32 = (bf16[128,4096]{1,0:T(8,128)(2,1)}, bf16[128,4096]{1,0:T(8,128)(2,1)}, u32[]{:S(2)}, u32[]{:S(2)}) collective-permute-start(bf16[128,4096]{1,0:T(8,128)(2,1)} %collective-permute-done.6.refs_3_.refs_4_), channel_id=1, source_target_pairs={{5,4},{2,3},{13,12},{10,11},{21,20},{18,19},{29,28},{26,27}} | collective-permute-start | bytes 3145736 | tf_op jit(solution)/shard_map/ppermute | solution.py:462
  215.8 13.6 %collective-permute-done.5.refs_1_ = bf16[128,4096]{1,0:T(8,128)(2,1)} collective-permute-done((bf16[128,4096]{1,0:T(8,128)(2,1)}, bf16[128,4096]{1,0:T(8,128)(2,1)}, u32[]{:S(2)}, u32[]{:S(2)}) %collective-permute-start.5) | collective-permute-done | bytes 1048608 | tf_op jit(solution)/shard_map/ppermute | solution.py:551
  230.0 3.0 shard_map.133.refs_0_.refs_28_
  233.3 10.7 %collective-permute-done.25.refs_19_.refs_13_.refs_25_ = bf16[2,2,128,512]{3,2,1,0:T(8,128)(2,1)} collective-permute-done((bf16[2,2,128,512]{3,2,1,0:T(8,128)(2,1)}, bf16[2,2,128,512]{3,2,1,0:T(8,128)(2,1)}, u32[]{:S(2)}, u32[]{:S(2)}) %collective-permute-start.25) | collective-permute-done | bytes 524320 | tf_op jit(solution)/shard_map/ppermute | solution.py:486
  245.5 3.8 %collective-permute-start.33 = (bf16[128,4096]{1,0:T(8,128)(2,1)}, bf16[128,4096]{1,0:T(8,128)(2,1)}, u32[]{:S(2)}, u32[]{:S(2)}) collective-permute-start(bf16[128,4096]{1,0:T(8,128)(2,1)} %collective-permute-done.9.refs_4_.refs_5_), channel_id=1, source_target_pairs={{5,4},{2,3},{13,12},{10,11},{21,20},{18,19},{29,28},{26,27}} | collective-permute-start | bytes 3145736 | tf_op jit(solution)/shard_map/ppermute | solution.py:462
  251.0 2.3 collective-permute-start.29
  253.3 5.3 %collective-permute-done.12.refs_1_.refs_29_ = bf16[2,2,128,512]{3,2,1,0:T(8,128)(2,1)S(1)} collective-permute-done((bf16[2,2,128,512]{3,2,1,0:T(8,128)(2,1)}, bf16[2,2,128,512]{3,2,1,0:T(8,128)(2,1)S(1)}, u32[]{:S(2)}, u32[]{:S(2)}) %collective-permute-start.12) | collective-permute-done | bytes 524320 | tf_op jit(solution)/shard_map/ppermute | solution.py:486
  258.6 19.9 %shard_map.138 = (f32[2,1024,512]{2,1,0:T(8,128)}, bf16[2,640,1536]{2,1,0:T(8,128)(2,1)}) custom-call(s32[1]{0:T(128)} %bitcast.device_ref, s32[32,49]{1,0:T(8,128)} %constant.43.clone.plan_ref, s32[2,8]{1,0:T(2,128)} %convert_element_type.3.used_ref, bf16[128,4096]{1,0:T(8,128)(2,1)} %shard_map.131.refs_0_, bf16[128,4096]{1,0:T(8,128)(2,1)} %shard_map.132.refs_1_, ...), custom_call_target="tpu_custom_call" | custom-call | flops 10737418240 | bytes 83886080 | tf_op jit(solution)/shard_map/pallas_call | solution.py:411
  278.6 11.2 %shard_map.139 = (f32[2,1024,512]{2,1,0:T(8,128)}, bf16[2,256,1536]{2,1,0:T(8,128)(2,1)}) custom-call(s32[1]{0:T(128)} %bitcast.device_ref, s32[32,46]{1,0:T(8,128)} %constant.44.clone.plan_ref, s32[2,8]{1,0:T(2,128)} %convert_element_type.3.used_ref, bf16[128,4096]{1,0:T(8,128)(2,1)} %collective-permute-done.2.refs_0_, ...), custom_call_target="tpu_custom_call", output_to_operand_aliasing={{0}: (19, {})} | custom-call | flops 4294967296 | bytes 83886080 | tf_op jit(solution)/shard_map/pallas_call | solution.py:411
  290.8 18.7 %shard_map.140 = f32[2,1024,512]{2,1,0:T(8,128)} custom-call(s32[1]{0:T(128)} %bitcast.device_ref, s32[32,53]{1,0:T(8,128)} %constant.45.clone.plan_ref, s32[2,8]{1,0:T(2,128)} %convert_element_type.3.used_ref, bf16[2,2,128,512]{3,2,1,0:T(8,128)(2,1)} %shard_map.133.refs_0_.refs_28_, ...), custom_call_target="tpu_custom_call", output_to_operand_aliasing={{}: (39, {})} | custom-call | flops 7784628224 | bytes 83886080 | tf_op jit(solution)/shard_map/pallas_call | solution.py:411
  (94 shorter events, 22.8 us)
Async XLA Ops:
  33.9 30.0 %all-to-all-start.1 = ((bf16[32,128,128]{2,1,0:T(8,128)(2,1)}), bf16[32,128,128]{2,1,0:T(8,128)(2,1)S(1)}, u32[]{:S(2)}, u32[]{:S(2)}) async-start(bf16[32,128,128]{2,1,0:T(8,128)(2,1)} %get-tuple-element.12), calls=%async_computation.1 | async-start | bytes 2097152 | tf_op jit(solution)/shard_map/all_to_all | solution.py:498
  71.6 8.8 %collective-permute-start.19 = (bf16[1,2,128,512]{3,2,1,0:T(8,128)(2,1)}, bf16[1,2,128,512]{3,2,1,0:T(8,128)(2,1)S(1)}, u32[]{:S(2)}, u32[]{:S(2)}) collective-permute-start(bf16[1,2,128,512]{3,2,1,0:T(8,128)(2,1)} %shard_map.135.refs_10_.refs_4_.refs_16_), channel_id=1, source_target_pairs={{0,16},{8,24},{16,0},{24,8},{1,17},{9,25},{17,1},{25,9},{2,18},{10... | collective-permute-start | bytes 786440 | tf_op jit(solution)/shard_map/ppermute | solution.py:486
  73.3 63.3 %collective-permute-start.9 = (bf16[128,4096]{1,0:T(8,128)(2,1)}, bf16[128,4096]{1,0:T(8,128)(2,1)}, u32[]{:S(2)}, u32[]{:S(2)}) collective-permute-start(bf16[128,4096]{1,0:T(8,128)(2,1)} %shard_map.132.refs_1_), channel_id=1, source_target_pairs={{2,0},{4,2},{6,4},{7,6},{5,7},{3,5},{1,3},{0,1},{10,8},{12,10},{14... | collective-permute-start | bytes 3145736 | tf_op jit(solution)/shard_map/ppermute | solution.py:504
  74.1 62.5 %collective-permute-start = (bf16[128,4096]{1,0:T(8,128)(2,1)S(1)}, bf16[128,4096]{1,0:T(8,128)(2,1)}, u32[]{:S(2)}, u32[]{:S(2)}) collective-permute-start(bf16[128,4096]{1,0:T(8,128)(2,1)S(1)} %copy-done.1), channel_id=1, source_target_pairs={{0,2},{2,4},{4,6},{6,7},{7,5},{5,3},{3,1},{1,0},{8,10},{10,12},{12... | collective-permute-start | bytes 3145736 | tf_op jit(solution)/shard_map/ppermute | solution.py:503
  75.3 63.3 %collective-permute-start.3 = (bf16[128,4096]{1,0:T(8,128)(2,1)}, bf16[128,4096]{1,0:T(8,128)(2,1)}, u32[]{:S(2)}, u32[]{:S(2)}) collective-permute-start(bf16[128,4096]{1,0:T(8,128)(2,1)} %shard_map.132.refs_1_), channel_id=1, source_target_pairs={{0,2},{2,4},{4,6},{6,7},{7,5},{5,3},{3,1},{1,0},{8,10},{10,12},{12... | collective-permute-start | bytes 3145736 | tf_op jit(solution)/shard_map/ppermute | solution.py:503
  76.1 8.4 %collective-permute-start.20 = (bf16[1,2,128,512]{3,2,1,0:T(8,128)(2,1)}, bf16[1,2,128,512]{3,2,1,0:T(8,128)(2,1)}, u32[]{:S(2)}, u32[]{:S(2)}) collective-permute-start(bf16[1,2,128,512]{3,2,1,0:T(8,128)(2,1)} %shard_map.135.refs_10_.refs_4_.refs_16_), channel_id=1, source_target_pairs={{0,8},{8,0},{16,24},{24,16},{1,9},{9,1},{17,25},{25,17},{2,10},{10... | collective-permute-start | bytes 786440 | tf_op jit(solution)/shard_map/ppermute | solution.py:486
  80.4 58.7 %collective-permute-start.6 = (bf16[128,4096]{1,0:T(8,128)(2,1)S(1)}, bf16[128,4096]{1,0:T(8,128)(2,1)}, u32[]{:S(2)}, u32[]{:S(2)}) collective-permute-start(bf16[128,4096]{1,0:T(8,128)(2,1)S(1)} %copy-done.1), channel_id=1, source_target_pairs={{2,0},{4,2},{6,4},{7,6},{5,7},{3,5},{1,3},{0,1},{10,8},{12,10},{14... | collective-permute-start | bytes 3145736 | tf_op jit(solution)/shard_map/ppermute | solution.py:504
  84.5 49.1 %collective-permute-start.15 = (bf16[1,2,128,512]{3,2,1,0:T(8,128)(2,1)}, bf16[1,2,128,512]{3,2,1,0:T(8,128)(2,1)S(1)}, u32[]{:S(2)}, u32[]{:S(2)}) collective-permute-start(bf16[1,2,128,512]{3,2,1,0:T(8,128)(2,1)} %shard_map.134), channel_id=1, source_target_pairs={{0,7},{2,5},{4,3},{6,1},{7,0},{5,2},{3,4},{1,6},{8,15},{10,13},{12... | collective-permute-start | bytes 786440 | tf_op jit(solution)/shard_map/ppermute | solution.py:560
  135.2 8.3 %collective-permute-start.16 = (bf16[1,2,128,512]{3,2,1,0:T(8,128)(2,1)S(1)}, bf16[1,2,128,512]{3,2,1,0:T(8,128)(2,1)S(1)}, u32[]{:S(2)}, u32[]{:S(2)}) collective-permute-start(bf16[1,2,128,512]{3,2,1,0:T(8,128)(2,1)S(1)} %collective-permute-done.15.refs_4_.refs_32_), channel_id=1, source_target_pairs={{0,16},{8,24},{16,0},{24,8},{1,17},{9,25},{17,1},{25,9},{2,18},{10... | collective-permute-start | bytes 786440 | tf_op jit(solution)/shard_map/ppermute | solution.py:486
  136.6 26.3 %collective-permute-start.10 = (bf16[128,4096]{1,0:T(8,128)(2,1)}, bf16[128,4096]{1,0:T(8,128)(2,1)}, u32[]{:S(2)}, u32[]{:S(2)}) collective-permute-start(bf16[128,4096]{1,0:T(8,128)(2,1)} %collective-permute-done.9.refs_4_.refs_5_), channel_id=1, source_target_pairs={{2,0},{4,2},{6,4},{7,6},{5,7},{3,5},{1,3},{0,1},{10,8},{12,10},{14... | collective-permute-start | bytes 3145736 | tf_op jit(solution)/shard_map/ppermute | solution.py:552
  136.6 26.4 %collective-permute-start.1 = (bf16[128,4096]{1,0:T(8,128)(2,1)}, bf16[128,4096]{1,0:T(8,128)(2,1)}, u32[]{:S(2)}, u32[]{:S(2)}) collective-permute-start(bf16[128,4096]{1,0:T(8,128)(2,1)} %collective-permute-done.refs_0_.refs_2_), channel_id=1, source_target_pairs={{0,2},{2,4},{4,6},{6,7},{7,5},{5,3},{3,1},{1,0},{8,10},{10,12},{12... | collective-permute-start | bytes 3145736 | tf_op jit(solution)/shard_map/ppermute | solution.py:551
  138.7 46.8 %collective-permute-start.4 = (bf16[128,4096]{1,0:T(8,128)(2,1)}, bf16[128,4096]{1,0:T(8,128)(2,1)}, u32[]{:S(2)}, u32[]{:S(2)}) collective-permute-start(bf16[128,4096]{1,0:T(8,128)(2,1)} %collective-permute-done.3.refs_1_.refs_3_), channel_id=1, source_target_pairs={{0,2},{2,4},{4,6},{6,7},{7,5},{5,3},{3,1},{1,0},{8,10},{10,12},{12... | collective-permute-start | bytes 3145736 | tf_op jit(solution)/shard_map/ppermute | solution.py:551
  139.2 48.3 %collective-permute-start.7 = (bf16[128,4096]{1,0:T(8,128)(2,1)}, bf16[128,4096]{1,0:T(8,128)(2,1)}, u32[]{:S(2)}, u32[]{:S(2)}) collective-permute-start(bf16[128,4096]{1,0:T(8,128)(2,1)} %collective-permute-done.6.refs_3_.refs_4_), channel_id=1, source_target_pairs={{2,0},{4,2},{6,4},{7,6},{5,7},{3,5},{1,3},{0,1},{10,8},{12,10},{14... | collective-permute-start | bytes 3145736 | tf_op jit(solution)/shard_map/ppermute | solution.py:552
  145.1 3.2 %collective-permute-start.18 = (bf16[1,2,128,512]{3,2,1,0:T(8,128)(2,1)S(1)}, bf16[1,2,128,512]{3,2,1,0:T(8,128)(2,1)S(1)}, u32[]{:S(2)}, u32[]{:S(2)}) collective-permute-start(bf16[1,2,128,512]{3,2,1,0:T(8,128)(2,1)S(1)} %collective-permute-done.16.refs_5_.refs_33_), channel_id=1, source_target_pairs={{0,8},{8,0},{16,24},{24,16},{1,9},{9,1},{17,25},{25,17},{2,10},{10... | collective-permute-start | bytes 786440 | tf_op jit(solution)/shard_map/ppermute | solution.py:486
  148.3 39.3 %collective-permute-start.22 = (bf16[2,2,128,512]{3,2,1,0:T(8,128)(2,1)}, bf16[2,2,128,512]{3,2,1,0:T(8,128)(2,1)S(1)}, u32[]{:S(2)}, u32[]{:S(2)}) collective-permute-start(bf16[2,2,128,512]{3,2,1,0:T(8,128)(2,1)} %shard_map.136.refs_14_.refs_8_.refs_20_), channel_id=1, source_target_pairs={{0,16},{8,24},{16,0},{24,8},{1,17},{9,25},{17,1},{25,9},{2,18},{10... | collective-permute-start | bytes 1572872 | tf_op jit(solution)/shard_map/ppermute | solution.py:486
  163.0 44.9 %collective-permute-start.11 = (bf16[128,4096]{1,0:T(8,128)(2,1)}, bf16[128,4096]{1,0:T(8,128)(2,1)}, u32[]{:S(2)}, u32[]{:S(2)}) collective-permute-start(bf16[128,4096]{1,0:T(8,128)(2,1)} %collective-permute-done.10.refs_4_.refs_9_), channel_id=1, source_target_pairs={{2,0},{4,2},{6,4},{7,6},{5,7},{3,5},{1,3},{0,1},{10,8},{12,10},{14... | collective-permute-start | bytes 3145736 | tf_op jit(solution)/shard_map/ppermute | solution.py:552
  163.0 46.2 %collective-permute-start.2 = (bf16[128,4096]{1,0:T(8,128)(2,1)}, bf16[128,4096]{1,0:T(8,128)(2,1)}, u32[]{:S(2)}, u32[]{:S(2)}) collective-permute-start(bf16[128,4096]{1,0:T(8,128)(2,1)} %collective-permute-done.1.refs_0_.refs_6_), channel_id=1, source_target_pairs={{0,2},{2,4},{4,6},{6,7},{7,5},{5,3},{3,1},{1,0},{8,10},{10,12},{12... | collective-permute-start | bytes 3145736 | tf_op jit(solution)/shard_map/ppermute | solution.py:551
  185.5 43.8 %collective-permute-start.5 = (bf16[128,4096]{1,0:T(8,128)(2,1)}, bf16[128,4096]{1,0:T(8,128)(2,1)}, u32[]{:S(2)}, u32[]{:S(2)}) collective-permute-start(bf16[128,4096]{1,0:T(8,128)(2,1)} %collective-permute-done.4.refs_1_.refs_7_), channel_id=1, source_target_pairs={{0,2},{2,4},{4,6},{6,7},{7,5},{5,3},{3,1},{1,0},{8,10},{10,12},{12... | collective-permute-start | bytes 3145736 | tf_op jit(solution)/shard_map/ppermute | solution.py:551
  187.5 41.9 %collective-permute-start.8 = (bf16[128,4096]{1,0:T(8,128)(2,1)}, bf16[128,4096]{1,0:T(8,128)(2,1)}, u32[]{:S(2)}, u32[]{:S(2)}) collective-permute-start(bf16[128,4096]{1,0:T(8,128)(2,1)} %collective-permute-done.7.refs_3_.refs_8_), channel_id=1, source_target_pairs={{2,0},{4,2},{6,4},{7,6},{5,7},{3,5},{1,3},{0,1},{10,8},{12,10},{14... | collective-permute-start | bytes 3145736 | tf_op jit(solution)/shard_map/ppermute | solution.py:552
  189.7 54.3 %collective-permute-start.30 = (bf16[128,4096]{1,0:T(8,128)(2,1)}, bf16[128,4096]{1,0:T(8,128)(2,1)S(1)}, u32[]{:S(2)}, u32[]{:S(2)}) collective-permute-start(bf16[128,4096]{1,0:T(8,128)(2,1)} %collective-permute-done.refs_0_.refs_2_), channel_id=1, source_target_pairs={{3,2},{4,5},{11,10},{12,13},{19,18},{20,21},{27,26},{28,29}} | collective-permute-start | bytes 3145736 | tf_op jit(solution)/shard_map/ppermute | solution.py:462
  207.9 37.6 %collective-permute-start.31 = (bf16[128,4096]{1,0:T(8,128)(2,1)}, bf16[128,4096]{1,0:T(8,128)(2,1)}, u32[]{:S(2)}, u32[]{:S(2)}) collective-permute-start(bf16[128,4096]{1,0:T(8,128)(2,1)} %collective-permute-done.3.refs_1_.refs_3_), channel_id=1, source_target_pairs={{3,2},{4,5},{11,10},{12,13},{19,18},{20,21},{27,26},{28,29}} | collective-permute-start | bytes 3145736 | tf_op jit(solution)/shard_map/ppermute | solution.py:462
  209.2 40.1 %collective-permute-start.32 = (bf16[128,4096]{1,0:T(8,128)(2,1)}, bf16[128,4096]{1,0:T(8,128)(2,1)}, u32[]{:S(2)}, u32[]{:S(2)}) collective-permute-start(bf16[128,4096]{1,0:T(8,128)(2,1)} %collective-permute-done.6.refs_3_.refs_4_), channel_id=1, source_target_pairs={{5,4},{2,3},{13,12},{10,11},{21,20},{18,19},{29,28},{26,27}} | collective-permute-start | bytes 3145736 | tf_op jit(solution)/shard_map/ppermute | solution.py:462
  229.3 3.7 %collective-permute-start.24 = (bf16[2,2,128,512]{3,2,1,0:T(8,128)(2,1)S(1)}, bf16[2,2,128,512]{3,2,1,0:T(8,128)(2,1)S(1)}, u32[]{:S(2)}, u32[]{:S(2)}) collective-permute-start(bf16[2,2,128,512]{3,2,1,0:T(8,128)(2,1)S(1)} %collective-permute-done.22.refs_15_.refs_9_.refs_21_), channel_id=1, source_target_pairs={{0,8},{8,0},{16,24},{24,16},{1,9},{9,1},{17,25},{25,17},{2,10},{10... | collective-permute-start | bytes 1572872 | tf_op jit(solution)/shard_map/ppermute | solution.py:486
  229.4 14.7 %collective-permute-start.25 = (bf16[2,2,128,512]{3,2,1,0:T(8,128)(2,1)}, bf16[2,2,128,512]{3,2,1,0:T(8,128)(2,1)}, u32[]{:S(2)}, u32[]{:S(2)}) collective-permute-start(bf16[2,2,128,512]{3,2,1,0:T(8,128)(2,1)} %shard_map.137.refs_18_.refs_12_.refs_24_), channel_id=1, source_target_pairs={{0,16},{8,24},{16,0},{24,8},{1,17},{9,25},{17,1},{25,9},{2,18},{10... | collective-permute-start | bytes 1572872 | tf_op jit(solution)/shard_map/ppermute | solution.py:486
  233.0 16.3 %collective-permute-start.26 = (bf16[2,2,128,512]{3,2,1,0:T(8,128)(2,1)S(1)}, bf16[2,2,128,512]{3,2,1,0:T(8,128)(2,1)S(1)}, u32[]{:S(2)}, u32[]{:S(2)}) collective-permute-start(bf16[2,2,128,512]{3,2,1,0:T(8,128)(2,1)S(1)} %copy-done.6), channel_id=1, source_target_pairs={{0,8},{8,0},{16,24},{24,16},{1,9},{9,1},{17,25},{25,17},{2,10},{10... | collective-permute-start | bytes 1572872 | tf_op jit(solution)/shard_map/ppermute | solution.py:486
  244.0 7.0 %collective-permute-start.27 = (bf16[2,2,128,512]{3,2,1,0:T(8,128)(2,1)}, bf16[2,2,128,512]{3,2,1,0:T(8,128)(2,1)S(1)}, u32[]{:S(2)}, u32[]{:S(2)}) collective-permute-start(bf16[2,2,128,512]{3,2,1,0:T(8,128)(2,1)} %collective-permute-done.25.refs_19_.refs_13_.refs_25_), channel_id=1, source_target_pairs={{0,8},{8,0},{16,24},{24,16},{1,9},{9,1},{17,25},{25,17},{2,10},{10... | collective-permute-start | bytes 1572872 | tf_op jit(solution)/shard_map/ppermute | solution.py:486
  244.0 14.6 %collective-permute-start.12 = (bf16[2,2,128,512]{3,2,1,0:T(8,128)(2,1)}, bf16[2,2,128,512]{3,2,1,0:T(8,128)(2,1)S(1)}, u32[]{:S(2)}, u32[]{:S(2)}) collective-permute-start(bf16[2,2,128,512]{3,2,1,0:T(8,128)(2,1)} %shard_map.133.refs_0_.refs_28_), channel_id=1, source_target_pairs={{0,16},{8,24},{16,0},{24,8},{1,17},{9,25},{17,1},{25,9},{2,18},{10... | collective-permute-start | bytes 1572872 | tf_op jit(solution)/shard_map/ppermute | solution.py:486
  245.5 44.3 %collective-permute-start.33 = (bf16[128,4096]{1,0:T(8,128)(2,1)}, bf16[128,4096]{1,0:T(8,128)(2,1)}, u32[]{:S(2)}, u32[]{:S(2)}) collective-permute-start(bf16[128,4096]{1,0:T(8,128)(2,1)} %collective-permute-done.9.refs_4_.refs_5_), channel_id=1, source_target_pairs={{5,4},{2,3},{13,12},{10,11},{21,20},{18,19},{29,28},{26,27}} | collective-permute-start | bytes 3145736 | tf_op jit(solution)/shard_map/ppermute | solution.py:462
  249.3 40.5 %collective-permute-start.13 = (bf16[2,2,128,512]{3,2,1,0:T(8,128)(2,1)}, bf16[2,2,128,512]{3,2,1,0:T(8,128)(2,1)S(1)}, u32[]{:S(2)}, u32[]{:S(2)}) collective-permute-start(bf16[2,2,128,512]{3,2,1,0:T(8,128)(2,1)} %shard_map.133.refs_0_.refs_28_), channel_id=1, source_target_pairs={{0,8},{8,0},{16,24},{24,16},{1,9},{9,1},{17,25},{25,17},{2,10},{10... | collective-permute-start | bytes 1572872 | tf_op jit(solution)/shard_map/ppermute | solution.py:486
  249.4 40.5 %collective-permute-start.28 = (bf16[128,4096]{1,0:T(8,128)(2,1)}, bf16[128,4096]{1,0:T(8,128)(2,1)}, u32[]{:S(2)}, u32[]{:S(2)}) collective-permute-start(bf16[128,4096]{1,0:T(8,128)(2,1)} %collective-permute-done.2.refs_0_), channel_id=1, source_target_pairs={{1,0},{4,6},{6,7},{3,1},{9,8},{12,14},{14,15},{11,9},{17,16},{20,2... | collective-permute-start | bytes 3145736 | tf_op jit(solution)/shard_map/ppermute | solution.py:572
  251.0 38.9 %collective-permute-start.29 = (bf16[128,4096]{1,0:T(8,128)(2,1)}, bf16[128,4096]{1,0:T(8,128)(2,1)}, u32[]{:S(2)}, u32[]{:S(2)}) collective-permute-start(bf16[128,4096]{1,0:T(8,128)(2,1)} %collective-permute-done.11.refs_4_.refs_3_), channel_id=1, source_target_pairs={{2,0},{7,6},{5,7},{0,1},{10,8},{15,14},{13,15},{8,9},{18,16},{23,2... | collective-permute-start | bytes 3145736 | tf_op jit(solution)/shard_map/ppermute | solution.py:572
  258.6 31.2 %collective-permute-start.14 = (bf16[2,2,128,512]{3,2,1,0:T(8,128)(2,1)S(1)}, bf16[2,2,128,512]{3,2,1,0:T(8,128)(2,1)S(1)}, u32[]{:S(2)}, u32[]{:S(2)}) collective-permute-start(bf16[2,2,128,512]{3,2,1,0:T(8,128)(2,1)S(1)} %collective-permute-done.12.refs_1_.refs_29_), channel_id=1, source_target_pairs={{0,8},{8,0},{16,24},{24,16},{1,9},{9,1},{17,25},{25,17},{2,10},{10... | collective-permute-start | bytes 1572872 | tf_op jit(solution)/shard_map/ppermute | solution.py:486
  (22 other events, 812.2 us)
